TPU v7x, 32 devices: a whole 2x2x4 slice. The times are simulated.
32 devices in a mesh: groups: 2 (over x), sub: 16 (over z, y, core).
Axes of the slice: x: 2, y: 2, z: 4, core: 2. Of those that a mesh axis runs over, the one named last changes fastest.
Arguments:
- modes_start: float32 [48, 6, 8192], P(None, None, ('groups', 'sub')), parts along dimension 2, may hold values from -6 to 6
- stiffness: float32 [24, 24, 8192], P(None, None, ('groups', 'sub')), parts along dimension 2, as said below
- mass: float32 [24, 24, 8192], P(None, None, ('groups', 'sub')), parts along dimension 2, as said below
- connect: int32 [4, 8192], P(None, ('groups', 'sub')), parts along dimension 1, may hold values from 0 to 382, as said below
Outputs:
- modes: float32 [48, 6, 8192], P(None, None, ('groups', 'sub')), parts along dimension 2
- ritz: float32 [96], P('groups'), parts along dimension 0
There are 2 independent parts, one for each index of `groups`. A program takes and returns all parts, laid end to end along the dimension named above; each array names one. Nothing has to cross between parts.
Inputs may be any that keep to these rules, and one draw needn't show every extreme that they name: `connect`: for element l of a subdomain, the four nodes are l + 64, one above it by less than 32, one below it by at most 64, and one above it by 32 or more and less than 64. `stiffness`: each block is symmetric positive definite. `mass`: each block is symmetric positive definite.
All inputs are finite; a program needn't handle non-finite values.
Results may differ from a plain program's by a relative error of at most 0.0001.
Values sent between devices are 32-bit elements; how exact they have to be, the bound alone decides.
No kernel may reach another device: no remote copies, remote signals or barrier semaphores. Data moves between devices by JAX's collectives and lax.ppermute only.
A program may use at most 64 MiB of HBM per device.

v0:
```python
import jax
import jax.numpy as jnp
from jax import lax
from jax.sharding import PartitionSpec as P

MODES = 48
HALO = 64
ITERS = 2
SMALL_STEPS = 2


highest = lax.Precision.HIGHEST


def with_halo(block, sides, width):
    for axis, dim in sides:
        count = lax.axis_size(axis)
        forward = [(i, i + 1) for i in range(count - 1)]
        backward = [(target, source) for source, target in forward]
        low = lax.ppermute(
            lax.slice_in_dim(block, block.shape[dim] - width, None, axis=dim), axis, forward
        )
        high = lax.ppermute(lax.slice_in_dim(block, 0, width, axis=dim), axis, backward)
        block = jnp.concatenate([low, block, high], axis=dim)
    return block


def shifted(value, axis, steps):
    count = lax.axis_size(axis)
    initial, last = (max(0, -steps), min(count, count - steps))
    return lax.ppermute(value, axis, [(source, source + steps) for source in range(initial, last)])


def inner(left, right):
    return jnp.einsum("acn,bcn->ab", left, right, precision=highest)


def combine(coeff, block):
    return jnp.einsum("ab,bcn->acn", coeff, block, precision=highest)


def symmetric(matrix):
    return 0.5 * (matrix + matrix.T)


def lower_solve(factor, rhs, transpose):
    return lax.linalg.triangular_solve(
        factor, rhs, left_side=True, lower=True, transpose_a=transpose
    )


def small_step(stiff_gram, mass_gram):
    scaling = 1.0 / jnp.sqrt(jnp.diagonal(mass_gram))
    outer = scaling[:, None] * scaling[None, :]
    stiff_scaled = symmetric(stiff_gram * outer)
    mass_scaled = symmetric(mass_gram * outer)
    factor = jnp.linalg.cholesky(stiff_scaled)
    coeff = jnp.eye(stiff_gram.shape[0], MODES, dtype=stiff_gram.dtype)
    for sweep in range(SMALL_STEPS):
        pushed = jnp.dot(mass_scaled, coeff, precision=highest)
        solved = lower_solve(factor, lower_solve(factor, pushed, False), True)
        normal_gram = symmetric(
            jnp.dot(solved.T, jnp.dot(mass_scaled, solved, precision=highest), precision=highest)
        )
        small_factor = jnp.linalg.cholesky(normal_gram)
        coeff = lower_solve(small_factor, solved.T, False).T
    return coeff * scaling[:, None]


def apply_pair(block, stiffness, mass, connect):
    rows = block.shape[0]
    count = block.shape[2]
    extended = with_halo(block, (("sub", 2),), HALO)
    width = count + 2 * HALO
    span = 128
    blocks = count // span
    window = span + 2 * HALO
    positions = jnp.arange(window, dtype=jnp.int32)
    stiff_blocks = stiffness.reshape(24, 24, blocks, span).transpose(2, 0, 1, 3)
    mass_blocks = mass.reshape(24, 24, blocks, span).transpose(2, 0, 1, 3)
    link_blocks = connect.reshape(4, blocks, span).transpose(1, 0, 2)

    def one_block(total, inputs):
        index, stiff_here, mass_here, link_here = inputs
        start = index * span
        local_window = lax.dynamic_slice_in_dim(extended, start, window, 2)
        selector = (link_here[:, :, None] - start == positions[None, None, :]).astype(block.dtype)
        picked = jnp.einsum("rcw,aew->rcae", local_window, selector, precision=highest).reshape(
            rows, 24, span
        )
        stiff_part = jnp.einsum("ije,rje->rie", stiff_here, picked, precision=highest)
        mass_part = jnp.einsum("ije,rje->rie", mass_here, picked, precision=highest)
        parts = jnp.stack([stiff_part, mass_part]).reshape(2, rows, 6, 4, span)
        placed = jnp.einsum("xrcae,aew->xrcw", parts, selector, precision=highest)
        old = lax.dynamic_slice_in_dim(total, start, window, 3)
        return (lax.dynamic_update_slice_in_dim(total, old + placed, start, 3), None)

    initial = jnp.zeros((2, rows, 6, width), block.dtype)
    summed, unused = lax.scan(
        one_block,
        initial,
        (jnp.arange(blocks, dtype=jnp.int32), stiff_blocks, mass_blocks, link_blocks),
    )
    from_below = shifted(summed[:, :, :, count + HALO :], "sub", 1)
    from_above = shifted(summed[:, :, :, :HALO], "sub", -1)
    inside = summed[:, :, :, HALO : count + HALO]
    inside = inside.at[:, :, :, :HALO].add(from_below)
    inside = inside.at[:, :, :, count - HALO :].add(from_above)
    return (inside[0], inside[1])


def body(modes_start, stiffness, mass, connect):
    stiff_start, mass_start = apply_pair(modes_start, stiffness, mass, connect)
    stiff_proj, mass_proj = lax.psum(
        (inner(modes_start, stiff_start), inner(modes_start, mass_start)), "sub"
    )
    factor = jnp.linalg.cholesky(symmetric(mass_proj))
    inverse = lower_solve(factor, jnp.eye(MODES, dtype=mass_proj.dtype), False)
    current = combine(inverse, modes_start)
    stiff_cur = combine(inverse, stiff_start)
    mass_cur = combine(inverse, mass_start)
    rayleigh = symmetric(
        jnp.dot(inverse, jnp.dot(stiff_proj, inverse.T, precision=highest), precision=highest)
    )
    direction = current
    stiff_dir = current
    mass_dir = current
    carried = rayleigh
    for sweep in range(ITERS):
        if sweep > 0:
            rayleigh = symmetric(lax.psum(inner(current, stiff_cur), "sub"))
        residual = stiff_cur - combine(rayleigh, mass_cur)
        stiff_res, mass_res = apply_pair(residual, stiffness, mass, connect)
        if sweep == 0:
            basis = jnp.concatenate([current, residual])
            stiff_basis = jnp.concatenate([stiff_cur, stiff_res])
            mass_basis = jnp.concatenate([mass_cur, mass_res])
        else:
            basis = jnp.concatenate([current, residual, direction])
            stiff_basis = jnp.concatenate([stiff_cur, stiff_res, stiff_dir])
            mass_basis = jnp.concatenate([mass_cur, mass_res, mass_dir])
        stiff_gram, mass_gram = lax.psum(
            (inner(basis, stiff_basis), inner(basis, mass_basis)), "sub"
        )
        coeff = small_step(stiff_gram, mass_gram)
        carried = symmetric(
            jnp.dot(coeff.T, jnp.dot(stiff_gram, coeff, precision=highest), precision=highest)
        )
        current = combine(coeff.T, basis)
        direction = combine(coeff[MODES:].T, basis[MODES:])
        if sweep + 1 < ITERS:
            stiff_cur = combine(coeff.T, stiff_basis)
            mass_cur = combine(coeff.T, mass_basis)
            stiff_dir = combine(coeff[MODES:].T, stiff_basis[MODES:])
            mass_dir = combine(coeff[MODES:].T, mass_basis[MODES:])
    return (current, jnp.diagonal(carried))


def solution(mesh):
    in_specs = (
        P(None, None, ("groups", "sub")),
        P(None, None, ("groups", "sub")),
        P(None, None, ("groups", "sub")),
        P(None, ("groups", "sub")),
    )
    out_specs = (P(None, None, ("groups", "sub")), P("groups"))
    return jax.shard_map(body, mesh=mesh, in_specs=in_specs, out_specs=out_specs, check_vma=False)
```

profile of v0, /device:TPU:0, one launch (start us, length us, event | category | flops | bytes accessed | tf_op | source)
XLA Modules:
  0.0 624.3 jit_solution(5031614352455597482)
XLA Ops:
  8.3 2.4 collective-permute-start
  12.2 3.1 copy.66
  15.2 2.2 copy.67
  19.5 33.1 %while.45 = (s32[]{:T(128)}, f32[2,48,6,384]{3,1,2,0:T(8,128)}, s32[2]{0:T(128)S(1)}, f32[48,6,384]{2,0,1:T(8,128)}, s32[2,4,128]{2,1,0:T(4,128)S(1)}, /*index=5...) while((s32[]{:T(128)}, f32[2,48,6,384]{3,1,2,0:T(8,128)}, ...), condition=%wide.region_1.2_spmd.clone, body=%wide.region_0.1_spmd.clone.sunk | while | flops 1444594176 | bytes 14656723 | solution.py:99
  20.7 1.5 fusion.318
  22.8 4.0 fusion.320
  28.2 4.0 fusion.319
  33.3 2.7 fusion.321
  37.3 1.5 fusion.318
  39.3 4.0 fusion.320
  44.8 4.0 fusion.319
  49.9 2.7 fusion.321
  53.9 5.2 collective-permute-start.2
  61.3 2.7 collective-permute-done.3
  64.1 2.3 scatter-add.21
  67.2 63.9 %all-reduce.6 = (f32[48,48]{1,0:T(8,128)S(1)}, f32[48,48]{0,1:T(8,128)S(1)}) all-reduce(f32[48,48]{1,0:T(8,128)S(1)} %convolution_bitcast_fusion.9, f32[48,48]{0,1:T(8,128)S(1)} %convolution_bitcast_fusion.8), channel_id=1, replica_groups=mesh['groups'=2,'sub'=16] {'sub'}, use_global_device_ids=true, to_apply=%region_2.3 | all-reduce | flops 4608 | bytes 36864 | tf_op jit(solution)/shard_map/psum | solution.py:114
  131.3 4.4 cholesky.251
  137.0 3.7 custom-call.37
  145.3 1.9 collective-permute-done.5
  148.5 31.3 %while.46 = (s32[]{:T(128)}, f32[2,48,6,384]{3,1,2,0:T(8,128)}, s32[2]{0:T(128)S(1)}, f32[48,6,384]{2,0,1:T(8,128)S(1)}, s32[2,4,128]{2,1,0:T(4,128)S(1)}, /*ind...) while((s32[]{:T(128)}, f32[2,48,6,384]{3,1,2,0:T(8,128)}, ...), condition=%wide.region_7.9_spmd.clone, body=%wide.region_6.8_spmd.clone.sunk | while | flops 1444594176 | bytes 18195724 | solution.py:99
  151.0 4.0 fusion.332
  156.4 4.0 fusion.331
  161.5 2.7 fusion.333
  166.6 4.0 fusion.332
  172.0 4.0 fusion.331
  177.2 2.7 fusion.333
  181.1 2.9 collective-permute-start.6
  185.6 1.5 collective-permute-start.7
  189.3 2.3 scatter-add.25
  194.2 91.6 %all-reduce.11.cloned.1.call-done = (f32[96,96]{0,1:T(8,128)}, f32[96,96]{0,1:T(8,128)}) async-done(((f32[96,96]{0,1:T(8,128)}, f32[96,96]{0,1:T(8,128)}), (f32[96,96]{0,1:T(8,128)}, f32[96,96]{0,1:T(8,128)})) %all-reduce.11.cloned.1.call-update) | async-done | bytes 73744 | tf_op jit(solution)/shard_map/psum | solution.py:142
  285.8 2.2 gather_fusion
  289.3 8.8 %cholesky.95 = f32[96,96]{1,0:T(8,128)S(1)} custom-call(f32[96,96]{1,0:T(8,128)S(1)} %broadcast_multiply_fusion.1), custom_call_target="Cholesky" | custom-call | tf_op jit(solution)/shard_map/jit(cholesky)/cholesky | solution.py:57
  299.4 7.4 %custom-call.55 = f32[1,96,96]{1,2,0:T(8,128)S(1)} custom-call(f32[1,96,96]{2,1,0:T(8,128)S(1)} %fusion.104), custom_call_target="InvertDiagBlocksLowerTriangular" | custom-call | tf_op jit(solution)/shard_map/triangular_solve/custom-call.7 | solution.py:47
  308.1 4.4 cholesky.262
  313.8 3.7 custom-call.53
  319.0 4.4 cholesky.273
  324.7 3.7 custom-call.56
  331.5 58.5 %psum.53 = f32[48,48]{1,0:T(8,128)S(1)} all-reduce(f32[48,48]{1,0:T(8,128)S(1)} %convolution_bitcast_fusion.7), channel_id=1, replica_groups=mesh['groups'=2,'sub'=16] {'sub'}, use_global_device_ids=true, to_apply=%region_12.17 | all-reduce | flops 2304 | bytes 18432 | tf_op jit(solution)/shard_map/psum | solution.py:131
  392.0 1.5 collective-permute-start.9
  397.2 33.2 %while.47 = (s32[]{:T(128)}, f32[2,48,6,384]{3,1,2,0:T(8,128)}, s32[2]{0:T(128)S(1)}, f32[48,6,384]{2,0,1:T(8,128)}, s32[2,4,128]{2,1,0:T(4,128)S(1)}, /*index=5...) while((s32[]{:T(128)}, f32[2,48,6,384]{3,1,2,0:T(8,128)}, ...), condition=%wide.region_14.19_spmd.clone, body=%wide.region_13.18_spmd.clone.sunk | while | flops 1444594176 | bytes 14656723 | solution.py:99
  398.5 1.5 fusion.342
  400.6 4.0 fusion.344
  406.0 4.0 fusion.343
  411.2 2.7 fusion.345
  415.1 1.5 fusion.342
  417.2 4.0 fusion.344
  422.7 4.0 fusion.343
  427.8 2.7 fusion.345
  431.7 2.9 collective-permute-start.10
  436.3 1.7 collective-permute-start.11
  439.9 2.3 scatter-add.29
  442.3 1.5 convolution_bitcast_fusion.3
  443.8 1.5 convolution_bitcast_fusion.4
  445.4 93.9 %all-reduce.13.cloned.1.call-done = (f32[144,144]{0,1:T(8,128)}, f32[144,144]{0,1:T(8,128)}) async-done(((f32[144,144]{0,1:T(8,128)}, f32[144,144]{0,1:T(8,128)}), (f32[144,144]{0,1:T(8,128)}, f32[144,144]{0,1:T(8,128)})) %all-reduce.13.cloned.1.call-update) | async-done | bytes 165904 | tf_op jit(solution)/shard_map/psum | solution.py:142
  539.3 3.2 gather_fusion.1
  544.4 11.7 %cholesky.155 = f32[128,128]{1,0:T(8,128)S(1)} custom-call(f32[128,128]{1,0:T(8,128)S(1)} %cholesky.304), custom_call_target="Cholesky" | custom-call | tf_op jit(solution)/shard_map/jit(cholesky)/cholesky | solution.py:57
  556.2 9.8 %custom-call.38 = f32[1,128,128]{1,2,0:T(8,128)S(1)} custom-call(f32[1,128,128]{2,1,0:T(8,128)S(1)} %get-tuple-element.375), custom_call_target="InvertDiagBlocksLowerTriangular" | custom-call | tf_op jit(solution)/shard_map/jit(cholesky)/cholesky | solution.py:57
  566.3 1.5 cholesky.175
  570.6 19.8 %custom-call.61 = f32[2,128,128]{1,2,0:T(8,128)S(1)} custom-call(f32[2,128,128]{2,1,0:T(8,128)S(1)} %pad_maximum_fusion.17), custom_call_target="InvertDiagBlocksLowerTriangular" | custom-call | tf_op jit(solution)/shard_map/triangular_solve/custom-call.10 | solution.py:47
  592.3 4.4 cholesky.284
  598.0 3.7 custom-call.59
  604.1 4.4 cholesky.295
  609.8 3.7 custom-call.62
  615.9 1.5 gather_fusion.2
  (279 shorter events, 80.6 us)
Async XLA Ops:
  7.2 278.7 %all-reduce.11.cloned.1.call-start = ((), (), s32[]{:S(2)}) async-start(), calls=%async_computation | async-start | bytes 196608 | tf_op jit(solution)/shard_map/psum | solution.py:142
  8.3 9.2 %collective-permute-start = (f32[48,6,64]{2,0,1:T(8,128)S(1)}, f32[48,6,64]{2,0,1:T(8,128)S(1)}, u32[]{:S(2)}, u32[]{:S(2)}) collective-permute-start(f32[48,6,64]{2,0,1:T(8,128)S(1)} %get-tuple-element.372), channel_id=1, source_target_pairs={{0,1},{1,2},{2,3},{3,4},{4,5},{5,6},{6,7},{7,8},{8,9},{9,10},{10,1... | collective-permute-start | bytes 221192 | tf_op jit(solution)/shard_map/ppermute | solution.py:20
  10.7 4.5 copy-start.23
  10.7 6.7 %collective-permute-start.1 = (f32[48,6,64]{2,0,1:T(8,128)S(1)}, f32[48,6,64]{2,0,1:T(8,128)S(1)}, u32[]{:S(2)}, u32[]{:S(2)}) collective-permute-start(f32[48,6,64]{2,0,1:T(8,128)S(1)} %get-tuple-element.373), channel_id=1, source_target_pairs={{1,0},{2,1},{3,2},{4,3},{5,4},{6,5},{7,6},{8,7},{9,8},{10,9},{11,1... | collective-permute-start | bytes 221192 | tf_op jit(solution)/shard_map/ppermute | solution.py:23
  15.2 2.2 copy-start.8
  17.5 2.0 copy-start.26
  32.3 1.1 copy-start
  48.8 1.1 copy-start
  52.6 6.5 %copy-start.3 = (f32[2,48,6,384]{3,1,2,0:T(8,128)S(1)}, f32[2,48,6,384]{3,1,2,0:T(8,128)}, u32[]{:S(2)}) copy-start(f32[2,48,6,384]{3,1,2,0:T(8,128)} %get-tuple-element.207) | copy-start | bytes 2654212
  53.9 6.7 %collective-permute-start.2 = (f32[2,48,6,64]{3,1,2,0:T(8,128)S(1)}, f32[2,48,6,64]{3,1,2,0:T(8,128)S(1)}, u32[]{:S(2)}, u32[]{:S(2)}) collective-permute-start(f32[2,48,6,64]{3,1,2,0:T(8,128)S(1)} %get-tuple-element.363), channel_id=1, source_target_pairs={{0,1},{1,2},{2,3},{3,4},{4,5},{5,6},{6,7},{7,8},{8,9},{9,10},{10,1... | collective-permute-start | bytes 442376 | tf_op jit(solution)/shard_map/ppermute | solution.py:31
  59.3 4.7 collective-permute-start.3
  141.3 6.2 copy-start.10
  141.7 6.8 %copy-start.12 = (f32[48,6,256]{2,0,1:T(8,128)}, f32[48,6,256]{2,0,1:T(8,128)S(1)}, u32[]{:S(2)}) copy-start(f32[48,6,256]{2,0,1:T(8,128)S(1)} %fusion.93) | copy-start | bytes 884740
  142.7 2.6 collective-permute-start.4
  144.0 3.3 collective-permute-start.5
  148.5 2.4 copy-start.6
  160.4 1.1 copy-start.1
  161.1 3.1 copy-start.7
  164.2 2.4 copy-start.6
  176.1 1.1 copy-start.1
  176.8 3.1 copy-start.7
  179.9 5.6 copy-start.4
  181.1 6.0 collective-permute-start.6
  185.6 3.5 collective-permute-start.7
  187.3 4.3 copy-start.13
  189.3 3.6 copy-start.11
  191.5 138.4 %copy-start.9 = (f32[2,48,6,256]{3,1,2,0:T(8,128)}, f32[2,48,6,256]{3,1,2,0:T(8,128)S(1)}, u32[]{:S(2)}) copy-start(f32[2,48,6,256]{3,1,2,0:T(8,128)S(1)} %scatter-add.25) | copy-start | bytes 1769476
  194.1 345.2 %all-reduce.13.cloned.1.call-start = ((), (), s32[]{:S(2)}) async-start(), calls=%async_computation.1 | async-start | bytes 589824 | tf_op jit(solution)/shard_map/psum | solution.py:142
  329.1 61.0 %copy-start.18 = (f32[48,6,256]{2,0,1:T(8,128)}, f32[48,6,256]{2,0,1:T(8,128)S(1)}, u32[]{:S(2)}) copy-start(f32[48,6,256]{2,0,1:T(8,128)S(1)} %fusion.90) | copy-start | bytes 884740
  329.5 61.0 %copy-start.16 = (f32[48,6,256]{2,0,1:T(8,128)}, f32[48,6,256]{2,0,1:T(8,128)S(1)}, u32[]{:S(2)}) copy-start(f32[48,6,256]{2,0,1:T(8,128)S(1)} %fusion.89) | copy-start | bytes 884740
  330.0 64.7 %copy-start.20 = (f32[48,6,256]{2,0,1:T(8,128)}, f32[48,6,256]{2,0,1:T(8,128)S(1)}, u32[]{:S(2)}) copy-start(f32[48,6,256]{2,0,1:T(8,128)S(1)} %fusion.88) | copy-start | bytes 884740
  390.5 4.7 copy-start.14
  390.7 4.0 collective-permute-start.8
  392.0 3.3 collective-permute-start.9
  410.1 1.1 copy-start.2
  426.7 1.1 copy-start.2
  430.5 5.6 copy-start.5
  431.7 6.3 %collective-permute-start.10 = (f32[2,48,6,64]{3,1,2,0:T(8,128)S(1)}, f32[2,48,6,64]{3,1,2,0:T(8,128)S(1)}, u32[]{:S(2)}, u32[]{:S(2)}) collective-permute-start(f32[2,48,6,64]{3,1,2,0:T(8,128)S(1)} %get-tuple-element.359), channel_id=1, source_target_pairs={{0,1},{1,2},{2,3},{3,4},{4,5},{5,6},{6,7},{7,8},{8,9},{9,10},{10,1... | collective-permute-start | bytes 442376 | tf_op jit(solution)/shard_map/ppermute | solution.py:31
  436.3 3.5 collective-permute-start.11
  438.2 4.1 copy-start.15
  438.2 4.1 copy-start.19
  438.2 4.1 copy-start.21
  438.2 4.1 copy-start.22
  438.2 4.1 copy-start.25
  442.2 1.6 copy-start.17
  570.5 43.2 %copy-start.24 = (f32[144,144]{0,1:T(8,128)S(1)}, f32[144,144]{0,1:T(8,128)}, u32[]{:S(2)}) copy-start(f32[144,144]{0,1:T(8,128)} %get-tuple-element.356) | copy-start | bytes 248836
Sparse Core Ops, SparseCore 0:
  194.2 91.5 all-reduce.10
  445.5 93.7 all-reduce.12
where the time goes:
time: 634 us; the launch traced here: 624 us
  waiting for transfers between devices  193 us (30%)
  blocking collectives  122 us (19%)
  other arithmetic  114 us (18%)
  matrix products  96 us (15%)
  local copies, waits for them, and re-layouts  52.9 us (8%)
  starting transfers between devices  24.7 us (4%)
  between operations  16.8 us (3%)
    psum x2, waiting for transfers between devices, body(): lax.psum((inner(basis, stiff_basis), inner(basis, mass_basis)), 'sub')  186 us
    psum x1, blocking collectives, body(): lax.psum((inner(modes_start, stiff_start), inner(modes_start, mass_start)...  63.9 us
    psum x1, blocking collectives, body(): rayleigh = symmetric(lax.psum(inner(current, stiff_cur), 'sub'))  58.5 us
    another operation x18, other arithmetic, lower_solve(): lax.linalg.triangular_solve(factor, rhs, left_side=True, lower=True, tran...  49.6 us
    another operation x10, other arithmetic, small_step(): factor = jnp.linalg.cholesky(stiff_scaled)  33.8 us
    dot_general x6, matrix products, one_block(): jnp.einsum('ije,rje->rie', stiff_here, picked, precision=highest)  24.3 us
    dot_general x6, matrix products, one_block(): mass_part = jnp.einsum('ije,rje->rie', mass_here, picked, precision=highest)  24.3 us
    another operation x12, other arithmetic, small_step(): small_factor = jnp.linalg.cholesky(normal_gram)  20.2 us
  transfers between devices with their start and end apart: 14, of which 7 were waited for; matrix products, arithmetic and copies ran while one was open for 2% of the time, Pallas kernels for 0%

commit v1 on v0

v1 whole, which is shorter than its diff:
```python
import functools

import jax
import jax.numpy as jnp
from jax import lax
from jax.experimental import pallas as pl
from jax.experimental.pallas import tpu as pltpu
from jax.sharding import PartitionSpec as P

HALO = 64
LANES = 128
CORNERS = 4
F32 = jnp.float32
BF16 = jnp.bfloat16

NN = (((1,), (0,)), ((), ()))
NT = (((1,), (1,)), ((), ()))
TN = (((0,), (0,)), ((), ()))


def split(value):
    high = value.astype(BF16)
    return high, (value - high.astype(F32)).astype(BF16)


def dot1(left, right, dims):
    return lax.dot_general(left, right, dims, preferred_element_type=F32)


def dot3(left, right, dims=NN):
    left_high, left_low = split(left)
    right_high, right_low = split(right)
    return dot1(left_high, right_high, dims) + (
        dot1(left_high, right_low, dims) + dot1(left_low, right_high, dims)
    )


def dotf(left, right, dims=NN):
    return lax.dot_general(
        left, right, dims, precision=lax.Precision.HIGHEST, preferred_element_type=F32
    )


def symmetric(matrix):
    return 0.5 * (matrix + matrix.T)


def eliminate(work, modes):
    rows = lax.broadcasted_iota(jnp.int32, (modes, 1), 0)
    scale = jnp.zeros((modes, 1), F32)
    for k in range(modes):
        pivot = work[k : k + 1, :]
        inverse = 1.0 / pivot[:, k : k + 1]
        column = work[:, k : k + 1]
        factor = jnp.where(rows > k, column * inverse, 0.0)
        scale = jnp.where(rows == k, inverse, scale)
        work = work - factor * pivot
    return (work * jnp.sqrt(scale))[:, modes:]


def eye(modes):
    row = lax.broadcasted_iota(jnp.int32, (modes, modes), 0)
    col = lax.broadcasted_iota(jnp.int32, (modes, modes), 1)
    return (row == col).astype(F32)


def store_lanes(ref, value):
    rows, width = value.shape
    ref[0:rows, 0:width] = value


def element_products(dims, ext, stiffness, mass, stiff_edge, mass_edge, connect, edge_nodes, picked, high, low, out):
    comps, modes = dims
    ext_high, ext_low = split(ext[...])
    own_nodes = connect[...] + (LANES - HALO)
    blocks = (
        (stiffness, mass, 0, own_nodes[:, :LANES], 0, 3 * LANES),
        (stiffness, mass, LANES, own_nodes[:, LANES:], LANES, 3 * LANES),
        (stiff_edge, mass_edge, 0, edge_nodes, 0, 4 * LANES),
    )
    for number, (stiff, weigh, lane, nodes, base, window) in enumerate(blocks):
        place = lax.broadcasted_iota(jnp.int32, (window, LANES), 0) + base
        chosen = jnp.concatenate(
            [(place == nodes[a : a + 1, :]).astype(F32).astype(BF16) for a in range(CORNERS)], axis=1
        )
        picked[...] = dot1(ext_high[:, base : base + window], chosen, NN) + dot1(
            ext_low[:, base : base + window], chosen, NN
        )

        def one(step, unused):
            comp = step // 2
            pair = (step % 2) * 2
            totals = [jnp.zeros((modes, LANES), F32) for _ in range(4)]
            for j in range(comps * CORNERS):
                start = (j // CORNERS) * modes
                value = picked[start : start + modes, (j % CORNERS) * LANES : (j % CORNERS + 1) * LANES]
                for q in range(2):
                    for m, matrix in enumerate((stiff, weigh)):
                        entry = matrix[comp * CORNERS + pair + q, j : j + 1, lane : lane + LANES]
                        totals[2 * q + m] = totals[2 * q + m] + entry * value
            for q in range(2):
                for m in range(2):
                    upper, lower = split(totals[2 * q + m])
                    row = pl.multiple_of((comp * 2 + m) * modes, 16)
                    col = pl.multiple_of((pair + q) * LANES, LANES)
                    high[pl.ds(row, modes), pl.ds(col, LANES)] = upper
                    low[pl.ds(row, modes), pl.ds(col, LANES)] = lower
            return unused

        lax.fori_loop(0, comps * 2, one, 0)
        target = chosen[LANES - base : 3 * LANES - base, :]
        total = dot1(high[...], target, NT) + dot1(low[...], target, NT)
        if number == 0:
            out[...] = total
        else:
            out[...] += total


def grams(basis, products, dims):
    comps, modes = dims
    total = None
    for c in range(comps):
        left = jnp.concatenate([part[c * modes : (c + 1) * modes, :] for part in basis], axis=0)
        right = products[c * 2 * modes : (c + 1) * 2 * modes, :]
        term = dot3(left, right, NT)
        total = term if total is None else total + term
    return total


def pack_kernel(dims, block, stiffness, mass, connect, up, down):
    comps, modes = dims
    size = comps * CORNERS
    first = lax.broadcasted_iota(jnp.int32, (size, LANES), 1) < HALO

    def one(i, unused):
        row = pl.multiple_of(i * size, 8)
        up[pl.ds(row, size), :] = jnp.where(
            first, pltpu.roll(stiffness[i, :, LANES:], HALO, 1), mass[i, :, LANES:]
        )
        down[pl.ds(row, size), :] = jnp.where(
            first, stiffness[i, :, :LANES], pltpu.roll(mass[i, :, :LANES], HALO, 1)
        )
        return unused

    lax.fori_loop(0, size, one, 0)
    links = connect[...].astype(F32)
    pad = jnp.zeros((8 - CORNERS, LANES), F32)
    top = size * size
    up[top : top + 8, :] = jnp.concatenate([pltpu.roll(links[:, LANES:], HALO, 1), pad], axis=0)
    down[top : top + 8, :] = jnp.concatenate([links[:, :LANES], pad], axis=0)
    for c in range(comps):
        row = top + 8 + c * modes
        up[row : row + modes, :] = block[:, c, LANES:]
        down[row : row + modes, :] = block[:, c, :LANES]


def first_kernel(dims, stiffness, mass, connect, up, down, below, above, edges, edge_nodes, prod_low, prod_high, gram, ext, picked, high, low, out):
    comps, modes = dims
    size = comps * CORNERS
    top = size * size
    first = lax.broadcasted_iota(jnp.int32, (size, LANES), 1) < HALO

    def one(i, unused):
        row = pl.multiple_of(i * size, 8)
        lower = below[pl.ds(row, size), :]
        upper = above[pl.ds(row, size), :]
        edges[0, i] = jnp.where(first, lower, pltpu.roll(upper, HALO, 1))
        edges[1, i] = jnp.where(first, pltpu.roll(lower, HALO, 1), upper)
        return unused

    lax.fori_loop(0, size, one, 0)
    count = connect.shape[1]
    before = below[top : top + 8, :] + (LANES - HALO - count)
    after = pltpu.roll(above[top : top + 8, :], HALO, 1) + (LANES - HALO + count)
    edge_nodes[...] = jnp.where(first[:8], before, after).astype(jnp.int32)
    nodes = slice(top + 8, top + 8 + comps * modes)
    for tile, part in enumerate((below, down, up, above)):
        ext[:, tile * LANES : (tile + 1) * LANES] = part[nodes, :]
    element_products(dims, ext, stiffness, mass, edges.at[0], edges.at[1], connect, edge_nodes[...], picked, high, low, out)
    prod_low[...] = out[:, :LANES]
    prod_high[...] = out[:, LANES:]
    store_lanes(gram, grams([ext[:, LANES : 3 * LANES]], out[...], dims))


def second_kernel(dims, gram_in, stiffness, mass, connect, edges, edge_nodes, up, down, p_below, p_low, p_high, p_above, res_low, res_high, prod_low, prod_high, gram, state, ext, picked, high, low, out):
    comps, modes = dims
    size = comps * CORNERS
    reduced = gram_in[...]
    stiff_gram = symmetric(reduced[:, :modes])
    mass_gram = symmetric(reduced[:, modes : 2 * modes])
    unit = eye(modes)
    inverse = eliminate(jnp.concatenate([mass_gram, unit], axis=1), modes)
    stiff_root = eliminate(jnp.concatenate([stiff_gram, unit], axis=1), modes)
    ratio = dotf(stiff_gram, dotf(inverse, inverse, TN))
    state[0] = inverse
    state[1] = dotf(stiff_root, stiff_root, TN)
    state[2] = mass_gram
    ratio_high, ratio_low = split(ratio)
    for c in range(comps):
        for tile, part in enumerate((p_below, p_low, p_high, p_above)):
            row = c * 2 * modes
            right_high, right_low = split(part[row + modes : row + 2 * modes, :])
            moved = dot1(ratio_high, right_high, NN) + (dot1(ratio_high, right_low, NN) + dot1(ratio_low, right_high, NN))
            ext[c * modes : (c + 1) * modes, tile * LANES : (tile + 1) * LANES] = part[row : row + modes, :] - moved
    element_products(dims, ext, stiffness, mass, edges.at[0], edges.at[1], connect, edge_nodes[...], picked, high, low, out)
    prod_low[...] = out[:, :LANES]
    prod_high[...] = out[:, LANES:]
    res_low[...] = ext[:, LANES : 2 * LANES]
    res_high[...] = ext[:, 2 * LANES : 3 * LANES]
    nodes = slice(size * size + 8, size * size + 8 + comps * modes)
    block = jnp.concatenate([down[nodes, :], up[nodes, :]], axis=1)
    store_lanes(gram, grams([block, ext[:, LANES : 3 * LANES]], out[...], dims))


def small_step(reduced, solver, mass_old, start, modes):
    rows = reduced.shape[0]
    old = rows - modes
    turned = reduced.T
    cross = reduced[:old, :modes]
    corner = symmetric(reduced[old:, :modes])
    mass_cross = reduced[:old, modes : 2 * modes]
    mass_corner = symmetric(reduced[old:, modes : 2 * modes])
    mass_turned = turned[modes : 2 * modes, :old]
    mass_all = jnp.concatenate(
        [
            jnp.concatenate([mass_old, mass_cross], axis=1),
            jnp.concatenate([mass_turned, mass_corner], axis=1),
        ],
        axis=0,
    )
    unit = eye(modes)
    carried = dotf(turned[:modes, :old], solver)
    schur = symmetric(corner - dotf(carried, cross))
    root = eliminate(jnp.concatenate([schur, -carried, unit], axis=1), modes)
    wide = jnp.concatenate(
        [
            jnp.concatenate([solver, jnp.zeros((old, modes), F32)], axis=1),
            jnp.zeros((modes, rows), F32),
        ],
        axis=0,
    )
    solver = wide + dotf(root, root, TN)
    pushed = dotf(start, mass_all[: start.shape[1], :])
    solved = dotf(pushed, solver)
    again = dotf(solved, mass_all)
    pushed = eliminate(jnp.concatenate([symmetric(dotf(solved, again, NT)), again], axis=1), modes)
    solved = dotf(pushed, solver)
    again = dotf(solved, mass_all)
    normal = symmetric(dotf(solved, again, NT))
    energy = dotf(solved, pushed, NT)
    last = eliminate(jnp.concatenate([normal, solved, energy, unit], axis=1), modes)
    coeff = last[:, :rows]
    return coeff, last[:, rows : rows + modes], last[:, rows + modes :], solver, mass_all


def third_kernel(dims, gram_in, state_in, stiffness, mass, connect, edges, edge_nodes, up, down, p_below, p_low, p_high, p_above, q_below, q_low, q_high, q_above, res_low, res_high, new_low, new_high, gram, coeff_out, state, ext, picked, high, low, out):
    comps, modes = dims
    size = comps * CORNERS
    coeff, half, root, solver, mass_all = small_step(gram_in[...], state_in[1], state_in[2], state_in[0], modes)
    rayleigh = symmetric(dotf(half, root, NT))
    coeff_out[...] = coeff
    state[0] = solver
    state[1] = mass_all
    bent = dotf(rayleigh, coeff)
    mixed = jnp.concatenate([coeff[:, :modes], -bent[:, :modes], coeff[:, modes:], -bent[:, modes:]], axis=1)
    mixed_high, mixed_low = split(mixed)
    tiles = ((p_below, q_below), (p_low, q_low), (p_high, q_high), (p_above, q_above))
    for c in range(comps):
        for tile, parts in enumerate(tiles):
            row = c * 2 * modes
            right = jnp.concatenate([part[row : row + 2 * modes, :] for part in parts], axis=0)
            right_high, right_low = split(right)
            ext[c * modes : (c + 1) * modes, tile * LANES : (tile + 1) * LANES] = dot1(mixed_high, right_high, NN) + (
                dot1(mixed_high, right_low, NN) + dot1(mixed_low, right_high, NN)
            )
    element_products(dims, ext, stiffness, mass, edges.at[0], edges.at[1], connect, edge_nodes[...], picked, high, low, out)
    new_low[...] = ext[:, LANES : 2 * LANES]
    new_high[...] = ext[:, 2 * LANES : 3 * LANES]
    nodes = slice(size * size + 8, size * size + 8 + comps * modes)
    block = jnp.concatenate([down[nodes, :], up[nodes, :]], axis=1)
    residual = jnp.concatenate([res_low[...], res_high[...]], axis=1)
    store_lanes(gram, grams([block, residual, ext[:, LANES : 3 * LANES]], out[...], dims))


def last_kernel(dims, gram_in, coeff_in, state_in, up, down, res_low, res_high, new_low, new_high, modes_out, ritz_out):
    comps, modes = dims
    size = comps * CORNERS
    coeff, half, root, solver, mass_all = small_step(gram_in[...], state_in[0], state_in[1], coeff_in[...], modes)
    ritz = jnp.sum(half * root, axis=1, keepdims=True)
    ritz_out[...] = jnp.broadcast_to(ritz, (modes, LANES))
    coeff_high, coeff_low = split(coeff)
    top = size * size + 8
    for tile, parts in enumerate(((down, res_low, new_low), (up, res_high, new_high))):
        for c in range(comps):
            row = c * modes
            right = jnp.concatenate(
                [parts[0][top + row : top + row + modes, :]] + [part[row : row + modes, :] for part in parts[1:]], axis=0
            )
            right_high, right_low = split(right)
            modes_out[:, c, tile * LANES : (tile + 1) * LANES] = dot1(coeff_high, right_high, NN) + (
                dot1(coeff_high, right_low, NN) + dot1(coeff_low, right_high, NN)
            )


def total_over(value, axis):
    count = lax.axis_size(axis)
    if count & (count - 1):
        return lax.psum(value, axis)

    def from_partner(part, bits):
        return lax.ppermute(part, axis, [(i, i ^ bits) for i in range(count)])

    stride = 1
    while stride < count:
        if 4 * stride <= count:
            one, two, three = (from_partner(value, k * stride) for k in (1, 2, 3))
            value = (value + one) + (two + three)
            stride *= 4
        else:
            value = value + from_partner(value, stride)
            stride *= 2
    return value


def from_neighbours(upward, downward, axis):
    count = lax.axis_size(axis)
    below = lax.ppermute(upward, axis, [(i, i + 1) for i in range(count - 1)])
    above = lax.ppermute(downward, axis, [(i + 1, i) for i in range(count - 1)])
    return below, above


def call(kernel, dims, name, outs, scratch, *operands):
    shapes = tuple(jax.ShapeDtypeStruct(shape, dtype) for shape, dtype in outs)
    return pl.pallas_call(
        functools.partial(kernel, dims),
        out_shape=shapes,
        in_specs=[pl.BlockSpec(memory_space=pltpu.VMEM)] * len(operands),
        out_specs=tuple(pl.BlockSpec(memory_space=pltpu.VMEM) for _ in shapes),
        scratch_shapes=scratch,
        name=name,
    )(*operands)


def body(modes_start, stiffness, mass, connect):
    modes, comps, count = modes_start.shape
    size = comps * CORNERS
    dims = (comps, modes)
    packed = size * size + 8 + comps * modes
    scratch = [
        pltpu.VMEM((comps * modes, 4 * LANES), F32),
        pltpu.VMEM((comps * modes, 4 * LANES), F32),
        pltpu.VMEM((comps * 2 * modes, 4 * LANES), BF16),
        pltpu.VMEM((comps * 2 * modes, 4 * LANES), BF16),
        pltpu.VMEM((comps * 2 * modes, 2 * LANES), F32),
    ]
    half = ((comps * modes, LANES), F32)
    prods = ((comps * 2 * modes, LANES), F32)

    up, down = call(
        pack_kernel, dims, "pack", [((packed, LANES), F32)] * 2, [], modes_start, stiffness, mass, connect
    )
    below, above = from_neighbours(up, down, "sub")
    edges, edge_nodes, p_low, p_high, gram = call(
        first_kernel,
        dims,
        "first",
        [((2, size, size, LANES), F32), ((8, LANES), jnp.int32), prods, prods, ((modes, LANES), F32)],
        scratch,
        stiffness, mass, connect, up, down, below, above,
    )
    gram = total_over(gram, "sub")
    p_below, p_above = from_neighbours(p_high, p_low, "sub")
    res_low, res_high, q_low, q_high, gram, state = call(
        second_kernel,
        dims,
        "second",
        [half, half, prods, prods, ((2 * modes, LANES), F32), ((3, modes, modes), F32)],
        scratch,
        gram, stiffness, mass, connect, edges, edge_nodes, up, down, p_below, p_low, p_high, p_above,
    )
    gram = total_over(gram, "sub")
    q_below, q_above = from_neighbours(q_high, q_low, "sub")
    new_low, new_high, gram, coeff, state = call(
        third_kernel,
        dims,
        "third",
        [half, half, ((3 * modes, LANES), F32), ((modes, 2 * modes), F32), ((2, 2 * modes, 2 * modes), F32)],
        scratch,
        gram, state, stiffness, mass, connect, edges, edge_nodes, up, down,
        p_below, p_low, p_high, p_above, q_below, q_low, q_high, q_above, res_low, res_high,
    )
    gram = total_over(gram, "sub")
    result, ritz = call(
        last_kernel,
        dims,
        "last",
        [((modes, comps, count), F32), ((modes, LANES), F32)],
        [],
        gram, coeff, state, up, down, res_low, res_high, new_low, new_high,
    )
    return result, ritz[:, 0]


def solution(mesh):
    in_specs = (
        P(None, None, ("groups", "sub")),
        P(None, None, ("groups", "sub")),
        P(None, None, ("groups", "sub")),
        P(None, ("groups", "sub")),
    )
    out_specs = (P(None, None, ("groups", "sub")), P("groups"))
    return jax.shard_map(body, mesh=mesh, in_specs=in_specs, out_specs=out_specs, check_vma=False)
```

time: 634 us -> 164 us (0.26); the launches traced: 624 us -> 164 us
  waiting for transfers between devices: 193 us -> 23.7 us
  blocking collectives: 122 us -> 0 us
  other arithmetic: 114 us -> 4.36 us
  matrix products: 96 us -> 0 us
  Pallas kernels: 0 us -> 86.4 us
  local copies, waits for them, and re-layouts: 52.9 us -> 6.7 us
  starting transfers between devices: 24.7 us -> 41.7 us
  between operations: 16.8 us -> 0.81 us
    psum x2 -> x0, waiting for transfers between devices: 186 us -> none  [body(): lax.psum((inner(basis, stiff_basis), inner(basis, mass_basis)), 'sub')]
    psum x2 -> x0, blocking collectives: 122 us -> none  [the longest x1 63.9 us: body(): lax.psum((inner(modes_start, stiff_start), inner(modes_start, mass_start)...]
    another operation x43 -> x0, other arithmetic: 109 us -> none  [the longest x18 49.6 us: lower_solve(): lax.linalg.triangular_solve(factor, rhs, left_side=True, lower=True, tran...]
    dot_general x59 -> x0, matrix products: 91.3 us -> none  [the longest x6 24.3 us: one_block(): jnp.einsum('ije,rje->rie', stiff_here, picked, precision=highest)]
    pallas_call x0 -> x5, Pallas kernels: none -> 86.4 us  [call(): pl.pallas_call(functools.partial(kernel, dims), out_shape=shapes, in_spec...]
    ppermute x12 -> x24, starting transfers between devices: 24.7 us -> 41.7 us  [the longest x18 31 us: from_partner(): return lax.ppermute(part, axis, [(i, i ^ bits) for i in range(count)])]
    ppermute x12 -> x24, waiting for transfers between devices: 7.45 us -> 23.7 us  [the longest x18 19 us: from_partner(): return lax.ppermute(part, axis, [(i, i ^ bits) for i in range(count)])]
    another operation x20 -> x0, local copies, waits for them, and re-layouts: 15.3 us -> none  [the longest x12 12.2 us: one_block(): parts = jnp.stack([stiff_part, mass_part]).reshape(2, rows, 6, 4, span)]
  transfers between devices with their start and end apart: 14 -> 24, of which waited for: 7 -> 9; matrix products, arithmetic and copies ran while one was open for 2% -> 2% of each run, Pallas kernels for 0% -> 0%
where the time goes in v1:
time: 164 us
  Pallas kernels  86.4 us (53%)
  starting transfers between devices  41.7 us (25%)
  waiting for transfers between devices  23.7 us (14%)
  local copies, waits for them, and re-layouts  6.7 us (4%)
  other arithmetic  4.36 us (3%)
    pallas_call x5, Pallas kernels, call(): pl.pallas_call(functools.partial(kernel, dims), out_shape=shapes, in_spec...  86.4 us
    ppermute x18, starting transfers between devices, from_partner(): return lax.ppermute(part, axis, [(i, i ^ bits) for i in range(count)])  31 us
    ppermute x18, waiting for transfers between devices, from_partner(): return lax.ppermute(part, axis, [(i, i ^ bits) for i in range(count)])  19 us
    ppermute x3, starting transfers between devices, from_neighbours(): below = lax.ppermute(upward, axis, [(i, i + 1) for i in range(count - 1)])  6.63 us
    unnamed x16, local copies, waits for them, and re-layouts  6.07 us
    ppermute x3, waiting for transfers between devices, from_neighbours(): above = lax.ppermute(downward, axis, [(i + 1, i) for i in range(count - 1)])  4.41 us
    add x6, other arithmetic, total_over(): value = value + one + (two + three)  4.36 us
    ppermute x3, starting transfers between devices, from_neighbours(): above = lax.ppermute(downward, axis, [(i + 1, i) for i in range(count - 1)])  4.06 us
  transfers between devices with their start and end apart: 24, of which 9 were waited for; matrix products, arithmetic and copies ran while one was open for 2% of the time, Pallas kernels for 0%

profile of v1, /device:TPU:0, one launch (start us, length us, event | category | flops | bytes accessed | tf_op | source)
XLA Modules:
  0.0 163.6 jit_solution(12980774575701448720)
XLA Ops:
  0.6 1.9 %copy.8.block = f32[48,6,256]{2,1,0:T(8,128)} copy(f32[48,6,256]{2,0,1:T(8,128)} %param.4) | data formatting | bytes 589824 | tf_op args[0]
  2.5 4.2 %pack.1 = (f32[872,128]{1,0:T(8,128)}, f32[872,128]{1,0:T(8,128)}) custom-call(f32[48,6,256]{2,1,0:T(8,128)} %copy.8.block, f32[24,24,256]{2,1,0:T(8,128)} %stiffness.7, f32[24,24,256]{2,1,0:T(8,128)} %mass.7, s32[4,256]{1,0:T(4,128)} %connect.7), custom_call_target="tpu_custom_call" | custom-call | tf_op jit(solution)/shard_map/pack/pallas_call | solution.py:334
  6.7 2.4 %collective-permute-start = (f32[872,128]{1,0:T(8,128)}, f32[872,128]{1,0:T(8,128)S(1)}, u32[]{:S(2)}, u32[]{:S(2)}) collective-permute-start(f32[872,128]{1,0:T(8,128)} %get-tuple-element.22.up), channel_id=1, source_target_pairs={{0,1},{1,2},{2,3},{3,4},{4,5},{5,6},{6,7},{7,8},{8,9},{9,10},{10,1... | collective-permute-start | bytes 1339400 | tf_op jit(solution)/shard_map/ppermute | solution.py:327
  9.1 1.3 collective-permute-start.1
  10.4 0.3 collective-permute-done.below
  10.7 4.4 %collective-permute-done.1.above = f32[872,128]{1,0:T(8,128)S(1)} collective-permute-done((f32[872,128]{1,0:T(8,128)}, f32[872,128]{1,0:T(8,128)S(1)}, u32[]{:S(2)}, u32[]{:S(2)}) %collective-permute-start.1) | collective-permute-done | bytes 446496 | tf_op jit(solution)/shard_map/ppermute | solution.py:328
  15.1 0.8 copy-done.3
  15.9 14.3 %first.1 = (f32[2,24,24,128]{3,2,1,0:T(8,128)}, s32[8,128]{1,0:T(8,128)}, f32[576,128]{1,0:T(8,128)}, f32[576,128]{1,0:T(8,128)}, f32[48,128]{1,0:T(8,128)}) custom-call(f32[24,24,256]{2,1,0:T(8,128)} %stiffness.7, f32[24,24,256]{2,1,0:T(8,128)} %mass.7, s32[4,256]{1,0:T(4,128)} %connect.7, f32[872,128]{1,0:T(8,128)} %get-tuple-element.22.up, ...), custom_call_target="tpu_custom_call" | custom-call | tf_op jit(solution)/shard_map/first/pallas_call | solution.py:334
  30.2 8.6 %collective-permute-start.4 = (f32[48,128]{1,0:T(8,128)}, f32[48,128]{1,0:T(8,128)S(1)}, u32[]{:S(2)}, u32[]{:S(2)}) collective-permute-start(f32[48,128]{1,0:T(8,128)} %get-tuple-element.24), channel_id=1, source_target_pairs={{0,3},{1,2},{2,1},{3,0},{4,7},{5,6},{6,5},{7,4},{8,11},{9,10},{10,... | collective-permute-start | bytes 73736 | tf_op jit(solution)/shard_map/ppermute | solution.py:311
  38.8 1.4 collective-permute-start.3
  40.2 0.1 collective-permute-start.2
  40.3 2.3 %collective-permute-start.8 = (f32[576,128]{1,0:T(8,128)}, f32[576,128]{1,0:T(8,128)S(1)}, u32[]{:S(2)}, u32[]{:S(2)}) collective-permute-start(f32[576,128]{1,0:T(8,128)} %get-tuple-element.27.p_high), channel_id=1, source_target_pairs={{0,1},{1,2},{2,3},{3,4},{4,5},{5,6},{6,7},{7,8},{8,9},{9,10},{10,1... | collective-permute-start | bytes 884744 | tf_op jit(solution)/shard_map/ppermute | solution.py:327
  42.6 1.3 collective-permute-start.9
  43.9 0.0 collective-permute-done.4
  43.9 0.0 collective-permute-done.3
  43.9 0.0 collective-permute-done.2
  43.9 0.7 add_add_fusion.5
  44.7 6.4 %collective-permute-start.7 = (f32[48,128]{1,0:T(8,128)S(1)}, f32[48,128]{1,0:T(8,128)S(1)}, u32[]{:S(2)}, u32[]{:S(2)}) collective-permute-start(f32[48,128]{1,0:T(8,128)S(1)} %add_add_fusion.5), channel_id=1, source_target_pairs={{0,12},{1,13},{2,14},{3,15},{4,8},{5,9},{6,10},{7,11},{8,4},{9,5},... | collective-permute-start | bytes 73736 | tf_op jit(solution)/shard_map/ppermute | solution.py:311
  51.1 0.0 collective-permute-start.6
  51.1 0.6 collective-permute-start.5
  51.7 4.4 %collective-permute-done.7 = f32[48,128]{1,0:T(8,128)S(1)} collective-permute-done((f32[48,128]{1,0:T(8,128)S(1)}, f32[48,128]{1,0:T(8,128)S(1)}, u32[]{:S(2)}, u32[]{:S(2)}) %collective-permute-start.7) | collective-permute-done | bytes 24608 | tf_op jit(solution)/shard_map/ppermute | solution.py:311
  56.1 0.0 collective-permute-done.6
  56.1 0.0 collective-permute-done.5
  56.1 0.6 add_add_fusion.4.gram_in
  56.7 0.0 collective-permute-done.8.p_below
  56.7 0.0 collective-permute-done.9.p_above
  56.7 0.7 copy-done
  57.4 0.1 copy-done.1
  57.5 19.3 %second.1 = (f32[288,128]{1,0:T(8,128)}, f32[288,128]{1,0:T(8,128)}, f32[576,128]{1,0:T(8,128)}, f32[576,128]{1,0:T(8,128)}, f32[96,128]{1,0:T(8,128)}, /*index=5*/f32[3,48,48]{2,1,0:T(8,128)}) custom-call(f32[48,128]{1,0:T(8,128)} %add_add_fusion.4.gram_in, f32[24,24,256]{2,1,0:T(8,128)} %stiffness.7, f32[24,24,256]{2,1,0:T(8,128)} %mass.7, ...), custom_call_target="tpu_custom_call" | custom-call | tf_op jit(solution)/shard_map/second/pallas_call | solution.py:334
  76.8 0.1 collective-permute-start.12
  76.9 0.1 collective-permute-start.11
  77.0 1.8 %collective-permute-start.10 = (f32[96,128]{1,0:T(8,128)}, f32[96,128]{1,0:T(8,128)S(1)}, u32[]{:S(2)}, u32[]{:S(2)}) collective-permute-start(f32[96,128]{1,0:T(8,128)} %get-tuple-element.29), channel_id=1, source_target_pairs={{0,1},{1,0},{2,3},{3,2},{4,5},{5,4},{6,7},{7,6},{8,9},{9,8},{10,11... | collective-permute-start | bytes 147464 | tf_op jit(solution)/shard_map/ppermute | solution.py:311
  78.7 1.9 %collective-permute-start.16 = (f32[576,128]{1,0:T(8,128)}, f32[576,128]{1,0:T(8,128)S(1)}, u32[]{:S(2)}, u32[]{:S(2)}) collective-permute-start(f32[576,128]{1,0:T(8,128)} %get-tuple-element.31.q_high), channel_id=1, source_target_pairs={{0,1},{1,2},{2,3},{3,4},{4,5},{5,6},{6,7},{7,8},{8,9},{9,10},{10,1... | collective-permute-start | bytes 884744 | tf_op jit(solution)/shard_map/ppermute | solution.py:327
  80.7 1.5 collective-permute-start.17
  82.2 0.0 collective-permute-done.10
  82.2 0.8 add_add_fusion.3
  83.0 4.5 %collective-permute-start.15 = (f32[96,128]{1,0:T(8,128)S(1)}, f32[96,128]{1,0:T(8,128)S(1)}, u32[]{:S(2)}, u32[]{:S(2)}) collective-permute-start(f32[96,128]{1,0:T(8,128)S(1)} %add_add_fusion.3), channel_id=1, source_target_pairs={{0,12},{1,13},{2,14},{3,15},{4,8},{5,9},{6,10},{7,11},{8,4},{9,5},... | collective-permute-start | bytes 147464 | tf_op jit(solution)/shard_map/ppermute | solution.py:311
  87.5 1.1 collective-permute-start.14
  88.6 0.0 collective-permute-start.13
  88.6 4.9 %collective-permute-done.15 = f32[96,128]{1,0:T(8,128)S(1)} collective-permute-done((f32[96,128]{1,0:T(8,128)S(1)}, f32[96,128]{1,0:T(8,128)S(1)}, u32[]{:S(2)}, u32[]{:S(2)}) %collective-permute-start.15) | collective-permute-done | bytes 49184 | tf_op jit(solution)/shard_map/ppermute | solution.py:311
  93.5 2.0 %collective-permute-done.14 = f32[96,128]{1,0:T(8,128)S(1)} collective-permute-done((f32[96,128]{1,0:T(8,128)S(1)}, f32[96,128]{1,0:T(8,128)S(1)}, u32[]{:S(2)}, u32[]{:S(2)}) %collective-permute-start.14) | collective-permute-done | bytes 49184 | tf_op jit(solution)/shard_map/ppermute | solution.py:311
  95.4 0.0 collective-permute-done.13
  95.4 0.6 add_add_fusion.2.gram_in
  96.1 0.0 collective-permute-done.16.q_below
  96.1 0.0 collective-permute-done.17.q_above
  96.1 0.7 copy-done.4
  96.8 0.1 copy-done.5
  96.9 30.7 %third.1 = (f32[288,128]{1,0:T(8,128)}, f32[288,128]{1,0:T(8,128)}, f32[144,128]{1,0:T(8,128)}, f32[48,96]{1,0:T(8,128)}, f32[2,96,96]{2,1,0:T(8,128)}) custom-call(f32[96,128]{1,0:T(8,128)} %add_add_fusion.2.gram_in, f32[3,48,48]{2,1,0:T(8,128)} %get-tuple-element.30.state_in, f32[24,24,256]{2,1,0:T(8,128)} %stiffness.7, f32[24,24,256]{2,1,0:T(8,128)} %mass.7, ...), custom_call_target="tpu_custom_call" | custom-call | tf_op jit(solution)/shard_map/third/pallas_call | solution.py:334
  127.6 0.1 collective-permute-start.20
  127.7 0.1 collective-permute-start.19
  127.8 1.8 %collective-permute-start.18 = (f32[144,128]{1,0:T(8,128)}, f32[144,128]{1,0:T(8,128)S(1)}, u32[]{:S(2)}, u32[]{:S(2)}) collective-permute-start(f32[144,128]{1,0:T(8,128)} %get-tuple-element.35), channel_id=1, source_target_pairs={{0,1},{1,0},{2,3},{3,2},{4,5},{5,4},{6,7},{7,6},{8,9},{9,8},{10,11... | collective-permute-start | bytes 221192 | tf_op jit(solution)/shard_map/ppermute | solution.py:311
  129.5 2.3 %collective-permute-done.20 = f32[144,128]{1,0:T(8,128)S(1)} collective-permute-done((f32[144,128]{1,0:T(8,128)}, f32[144,128]{1,0:T(8,128)S(1)}, u32[]{:S(2)}, u32[]{:S(2)}) %collective-permute-start.20) | collective-permute-done | bytes 73760 | tf_op jit(solution)/shard_map/ppermute | solution.py:311
  131.8 1.3 collective-permute-done.19
  133.1 0.9 add_add_fusion.1
  134.0 0.1 collective-permute-start.23
  134.1 1.5 collective-permute-start.22
  135.6 2.9 %collective-permute-start.21 = (f32[144,128]{1,0:T(8,128)S(1)}, f32[144,128]{1,0:T(8,128)S(1)}, u32[]{:S(2)}, u32[]{:S(2)}) collective-permute-start(f32[144,128]{1,0:T(8,128)S(1)} %add_add_fusion.1), channel_id=1, source_target_pairs={{0,4},{1,5},{2,6},{3,7},{4,0},{5,1},{6,2},{7,3},{8,12},{9,13},{10,... | collective-permute-start | bytes 221192 | tf_op jit(solution)/shard_map/ppermute | solution.py:311
  138.5 2.6 %collective-permute-done.23 = f32[144,128]{1,0:T(8,128)S(1)} collective-permute-done((f32[144,128]{1,0:T(8,128)S(1)}, f32[144,128]{1,0:T(8,128)S(1)}, u32[]{:S(2)}, u32[]{:S(2)}) %collective-permute-start.23) | collective-permute-done | bytes 73760 | tf_op jit(solution)/shard_map/ppermute | solution.py:311
  141.1 1.6 collective-permute-done.22
  142.6 0.0 collective-permute-done.21
  142.6 0.7 add_add_fusion.gram_in
  143.3 17.9 %last.1 = (f32[48,6,256]{2,1,0:T(8,128)}, f32[48,128]{1,0:T(8,128)}) custom-call(f32[144,128]{1,0:T(8,128)} %add_add_fusion.gram_in, f32[48,96]{1,0:T(8,128)} %get-tuple-element.36.coeff_in, f32[2,96,96]{2,1,0:T(8,128)} %get-tuple-element.37.state_in, f32[872,128]{1,0:T(8,128)} %get-tuple-element.22.up, f32[872,128]{1,0:T(8,128)} %get-tuple-element.23.down, ...), custom_call_target="tpu_custom_call" | custom-call | tf_op jit(solution)/shard_map/last/pallas_call | solution.py:334
  161.2 1.8 %copy.9 = f32[48,6,256]{2,0,1:T(8,128)} copy(f32[48,6,256]{2,1,0:T(8,128)} %get-tuple-element.44) | data formatting | bytes 589824
  163.0 0.6 slice_reduce_fusion
  (12 shorter events, 0.0 us)
Async XLA Ops:
  6.7 4.0 %collective-permute-start = (f32[872,128]{1,0:T(8,128)}, f32[872,128]{1,0:T(8,128)S(1)}, u32[]{:S(2)}, u32[]{:S(2)}) collective-permute-start(f32[872,128]{1,0:T(8,128)} %get-tuple-element.22.up), channel_id=1, source_target_pairs={{0,1},{1,2},{2,3},{3,4},{4,5},{5,6},{6,7},{7,8},{8,9},{9,10},{10,1... | collective-permute-start | bytes 1339400 | tf_op jit(solution)/shard_map/ppermute | solution.py:327
  9.1 6.0 %collective-permute-start.1 = (f32[872,128]{1,0:T(8,128)}, f32[872,128]{1,0:T(8,128)S(1)}, u32[]{:S(2)}, u32[]{:S(2)}) collective-permute-start(f32[872,128]{1,0:T(8,128)} %get-tuple-element.23.down), channel_id=1, source_target_pairs={{1,0},{2,1},{3,2},{4,3},{5,4},{6,5},{7,6},{8,7},{9,8},{10,9},{11,1... | collective-permute-start | bytes 1339400 | tf_op jit(solution)/shard_map/ppermute | solution.py:328
  10.7 4.4 %copy-start.2 = (f32[872,128]{1,0:T(8,128)}, f32[872,128]{1,0:T(8,128)S(1)}, u32[]{:S(2)}) copy-start(f32[872,128]{1,0:T(8,128)S(1)} %collective-permute-done.below) | copy-start | bytes 1339396
  15.1 0.8 copy-start.3
  30.2 13.7 %collective-permute-start.4 = (f32[48,128]{1,0:T(8,128)}, f32[48,128]{1,0:T(8,128)S(1)}, u32[]{:S(2)}, u32[]{:S(2)}) collective-permute-start(f32[48,128]{1,0:T(8,128)} %get-tuple-element.24), channel_id=1, source_target_pairs={{0,3},{1,2},{2,1},{3,0},{4,7},{5,6},{6,5},{7,4},{8,11},{9,10},{10,... | collective-permute-start | bytes 73736 | tf_op jit(solution)/shard_map/ppermute | solution.py:311
  38.8 5.1 %collective-permute-start.3 = (f32[48,128]{1,0:T(8,128)}, f32[48,128]{1,0:T(8,128)S(1)}, u32[]{:S(2)}, u32[]{:S(2)}) collective-permute-start(f32[48,128]{1,0:T(8,128)} %get-tuple-element.24), channel_id=1, source_target_pairs={{0,2},{1,3},{2,0},{3,1},{4,6},{5,7},{6,4},{7,5},{8,10},{9,11},{10,... | collective-permute-start | bytes 73736 | tf_op jit(solution)/shard_map/ppermute | solution.py:311
  40.2 3.8 %collective-permute-start.2 = (f32[48,128]{1,0:T(8,128)}, f32[48,128]{1,0:T(8,128)S(1)}, u32[]{:S(2)}, u32[]{:S(2)}) collective-permute-start(f32[48,128]{1,0:T(8,128)} %get-tuple-element.24), channel_id=1, source_target_pairs={{0,1},{1,0},{2,3},{3,2},{4,5},{5,4},{6,7},{7,6},{8,9},{9,8},{10,11... | collective-permute-start | bytes 73736 | tf_op jit(solution)/shard_map/ppermute | solution.py:311
  40.3 16.4 %collective-permute-start.8 = (f32[576,128]{1,0:T(8,128)}, f32[576,128]{1,0:T(8,128)S(1)}, u32[]{:S(2)}, u32[]{:S(2)}) collective-permute-start(f32[576,128]{1,0:T(8,128)} %get-tuple-element.27.p_high), channel_id=1, source_target_pairs={{0,1},{1,2},{2,3},{3,4},{4,5},{5,6},{6,7},{7,8},{8,9},{9,10},{10,1... | collective-permute-start | bytes 884744 | tf_op jit(solution)/shard_map/ppermute | solution.py:327
  42.6 14.1 %collective-permute-start.9 = (f32[576,128]{1,0:T(8,128)}, f32[576,128]{1,0:T(8,128)S(1)}, u32[]{:S(2)}, u32[]{:S(2)}) collective-permute-start(f32[576,128]{1,0:T(8,128)} %get-tuple-element.28.p_low), channel_id=1, source_target_pairs={{1,0},{2,1},{3,2},{4,3},{5,4},{6,5},{7,6},{8,7},{9,8},{10,9},{11,1... | collective-permute-start | bytes 884744 | tf_op jit(solution)/shard_map/ppermute | solution.py:328
  44.7 11.4 %collective-permute-start.7 = (f32[48,128]{1,0:T(8,128)S(1)}, f32[48,128]{1,0:T(8,128)S(1)}, u32[]{:S(2)}, u32[]{:S(2)}) collective-permute-start(f32[48,128]{1,0:T(8,128)S(1)} %add_add_fusion.5), channel_id=1, source_target_pairs={{0,12},{1,13},{2,14},{3,15},{4,8},{5,9},{6,10},{7,11},{8,4},{9,5},... | collective-permute-start | bytes 73736 | tf_op jit(solution)/shard_map/ppermute | solution.py:311
  51.1 5.0 %collective-permute-start.6 = (f32[48,128]{1,0:T(8,128)S(1)}, f32[48,128]{1,0:T(8,128)S(1)}, u32[]{:S(2)}, u32[]{:S(2)}) collective-permute-start(f32[48,128]{1,0:T(8,128)S(1)} %add_add_fusion.5), channel_id=1, source_target_pairs={{0,8},{1,9},{2,10},{3,11},{4,12},{5,13},{6,14},{7,15},{8,0},{9,1},... | collective-permute-start | bytes 73736 | tf_op jit(solution)/shard_map/ppermute | solution.py:311
  51.1 5.0 %collective-permute-start.5 = (f32[48,128]{1,0:T(8,128)S(1)}, f32[48,128]{1,0:T(8,128)S(1)}, u32[]{:S(2)}, u32[]{:S(2)}) collective-permute-start(f32[48,128]{1,0:T(8,128)S(1)} %add_add_fusion.5), channel_id=1, source_target_pairs={{0,4},{1,5},{2,6},{3,7},{4,0},{5,1},{6,2},{7,3},{8,12},{9,13},{10,... | collective-permute-start | bytes 73736 | tf_op jit(solution)/shard_map/ppermute | solution.py:311
  56.7 0.7 copy-start
  56.7 0.8 copy-start.1
  76.8 5.3 %collective-permute-start.12 = (f32[96,128]{1,0:T(8,128)}, f32[96,128]{1,0:T(8,128)S(1)}, u32[]{:S(2)}, u32[]{:S(2)}) collective-permute-start(f32[96,128]{1,0:T(8,128)} %get-tuple-element.29), channel_id=1, source_target_pairs={{0,3},{1,2},{2,1},{3,0},{4,7},{5,6},{6,5},{7,4},{8,11},{9,10},{10,... | collective-permute-start | bytes 147464 | tf_op jit(solution)/shard_map/ppermute | solution.py:311
  76.9 5.3 %collective-permute-start.11 = (f32[96,128]{1,0:T(8,128)}, f32[96,128]{1,0:T(8,128)S(1)}, u32[]{:S(2)}, u32[]{:S(2)}) collective-permute-start(f32[96,128]{1,0:T(8,128)} %get-tuple-element.29), channel_id=1, source_target_pairs={{0,2},{1,3},{2,0},{3,1},{4,6},{5,7},{6,4},{7,5},{8,10},{9,11},{10,... | collective-permute-start | bytes 147464 | tf_op jit(solution)/shard_map/ppermute | solution.py:311
  77.0 5.2 %collective-permute-start.10 = (f32[96,128]{1,0:T(8,128)}, f32[96,128]{1,0:T(8,128)S(1)}, u32[]{:S(2)}, u32[]{:S(2)}) collective-permute-start(f32[96,128]{1,0:T(8,128)} %get-tuple-element.29), channel_id=1, source_target_pairs={{0,1},{1,0},{2,3},{3,2},{4,5},{5,4},{6,7},{7,6},{8,9},{9,8},{10,11... | collective-permute-start | bytes 147464 | tf_op jit(solution)/shard_map/ppermute | solution.py:311
  78.7 17.4 %collective-permute-start.16 = (f32[576,128]{1,0:T(8,128)}, f32[576,128]{1,0:T(8,128)S(1)}, u32[]{:S(2)}, u32[]{:S(2)}) collective-permute-start(f32[576,128]{1,0:T(8,128)} %get-tuple-element.31.q_high), channel_id=1, source_target_pairs={{0,1},{1,2},{2,3},{3,4},{4,5},{5,6},{6,7},{7,8},{8,9},{9,10},{10,1... | collective-permute-start | bytes 884744 | tf_op jit(solution)/shard_map/ppermute | solution.py:327
  80.7 15.4 %collective-permute-start.17 = (f32[576,128]{1,0:T(8,128)}, f32[576,128]{1,0:T(8,128)S(1)}, u32[]{:S(2)}, u32[]{:S(2)}) collective-permute-start(f32[576,128]{1,0:T(8,128)} %get-tuple-element.32.q_low), channel_id=1, source_target_pairs={{1,0},{2,1},{3,2},{4,3},{5,4},{6,5},{7,6},{8,7},{9,8},{10,9},{11,1... | collective-permute-start | bytes 884744 | tf_op jit(solution)/shard_map/ppermute | solution.py:328
  83.0 10.5 %collective-permute-start.15 = (f32[96,128]{1,0:T(8,128)S(1)}, f32[96,128]{1,0:T(8,128)S(1)}, u32[]{:S(2)}, u32[]{:S(2)}) collective-permute-start(f32[96,128]{1,0:T(8,128)S(1)} %add_add_fusion.3), channel_id=1, source_target_pairs={{0,12},{1,13},{2,14},{3,15},{4,8},{5,9},{6,10},{7,11},{8,4},{9,5},... | collective-permute-start | bytes 147464 | tf_op jit(solution)/shard_map/ppermute | solution.py:311
  87.5 8.0 %collective-permute-start.14 = (f32[96,128]{1,0:T(8,128)S(1)}, f32[96,128]{1,0:T(8,128)S(1)}, u32[]{:S(2)}, u32[]{:S(2)}) collective-permute-start(f32[96,128]{1,0:T(8,128)S(1)} %add_add_fusion.3), channel_id=1, source_target_pairs={{0,8},{1,9},{2,10},{3,11},{4,12},{5,13},{6,14},{7,15},{8,0},{9,1},... | collective-permute-start | bytes 147464 | tf_op jit(solution)/shard_map/ppermute | solution.py:311
  88.6 6.9 %collective-permute-start.13 = (f32[96,128]{1,0:T(8,128)S(1)}, f32[96,128]{1,0:T(8,128)S(1)}, u32[]{:S(2)}, u32[]{:S(2)}) collective-permute-start(f32[96,128]{1,0:T(8,128)S(1)} %add_add_fusion.3), channel_id=1, source_target_pairs={{0,4},{1,5},{2,6},{3,7},{4,0},{5,1},{6,2},{7,3},{8,12},{9,13},{10,... | collective-permute-start | bytes 147464 | tf_op jit(solution)/shard_map/ppermute | solution.py:311
  96.1 0.7 copy-start.4
  96.1 0.8 copy-start.5
  127.6 4.2 %collective-permute-start.20 = (f32[144,128]{1,0:T(8,128)}, f32[144,128]{1,0:T(8,128)S(1)}, u32[]{:S(2)}, u32[]{:S(2)}) collective-permute-start(f32[144,128]{1,0:T(8,128)} %get-tuple-element.35), channel_id=1, source_target_pairs={{0,3},{1,2},{2,1},{3,0},{4,7},{5,6},{6,5},{7,4},{8,11},{9,10},{10,... | collective-permute-start | bytes 221192 | tf_op jit(solution)/shard_map/ppermute | solution.py:311
  127.7 5.4 %collective-permute-start.19 = (f32[144,128]{1,0:T(8,128)}, f32[144,128]{1,0:T(8,128)S(1)}, u32[]{:S(2)}, u32[]{:S(2)}) collective-permute-start(f32[144,128]{1,0:T(8,128)} %get-tuple-element.35), channel_id=1, source_target_pairs={{0,2},{1,3},{2,0},{3,1},{4,6},{5,7},{6,4},{7,5},{8,10},{9,11},{10,... | collective-permute-start | bytes 221192 | tf_op jit(solution)/shard_map/ppermute | solution.py:311
  127.8 5.3 %collective-permute-start.18 = (f32[144,128]{1,0:T(8,128)}, f32[144,128]{1,0:T(8,128)S(1)}, u32[]{:S(2)}, u32[]{:S(2)}) collective-permute-start(f32[144,128]{1,0:T(8,128)} %get-tuple-element.35), channel_id=1, source_target_pairs={{0,1},{1,0},{2,3},{3,2},{4,5},{5,4},{6,7},{7,6},{8,9},{9,8},{10,11... | collective-permute-start | bytes 221192 | tf_op jit(solution)/shard_map/ppermute | solution.py:311
  134.0 7.0 %collective-permute-start.23 = (f32[144,128]{1,0:T(8,128)S(1)}, f32[144,128]{1,0:T(8,128)S(1)}, u32[]{:S(2)}, u32[]{:S(2)}) collective-permute-start(f32[144,128]{1,0:T(8,128)S(1)} %add_add_fusion.1), channel_id=1, source_target_pairs={{0,12},{1,13},{2,14},{3,15},{4,8},{5,9},{6,10},{7,11},{8,4},{9,5},... | collective-permute-start | bytes 221192 | tf_op jit(solution)/shard_map/ppermute | solution.py:311
  134.1 8.6 %collective-permute-start.22 = (f32[144,128]{1,0:T(8,128)S(1)}, f32[144,128]{1,0:T(8,128)S(1)}, u32[]{:S(2)}, u32[]{:S(2)}) collective-permute-start(f32[144,128]{1,0:T(8,128)S(1)} %add_add_fusion.1), channel_id=1, source_target_pairs={{0,8},{1,9},{2,10},{3,11},{4,12},{5,13},{6,14},{7,15},{8,0},{9,1},... | collective-permute-start | bytes 221192 | tf_op jit(solution)/shard_map/ppermute | solution.py:311
  135.6 7.1 %collective-permute-start.21 = (f32[144,128]{1,0:T(8,128)S(1)}, f32[144,128]{1,0:T(8,128)S(1)}, u32[]{:S(2)}, u32[]{:S(2)}) collective-permute-start(f32[144,128]{1,0:T(8,128)S(1)} %add_add_fusion.1), channel_id=1, source_target_pairs={{0,4},{1,5},{2,6},{3,7},{4,0},{5,1},{6,2},{7,3},{8,12},{9,13},{10,... | collective-permute-start | bytes 221192 | tf_op jit(solution)/shard_map/ppermute | solution.py:311
  161.2 1.8 %copy-start.6 = (f32[48,128]{1,0:T(8,128)S(1)}, f32[48,128]{1,0:T(8,128)}, u32[]{:S(2)}) copy-start(f32[48,128]{1,0:T(8,128)} %get-tuple-element.41) | copy-start | bytes 73732

commit v2 on v1

v2 whole, which is shorter than its diff:
```python
import functools

import jax
import jax.numpy as jnp
from jax import lax
from jax.experimental import pallas as pl
from jax.experimental.pallas import tpu as pltpu
from jax.sharding import PartitionSpec as P

HALO = 64
LANES = 128
SUB = 8
CORNERS = 4
F32 = jnp.float32
BF16 = jnp.bfloat16

NN = (((1,), (0,)), ((), ()))
NT = (((1,), (1,)), ((), ()))
TN = (((0,), (0,)), ((), ()))


def split(value):
    high = value.astype(BF16)
    return high, (value - high.astype(F32)).astype(BF16)


def dot1(left, right, dims):
    return lax.dot_general(left, right, dims, preferred_element_type=F32)


def dot3(left, right, dims=NN):
    left_high, left_low = split(left)
    right_high, right_low = split(right)
    return dot1(left_high, right_high, dims) + (
        dot1(left_high, right_low, dims) + dot1(left_low, right_high, dims)
    )


def dotf(left, right, dims=NN):
    return lax.dot_general(
        left, right, dims, precision=lax.Precision.HIGHEST, preferred_element_type=F32
    )


def symmetric(matrix):
    return 0.5 * (matrix + matrix.T)


def whole(row):
    return jnp.broadcast_to(row,(SUB,row.shape[1]))
def eliminate(matrix, others, modes):
    tiles = modes // SUB
    chunks = []
    for other in others:
        for start in range(0, other.shape[1], LANES):
            chunks.append(other[:, start : start + LANES])
    unit = 1.0 / matrix[:1, :1]
    matrix = matrix * unit
    root = jnp.sqrt(jnp.broadcast_to(unit, (SUB, LANES)))
    left = [matrix[SUB * t : SUB * (t + 1), :] for t in range(tiles)]
    rest = [[chunk[SUB * t : SUB * (t + 1), :] for t in range(tiles)] for chunk in chunks]
    line = lax.broadcasted_iota(jnp.int32, (SUB, LANES), 0)
    outs = [[] for _ in chunks]
    for g in range(tiles):
        cols = [
            [jnp.broadcast_to(left[t][:, SUB * g + j : SUB * g + j + 1], (SUB, LANES)) for t in range(g, tiles)]
            for j in range(SUB)
        ]
        head = jnp.ones((SUB, LANES), F32)
        cross = jnp.zeros((SUB, LANES), F32)
        area = jnp.ones((SUB, LANES), F32)
        for s in range(0, SUB, 2):
            a = whole(cols[s][0][s : s + 1, :])
            b = whole(cols[s][0][s + 1 : s + 2, :])
            d = whole(cols[s + 1][0][s + 1 : s + 2, :])
            det = a * d - b * b
            inverse = 1.0 / det
            mine = (line // 2) == (s // 2)
            head = jnp.where(mine, a, head)
            cross = jnp.where(mine, b, cross)
            area = jnp.where(mine, det, area)
            p, q, r = d * inverse, b * inverse, a * inverse
            first, second = [], []
            for n, (x, y) in enumerate(zip(cols[s], cols[s + 1])):
                f0 = x * p - y * q
                f1 = y * r - x * q
                if n == 0:
                    f0 = jnp.where(line > s + 1, f0, 0.0)
                    f1 = jnp.where(line > s + 1, f1, 0.0)
                first.append(f0)
                second.append(f1)
            for j in range(s + 2, SUB):
                r0 = whole(cols[j][0][s : s + 1, :])
                r1 = whole(cols[j][0][s + 1 : s + 2, :])
                cols[j] = [c - (f0 * r0 + f1 * r1) for c, f0, f1 in zip(cols[j], first, second)]
            for group in ([left] if g + 1 < tiles else []) + rest:
                width = group[g].shape[1]
                r0 = whole(group[g][s : s + 1, :])
                r1 = whole(group[g][s + 1 : s + 2, :])
                for n, t in enumerate(range(g, tiles)):
                    if n == 0 and s + 2 == SUB:
                        continue
                    group[t] = group[t] - (first[n][:, :width] * r0 + second[n][:, :width] * r1)
        odd = (line % 2) == 1
        scale = lax.rsqrt(jnp.where(odd, area * head, head)) * root
        own = jnp.where(odd, head * scale, scale)
        mix = jnp.where(odd, cross * scale, 0.0)
        for i, group in enumerate(rest):
            width = group[g].shape[1]
            above = jnp.concatenate([group[g][SUB - 1 :, :], group[g][: SUB - 1, :]], axis=0)
            outs[i].append(own[:, :width] * group[g] - mix[:, :width] * above)
    joined = [jnp.concatenate(parts, axis=0) for parts in outs]
    results, at = [], 0
    for other in others:
        count = -(-other.shape[1] // LANES)
        part = joined[at : at + count]
        results.append(part[0] if count == 1 else jnp.concatenate(part, axis=1))
        at += count
    return results


def eye(modes):
    row = lax.broadcasted_iota(jnp.int32, (modes, modes), 0)
    col = lax.broadcasted_iota(jnp.int32, (modes, modes), 1)
    return (row == col).astype(F32)


def store_lanes(ref, value):
    rows, width = value.shape
    ref[0:rows, 0:width] = value


def element_products(dims, halves, stiff, weigh, lane, nodes, base, window, picked, high, low):
    comps, modes = dims
    place = lax.broadcasted_iota(jnp.int32, (window, LANES), 0) + base
    chosen = jnp.concatenate(
        [(place == nodes[a : a + 1, :]).astype(F32).astype(BF16) for a in range(CORNERS)], axis=1
    )
    picked[...] = dot1(halves[0][:, base : base + window], chosen, NN) + dot1(
        halves[1][:, base : base + window], chosen, NN
    )

    def one(step, unused):
        comp = step // 2
        pair = (step % 2) * 2
        totals = [jnp.zeros((modes, LANES), F32) for _ in range(4)]
        for j in range(comps * CORNERS):
            start = (j // CORNERS) * modes
            value = picked[start : start + modes, (j % CORNERS) * LANES : (j % CORNERS + 1) * LANES]
            for q in range(2):
                for m, matrix in enumerate((stiff, weigh)):
                    entry = matrix[comp * CORNERS + pair + q, j : j + 1, lane : lane + LANES]
                    totals[2 * q + m] = totals[2 * q + m] + entry * value
        for q in range(2):
            for m in range(2):
                upper, lower = split(totals[2 * q + m])
                row = pl.multiple_of((comp * 2 + m) * modes, 16)
                col = pl.multiple_of((pair + q) * LANES, LANES)
                high[pl.ds(row, modes), pl.ds(col, LANES)] = upper
                low[pl.ds(row, modes), pl.ds(col, LANES)] = lower
        return unused

    lax.fori_loop(0, comps * 2, one, 0)
    target = chosen[LANES - base : 3 * LANES - base, :]
    return dot1(high[...], target, NT) + dot1(low[...], target, NT)


def own_products(dims, halves, stiffness, mass, connect, picked, high, low, out):
    nodes = connect[...] + (LANES - HALO)
    for number in range(2):
        lane = number * LANES
        total = element_products(
            dims, halves, stiffness, mass, lane, nodes[:, lane : lane + LANES], lane, 3 * LANES, picked, high, low
        )
        if number == 0:
            out[...] = total
        else:
            out[...] += total


def edge_products(dims, halves, edges, edge_nodes, picked, high, low, out):
    out[...] += element_products(
        dims, halves, edges.at[0], edges.at[1], 0, edge_nodes, 0, 4 * LANES, picked, high, low
    )


def grams(basis, products, dims):
    comps, modes = dims
    total = None
    for c in range(comps):
        left = jnp.concatenate([part[c * modes : (c + 1) * modes, :] for part in basis], axis=0)
        right = products[c * 2 * modes : (c + 1) * 2 * modes, :]
        term = dot3(left, right, NT)
        total = term if total is None else total + term
    return total


def pack_kernel(dims, stiffness, mass, connect, up, down):
    comps, modes = dims
    size = comps * CORNERS
    first = lax.broadcasted_iota(jnp.int32, (size, LANES), 1) < HALO

    def one(i, unused):
        row = pl.multiple_of(i * size, 8)
        up[pl.ds(row, size), :] = jnp.where(
            first, pltpu.roll(stiffness[i, :, LANES:], HALO, 1), mass[i, :, LANES:]
        )
        down[pl.ds(row, size), :] = jnp.where(
            first, stiffness[i, :, :LANES], pltpu.roll(mass[i, :, :LANES], HALO, 1)
        )
        return unused

    lax.fori_loop(0, size, one, 0)
    links = connect[...].astype(F32)
    pad = jnp.zeros((SUB - CORNERS, LANES), F32)
    top = size * size
    up[top : top + SUB, :] = jnp.concatenate([pltpu.roll(links[:, LANES:], HALO, 1), pad], axis=0)
    down[top : top + SUB, :] = jnp.concatenate([links[:, :LANES], pad], axis=0)


def first_kernel(dims, block, below, above, stiffness, mass, connect, out, picked, high, low):
    ext = jnp.concatenate([below[...], block[...], above[...]], axis=1)
    own_products(dims, split(ext), stiffness, mass, connect, picked, high, low, out)


def edge_kernel(dims, block, below, above, part, from_below, from_above, connect, edges, edge_nodes, prod_low, prod_high, gram, picked, high, low, out):
    comps, modes = dims
    size = comps * CORNERS
    top = size * size
    first = lax.broadcasted_iota(jnp.int32, (size, LANES), 1) < HALO

    def one(i, unused):
        row = pl.multiple_of(i * size, 8)
        lower = from_below[pl.ds(row, size), :]
        upper = from_above[pl.ds(row, size), :]
        edges[0, i] = jnp.where(first, lower, pltpu.roll(upper, HALO, 1))
        edges[1, i] = jnp.where(first, pltpu.roll(lower, HALO, 1), upper)
        return unused

    lax.fori_loop(0, size, one, 0)
    count = connect.shape[1]
    before = from_below[top : top + SUB, :] + (LANES - HALO - count)
    after = pltpu.roll(from_above[top : top + SUB, :], HALO, 1) + (LANES - HALO + count)
    nodes = jnp.where(first[:SUB], before, after).astype(jnp.int32)
    edge_nodes[...] = nodes
    ext = jnp.concatenate([below[...], block[...], above[...]], axis=1)
    out[...] = part[...]
    edge_products(dims, split(ext), edges, nodes, picked, high, low, out)
    prod_low[...] = out[:, :LANES]
    prod_high[...] = out[:, LANES:]
    store_lanes(gram, grams([block[...]], out[...], dims))


def start_all(sources, targets, sems):
    copies = [pltpu.make_async_copy(a, b, sems.at[i]) for i, (a, b) in enumerate(zip(sources, targets))]
    for copy in copies:
        copy.start()
    return copies


def second_kernel(dims, gram_in, connect, edge_nodes, block, *refs):
    comps, modes = dims
    sources, refs = refs[:7], refs[7:]
    res_low, res_high, prod_low, prod_high, gram, state = refs[:6]
    ext, picked, high, low, out, *targets, sems = refs[6:]
    copies = start_all(sources, targets, sems)
    tiles, (stiffness, mass, edges) = targets[:4], targets[4:]
    reduced = gram_in[...]
    stiff_gram = symmetric(reduced[:, :modes])
    mass_gram = symmetric(reduced[:, modes : 2 * modes])
    unit = eye(modes)
    (inverse,) = eliminate(mass_gram, [unit], modes)
    (stiff_root,) = eliminate(stiff_gram, [unit], modes)
    ratio = dotf(stiff_gram, dotf(inverse, inverse, TN))
    state[0] = inverse
    state[1] = dotf(stiff_root, stiff_root, TN)
    state[2] = mass_gram
    ratio_high, ratio_low = split(ratio)
    for copy in copies[:4]:
        copy.wait()
    for c in range(comps):
        for tile, part in enumerate(tiles):
            row = c * 2 * modes
            right_high, right_low = split(part[row + modes : row + 2 * modes, :])
            moved = dot1(ratio_high, right_high, NN) + (dot1(ratio_high, right_low, NN) + dot1(ratio_low, right_high, NN))
            ext[c * modes : (c + 1) * modes, tile * LANES : (tile + 1) * LANES] = part[row : row + modes, :] - moved
    for copy in copies[4:]:
        copy.wait()
    halves = split(ext[...])
    own_products(dims, halves, stiffness, mass, connect, picked, high, low, out)
    edge_products(dims, halves, edges, edge_nodes[...], picked, high, low, out)
    prod_low[...] = out[:, :LANES]
    prod_high[...] = out[:, LANES:]
    res_low[...] = ext[:, LANES : 2 * LANES]
    res_high[...] = ext[:, 2 * LANES : 3 * LANES]
    store_lanes(gram, grams([block[...], ext[:, LANES : 3 * LANES]], out[...], dims))


def small_step(reduced, solver, mass_old, start, modes):
    rows = reduced.shape[0]
    old = rows - modes
    turned = reduced.T
    cross = reduced[:old, :modes]
    corner = symmetric(reduced[old:, :modes])
    mass_cross = reduced[:old, modes : 2 * modes]
    mass_corner = symmetric(reduced[old:, modes : 2 * modes])
    mass_turned = turned[modes : 2 * modes, :old]
    mass_all = jnp.concatenate(
        [
            jnp.concatenate([mass_old, mass_cross], axis=1),
            jnp.concatenate([mass_turned, mass_corner], axis=1),
        ],
        axis=0,
    )
    unit = eye(modes)
    carried = dotf(turned[:modes, :old], solver)
    schur = symmetric(corner - dotf(carried, cross))
    root = jnp.concatenate(eliminate(schur, [-carried, unit], modes), axis=1)
    wide = jnp.concatenate(
        [
            jnp.concatenate([solver, jnp.zeros((old, modes), F32)], axis=1),
            jnp.zeros((modes, rows), F32),
        ],
        axis=0,
    )
    solver = wide + dotf(root, root, TN)
    pushed = dotf(start, mass_all[: start.shape[1], :])
    solved = dotf(pushed, solver)
    again = dotf(solved, mass_all)
    (pushed,) = eliminate(symmetric(dotf(solved, again, NT)), [again], modes)
    solved = dotf(pushed, solver)
    again = dotf(solved, mass_all)
    normal = symmetric(dotf(solved, again, NT))
    energy = dotf(solved, pushed, NT)
    coeff, half, root = eliminate(normal, [solved, energy, unit], modes)
    return coeff, half, root, solver, mass_all


def third_kernel(dims, gram_in, state_in, connect, edge_nodes, block, *refs):
    comps, modes = dims
    sources, refs = refs[:13], refs[13:]
    new_low, new_high, gram, coeff_out, state = refs[:5]
    ext, picked, high, low, out, *targets, sems = refs[5:]
    copies = start_all(sources, targets, sems)
    coeff, half, root, solver, mass_all = small_step(gram_in[...], state_in[1], state_in[2], state_in[0], modes)
    rayleigh = symmetric(dotf(half, root, NT))
    coeff_out[...] = coeff
    state[0] = solver
    state[1] = mass_all
    bent = dotf(rayleigh, coeff)
    mixed = jnp.concatenate([coeff[:, :modes], -bent[:, :modes], coeff[:, modes:], -bent[:, modes:]], axis=1)
    mixed_high, mixed_low = split(mixed)
    for copy in copies[:8]:
        copy.wait()
    for c in range(comps):
        for tile in range(4):
            row = c * 2 * modes
            right = jnp.concatenate([part[row : row + 2 * modes, :] for part in (targets[tile], targets[4 + tile])], axis=0)
            right_high, right_low = split(right)
            ext[c * modes : (c + 1) * modes, tile * LANES : (tile + 1) * LANES] = dot1(mixed_high, right_high, NN) + (
                dot1(mixed_high, right_low, NN) + dot1(mixed_low, right_high, NN)
            )
    for copy in copies[8:]:
        copy.wait()
    stiffness, mass, edges, res_low, res_high = targets[8:]
    halves = split(ext[...])
    own_products(dims, halves, stiffness, mass, connect, picked, high, low, out)
    edge_products(dims, halves, edges, edge_nodes[...], picked, high, low, out)
    new_low[...] = ext[:, LANES : 2 * LANES]
    new_high[...] = ext[:, 2 * LANES : 3 * LANES]
    residual = jnp.concatenate([res_low[...], res_high[...]], axis=1)
    store_lanes(gram, grams([block[...], residual, ext[:, LANES : 3 * LANES]], out[...], dims))


def last_kernel(dims, gram_in, coeff_in, state_in, block, res_low, res_high, new_low, new_high, modes_out, ritz_out):
    comps, modes = dims
    coeff, half, root, solver, mass_all = small_step(gram_in[...], state_in[0], state_in[1], coeff_in[...], modes)
    ritz_out[...] = jnp.sum(dotf(half, root, NT) * eye(modes), axis=0, keepdims=True)
    coeff_high, coeff_low = split(coeff)
    for tile, parts in enumerate(((res_low, new_low), (res_high, new_high))):
        lanes = slice(tile * LANES, (tile + 1) * LANES)
        for c in range(comps):
            rows = slice(c * modes, (c + 1) * modes)
            right = jnp.concatenate([block[rows, lanes]] + [part[rows, :] for part in parts], axis=0)
            right_high, right_low = split(right)
            modes_out[rows, lanes] = dot1(coeff_high, right_high, NN) + (
                dot1(coeff_high, right_low, NN) + dot1(coeff_low, right_high, NN)
            )


def total_over(value, axis):
    count = lax.axis_size(axis)
    if count & (count - 1):
        return lax.psum(value, axis)

    def from_partner(part, bits):
        return lax.ppermute(part, axis, [(i, i ^ bits) for i in range(count)])

    stride = 1
    while stride < count:
        if 4 * stride <= count:
            one, two, three = (from_partner(value, k * stride) for k in (1, 2, 3))
            value = (value + one) + (two + three)
            stride *= 4
        else:
            value = value + from_partner(value, stride)
            stride *= 2
    return value


def from_neighbours(upward, downward, axis):
    count = lax.axis_size(axis)
    below = lax.ppermute(upward, axis, [(i, i + 1) for i in range(count - 1)])
    above = lax.ppermute(downward, axis, [(i + 1, i) for i in range(count - 1)])
    return below, above


VMEM = pl.BlockSpec(memory_space=pltpu.VMEM)
ANY = pl.BlockSpec(memory_space=pl.ANY)


def call(kernel, dims, name, outs, scratch, operands, remote=()):
    shapes = tuple(jax.ShapeDtypeStruct(shape, dtype) for shape, dtype in outs)
    if remote:
        scratch = scratch + [pltpu.VMEM(x.shape, x.dtype) for x in remote] + [pltpu.SemaphoreType.DMA((len(remote),))]
    return pl.pallas_call(
        functools.partial(kernel, dims),
        out_shape=shapes,
        in_specs=[VMEM] * len(operands) + [ANY] * len(remote),
        out_specs=tuple(VMEM for _ in shapes),
        scratch_shapes=scratch,
        name=name,
    )(*operands, *remote)


def body(modes_start, stiffness, mass, connect):
    modes, comps, count = modes_start.shape
    size = comps * CORNERS
    dims = (comps, modes)
    rows = comps * modes
    picked = pltpu.VMEM((rows, 4 * LANES), F32)
    parts = pltpu.VMEM((2 * rows, 4 * LANES), BF16)
    total = pltpu.VMEM((2 * rows, 2 * LANES), F32)
    half = ((rows, LANES), F32)
    prods = ((2 * rows, LANES), F32)
    packed = ((size * size + SUB, LANES), F32)
    block = modes_start.transpose(1, 0, 2).reshape(rows, count)

    v_below, v_above = from_neighbours(block[:, LANES:], block[:, :LANES], "sub")
    up, down = call(pack_kernel, dims, "pack", [packed, packed], [], (stiffness, mass, connect))
    below, above = from_neighbours(up, down, "sub")
    (part,) = call(
        first_kernel,
        dims,
        "first",
        [((2 * rows, 2 * LANES), F32)],
        [picked, parts, parts],
        (block, v_below, v_above, stiffness, mass, connect),
    )
    edges, edge_nodes, p_low, p_high, gram = call(
        edge_kernel,
        dims,
        "edge",
        [((2, size, size, LANES), F32), ((SUB, LANES), jnp.int32), prods, prods, ((modes, LANES), F32)],
        [picked, parts, parts, total],
        (block, v_below, v_above, part, below, above, connect),
    )
    gram = total_over(gram, "sub")
    p_below, p_above = from_neighbours(p_high, p_low, "sub")
    scratch = [picked, picked, parts, parts, total]
    res_low, res_high, q_low, q_high, gram, state = call(
        second_kernel,
        dims,
        "second",
        [half, half, prods, prods, ((2 * modes, LANES), F32), ((3, modes, modes), F32)],
        scratch,
        (gram, connect, edge_nodes, block),
        (p_below, p_low, p_high, p_above, stiffness, mass, edges),
    )
    gram = total_over(gram, "sub")
    q_below, q_above = from_neighbours(q_high, q_low, "sub")
    new_low, new_high, gram, coeff, state = call(
        third_kernel,
        dims,
        "third",
        [half, half, ((3 * modes, LANES), F32), ((modes, 2 * modes), F32), ((2, 2 * modes, 2 * modes), F32)],
        scratch,
        (gram, state, connect, edge_nodes, block),
        (p_below, p_low, p_high, p_above, q_below, q_low, q_high, q_above, stiffness, mass, edges, res_low, res_high),
    )
    gram = total_over(gram, "sub")
    result, ritz = call(
        last_kernel,
        dims,
        "last",
        [((rows, count), F32), ((1, modes), F32)],
        [],
        (gram, coeff, state, block, res_low, res_high, new_low, new_high),
    )
    return result.reshape(comps, modes, count).transpose(1, 0, 2), ritz.reshape(modes)


def solution(mesh):
    in_specs = (
        P(None, None, ("groups", "sub")),
        P(None, None, ("groups", "sub")),
        P(None, None, ("groups", "sub")),
        P(None, ("groups", "sub")),
    )
    out_specs = (P(None, None, ("groups", "sub")), P("groups"))
    return jax.shard_map(body, mesh=mesh, in_specs=in_specs, out_specs=out_specs, check_vma=False)
```

time: 164 us -> 142 us (0.87)
  Pallas kernels: 86.4 us -> 66.4 us
  starting transfers between devices: 41.7 us -> 46 us
  waiting for transfers between devices: 23.7 us -> 19.9 us
  local copies, waits for them, and re-layouts: 6.7 us -> 3.77 us
    pallas_call x5 -> x6, Pallas kernels: 86.4 us -> 66.4 us  [call(): pl.pallas_call(functools.partial(kernel, dims), out_shape=shapes, in_spec...]
    ppermute x3 -> x4, starting transfers between devices: 6.63 us -> 12.4 us  [from_neighbours(): below = lax.ppermute(upward, axis, [(i, i + 1) for i in range(count - 1)])]
    ppermute x3 -> x4, waiting for transfers between devices: 4.41 us -> 0.01 us  [from_neighbours(): above = lax.ppermute(downward, axis, [(i + 1, i) for i in range(count - 1)])]
    ppermute x18, starting transfers between devices: 31 us -> 28.3 us  [from_partner(): return lax.ppermute(part, axis, [(i, i ^ bits) for i in range(count)])]
    unnamed x16 -> x18, local copies, waits for them, and re-layouts: 6.07 us -> 3.75 us
    ppermute x3 -> x4, starting transfers between devices: 4.06 us -> 5.35 us  [from_neighbours(): above = lax.ppermute(downward, axis, [(i + 1, i) for i in range(count - 1)])]
  transfers between devices with their start and end apart: 24 -> 26, of which waited for: 9 -> 8; matrix products, arithmetic and copies ran while one was open for 2% -> 2% of each run, Pallas kernels for 0% -> 7%
where the time goes in v2:
time: 142 us; the launch traced here: 141 us
  Pallas kernels  66.4 us (47%)
  starting transfers between devices  46 us (32%)
  waiting for transfers between devices  19.9 us (14%)
  other arithmetic  4.39 us (3%)
  local copies, waits for them, and re-layouts  3.77 us (3%)
    pallas_call x6, Pallas kernels, call(): pl.pallas_call(functools.partial(kernel, dims), out_shape=shapes, in_spec...  66.4 us
    ppermute x18, starting transfers between devices, from_partner(): return lax.ppermute(part, axis, [(i, i ^ bits) for i in range(count)])  28.3 us
    ppermute x18, waiting for transfers between devices, from_partner(): return lax.ppermute(part, axis, [(i, i ^ bits) for i in range(count)])  18.9 us
    ppermute x4, starting transfers between devices, from_neighbours(): below = lax.ppermute(upward, axis, [(i, i + 1) for i in range(count - 1)])  12.4 us
    ppermute x4, starting transfers between devices, from_neighbours(): above = lax.ppermute(downward, axis, [(i + 1, i) for i in range(count - 1)])  5.35 us
    add x6, other arithmetic, total_over(): value = value + one + (two + three)  4.39 us
    unnamed x18, local copies, waits for them, and re-layouts  3.75 us
  transfers between devices with their start and end apart: 26, of which 8 were waited for; matrix products, arithmetic and copies ran while one was open for 2% of the time, Pallas kernels for 7%

profile of v2, /device:TPU:0, one launch (start us, length us, event | category | flops | bytes accessed | tf_op | source)
XLA Modules:
  0.0 141.4 jit_solution(4896101942102222998)
XLA Ops:
  0.6 0.0 copy-start
  0.6 3.9 %pack.1 = (f32[584,128]{1,0:T(8,128)}, f32[584,128]{1,0:T(8,128)}) custom-call(f32[24,24,256]{2,1,0:T(8,128)} %refs_8_.1, f32[24,24,256]{2,1,0:T(8,128)} %refs_9_.1, s32[4,256]{1,0:T(4,128)} %connect.9), custom_call_target="tpu_custom_call" | custom-call | tf_op jit(solution)/shard_map/pack/pallas_call | solution.py:426
  4.5 2.4 %collective-permute-start.2 = (f32[584,128]{1,0:T(8,128)}, f32[584,128]{1,0:T(8,128)S(1)}, u32[]{:S(2)}, u32[]{:S(2)}) collective-permute-start(f32[584,128]{1,0:T(8,128)} %get-tuple-element.22), channel_id=1, source_target_pairs={{0,1},{1,2},{2,3},{3,4},{4,5},{5,6},{6,7},{7,8},{8,9},{9,10},{10,1... | collective-permute-start | bytes 897032 | tf_op jit(solution)/shard_map/ppermute | solution.py:413
  6.9 1.3 collective-permute-start.3
  8.3 1.3 collective-permute-start.1
  9.6 5.8 %collective-permute-start = (f32[288,128]{1,0:T(8,128)S(1)}, f32[288,128]{1,0:T(8,128)S(1)}, u32[]{:S(2)}, u32[]{:S(2)}) collective-permute-start(f32[288,128]{1,0:T(8,128)S(1)} %get-tuple-element.43), channel_id=1, source_target_pairs={{0,1},{1,2},{2,3},{3,4},{4,5},{5,6},{6,7},{7,8},{8,9},{9,10},{10,1... | collective-permute-start | bytes 442376 | tf_op jit(solution)/shard_map/ppermute | solution.py:413
  15.4 0.0 collective-permute-done.1.above
  15.4 1.0 collective-permute-done.below
  16.3 0.7 copy-done.4
  17.0 9.2 %first.1.part = f32[576,256]{1,0:T(8,128)} custom-call(f32[288,256]{1,0:T(8,128)} %bitcast.7, f32[288,128]{1,0:T(8,128)} %copy-done.4, f32[288,128]{1,0:T(8,128)} %copy-done.3, f32[24,24,256]{2,1,0:T(8,128)} %refs_8_.1, f32[24,24,256]{2,1,0:T(8,128)} %refs_9_.1, s32[4,256]{1,0:T(4,128)} %connect.9), custom_call_target="tpu_custom_call" | custom-call | tf_op jit(solution)/shard_map/first/pallas_call | solution.py:426
  26.2 0.0 collective-permute-done.2.from_below
  26.2 0.0 collective-permute-done.3.from_above
  26.2 0.7 copy-done.5
  26.9 0.7 copy-done.6
  27.7 7.8 %edge.1 = (f32[2,24,24,128]{3,2,1,0:T(8,128)}, s32[8,128]{1,0:T(8,128)}, f32[576,128]{1,0:T(8,128)}, f32[576,128]{1,0:T(8,128)}, f32[48,128]{1,0:T(8,128)}) custom-call(f32[288,256]{1,0:T(8,128)} %bitcast.8, f32[288,128]{1,0:T(8,128)} %copy-done.4, f32[288,128]{1,0:T(8,128)} %copy-done.3, f32[576,256]{1,0:T(8,128)} %first.1.part, f32[584,128]{1,0:T(8,128)} %copy-done.5, ...), custom_call_target="tpu_custom_call" | custom-call | tf_op jit(solution)/shard_map/edge/pallas_call | solution.py:426
  35.5 5.9 %collective-permute-start.6 = (f32[48,128]{1,0:T(8,128)}, f32[48,128]{1,0:T(8,128)S(1)}, u32[]{:S(2)}, u32[]{:S(2)}) collective-permute-start(f32[48,128]{1,0:T(8,128)} %get-tuple-element.24), channel_id=1, source_target_pairs={{0,3},{1,2},{2,1},{3,0},{4,7},{5,6},{6,5},{7,4},{8,11},{9,10},{10,... | collective-permute-start | bytes 73736 | tf_op jit(solution)/shard_map/ppermute | solution.py:397
  41.4 1.4 collective-permute-start.5
  42.8 0.1 collective-permute-start.4
  42.9 2.3 %collective-permute-start.10 = (f32[576,128]{1,0:T(8,128)}, f32[576,128]{1,0:T(8,128)S(1)}, u32[]{:S(2)}, u32[]{:S(2)}) collective-permute-start(f32[576,128]{1,0:T(8,128)} %get-tuple-element.26.refs_2_), channel_id=1, source_target_pairs={{0,1},{1,2},{2,3},{3,4},{4,5},{5,6},{6,7},{7,8},{8,9},{9,10},{10,1... | collective-permute-start | bytes 884744 | tf_op jit(solution)/shard_map/ppermute | solution.py:413
  45.2 1.3 collective-permute-start.11
  46.5 0.0 collective-permute-done.5
  46.5 0.0 collective-permute-done.4
  46.5 0.7 add_add_fusion.5
  47.3 6.4 %collective-permute-start.9 = (f32[48,128]{1,0:T(8,128)S(1)}, f32[48,128]{1,0:T(8,128)S(1)}, u32[]{:S(2)}, u32[]{:S(2)}) collective-permute-start(f32[48,128]{1,0:T(8,128)S(1)} %add_add_fusion.5), channel_id=1, source_target_pairs={{0,12},{1,13},{2,14},{3,15},{4,8},{5,9},{6,10},{7,11},{8,4},{9,5},... | collective-permute-start | bytes 73736 | tf_op jit(solution)/shard_map/ppermute | solution.py:397
  53.7 0.6 collective-permute-start.7
  54.3 4.4 %collective-permute-done.9 = f32[48,128]{1,0:T(8,128)S(1)} collective-permute-done((f32[48,128]{1,0:T(8,128)S(1)}, f32[48,128]{1,0:T(8,128)S(1)}, u32[]{:S(2)}, u32[]{:S(2)}) %collective-permute-start.9) | collective-permute-done | bytes 24608 | tf_op jit(solution)/shard_map/ppermute | solution.py:397
  58.7 0.0 collective-permute-done.7
  58.7 0.6 add_add_fusion.4.gram_in
  59.3 0.7 copy-done.1
  60.0 0.1 copy-done.2
  60.1 16.2 %second.1 = (f32[288,128]{1,0:T(8,128)}, f32[288,128]{1,0:T(8,128)}, f32[576,128]{1,0:T(8,128)}, f32[576,128]{1,0:T(8,128)}, f32[96,128]{1,0:T(8,128)}, /*index=5*/f32[3,48,48]{2,1,0:T(8,128)}) custom-call(f32[48,128]{1,0:T(8,128)} %add_add_fusion.4.gram_in, s32[4,256]{1,0:T(4,128)} %connect.9, s32[8,128]{1,0:T(8,128)} %get-tuple-element.25.edge_nodes, ...), custom_call_target="tpu_custom_call" | custom-call | tf_op jit(solution)/shard_map/second/pallas_call | solution.py:426
  76.4 0.1 collective-permute-start.14
  76.5 0.1 collective-permute-start.13
  76.5 1.8 %collective-permute-start.12 = (f32[96,128]{1,0:T(8,128)}, f32[96,128]{1,0:T(8,128)S(1)}, u32[]{:S(2)}, u32[]{:S(2)}) collective-permute-start(f32[96,128]{1,0:T(8,128)} %get-tuple-element.29), channel_id=1, source_target_pairs={{0,1},{1,0},{2,3},{3,2},{4,5},{5,4},{6,7},{7,6},{8,9},{9,8},{10,11... | collective-permute-start | bytes 147464 | tf_op jit(solution)/shard_map/ppermute | solution.py:397
  78.3 1.9 %collective-permute-start.18 = (f32[576,128]{1,0:T(8,128)}, f32[576,128]{1,0:T(8,128)S(1)}, u32[]{:S(2)}, u32[]{:S(2)}) collective-permute-start(f32[576,128]{1,0:T(8,128)} %get-tuple-element.31.refs_6_), channel_id=1, source_target_pairs={{0,1},{1,2},{2,3},{3,4},{4,5},{5,6},{6,7},{7,8},{8,9},{9,10},{10,1... | collective-permute-start | bytes 884744 | tf_op jit(solution)/shard_map/ppermute | solution.py:413
  80.2 1.5 %collective-permute-start.19 = (f32[576,128]{1,0:T(8,128)}, f32[576,128]{1,0:T(8,128)S(1)}, u32[]{:S(2)}, u32[]{:S(2)}) collective-permute-start(f32[576,128]{1,0:T(8,128)} %get-tuple-element.32.refs_5_), channel_id=1, source_target_pairs={{1,0},{2,1},{3,2},{4,3},{5,4},{6,5},{7,6},{8,7},{9,8},{10,9},{11,1... | collective-permute-start | bytes 884744 | tf_op jit(solution)/shard_map/ppermute | solution.py:414
  81.7 0.0 collective-permute-done.13
  81.7 0.0 collective-permute-done.12
  81.7 0.8 add_add_fusion.3
  82.6 4.5 %collective-permute-start.17 = (f32[96,128]{1,0:T(8,128)S(1)}, f32[96,128]{1,0:T(8,128)S(1)}, u32[]{:S(2)}, u32[]{:S(2)}) collective-permute-start(f32[96,128]{1,0:T(8,128)S(1)} %add_add_fusion.3), channel_id=1, source_target_pairs={{0,12},{1,13},{2,14},{3,15},{4,8},{5,9},{6,10},{7,11},{8,4},{9,5},... | collective-permute-start | bytes 147464 | tf_op jit(solution)/shard_map/ppermute | solution.py:397
  87.1 1.1 collective-permute-start.16
  88.2 0.0 collective-permute-start.15
  88.2 4.9 %collective-permute-done.17 = f32[96,128]{1,0:T(8,128)S(1)} collective-permute-done((f32[96,128]{1,0:T(8,128)S(1)}, f32[96,128]{1,0:T(8,128)S(1)}, u32[]{:S(2)}, u32[]{:S(2)}) %collective-permute-start.17) | collective-permute-done | bytes 49184 | tf_op jit(solution)/shard_map/ppermute | solution.py:397
  93.1 2.0 %collective-permute-done.16 = f32[96,128]{1,0:T(8,128)S(1)} collective-permute-done((f32[96,128]{1,0:T(8,128)S(1)}, f32[96,128]{1,0:T(8,128)S(1)}, u32[]{:S(2)}, u32[]{:S(2)}) %collective-permute-start.16) | collective-permute-done | bytes 49184 | tf_op jit(solution)/shard_map/ppermute | solution.py:397
  95.0 0.0 collective-permute-done.15
  95.0 0.6 add_add_fusion.2.gram_in
  95.7 0.7 copy-done.7
  96.4 0.1 copy-done.8
  96.5 20.7 %third.1 = (f32[288,128]{1,0:T(8,128)}, f32[288,128]{1,0:T(8,128)}, f32[144,128]{1,0:T(8,128)}, f32[48,96]{1,0:T(8,128)}, f32[2,96,96]{2,1,0:T(8,128)}) custom-call(f32[96,128]{1,0:T(8,128)} %add_add_fusion.2.gram_in, f32[3,48,48]{2,1,0:T(8,128)} %get-tuple-element.30.state_in, s32[4,256]{1,0:T(4,128)} %connect.9, s32[8,128]{1,0:T(8,128)} %get-tuple-element.25.edge_nodes, ...), custom_call_target="tpu_custom_call" | custom-call | tf_op jit(solution)/shard_map/third/pallas_call | solution.py:426
  117.2 0.1 collective-permute-start.22
  117.2 0.1 collective-permute-start.21
  117.3 1.8 %collective-permute-start.20 = (f32[144,128]{1,0:T(8,128)}, f32[144,128]{1,0:T(8,128)S(1)}, u32[]{:S(2)}, u32[]{:S(2)}) collective-permute-start(f32[144,128]{1,0:T(8,128)} %get-tuple-element.35), channel_id=1, source_target_pairs={{0,1},{1,0},{2,3},{3,2},{4,5},{5,4},{6,7},{7,6},{8,9},{9,8},{10,11... | collective-permute-start | bytes 221192 | tf_op jit(solution)/shard_map/ppermute | solution.py:397
  119.1 2.3 %collective-permute-done.22 = f32[144,128]{1,0:T(8,128)S(1)} collective-permute-done((f32[144,128]{1,0:T(8,128)}, f32[144,128]{1,0:T(8,128)S(1)}, u32[]{:S(2)}, u32[]{:S(2)}) %collective-permute-start.22) | collective-permute-done | bytes 73760 | tf_op jit(solution)/shard_map/ppermute | solution.py:397
  121.4 1.3 collective-permute-done.21
  122.7 0.0 collective-permute-done.20
  122.7 0.9 add_add_fusion.1
  123.6 0.1 collective-permute-start.25
  123.7 1.5 %collective-permute-start.24 = (f32[144,128]{1,0:T(8,128)S(1)}, f32[144,128]{1,0:T(8,128)S(1)}, u32[]{:S(2)}, u32[]{:S(2)}) collective-permute-start(f32[144,128]{1,0:T(8,128)S(1)} %add_add_fusion.1), channel_id=1, source_target_pairs={{0,8},{1,9},{2,10},{3,11},{4,12},{5,13},{6,14},{7,15},{8,0},{9,1},... | collective-permute-start | bytes 221192 | tf_op jit(solution)/shard_map/ppermute | solution.py:397
  125.1 2.9 %collective-permute-start.23 = (f32[144,128]{1,0:T(8,128)S(1)}, f32[144,128]{1,0:T(8,128)S(1)}, u32[]{:S(2)}, u32[]{:S(2)}) collective-permute-start(f32[144,128]{1,0:T(8,128)S(1)} %add_add_fusion.1), channel_id=1, source_target_pairs={{0,4},{1,5},{2,6},{3,7},{4,0},{5,1},{6,2},{7,3},{8,12},{9,13},{10,... | collective-permute-start | bytes 221192 | tf_op jit(solution)/shard_map/ppermute | solution.py:397
  128.0 2.6 %collective-permute-done.25 = f32[144,128]{1,0:T(8,128)S(1)} collective-permute-done((f32[144,128]{1,0:T(8,128)S(1)}, f32[144,128]{1,0:T(8,128)S(1)}, u32[]{:S(2)}, u32[]{:S(2)}) %collective-permute-start.25) | collective-permute-done | bytes 73760 | tf_op jit(solution)/shard_map/ppermute | solution.py:397
  130.6 1.6 %collective-permute-done.24 = f32[144,128]{1,0:T(8,128)S(1)} collective-permute-done((f32[144,128]{1,0:T(8,128)S(1)}, f32[144,128]{1,0:T(8,128)S(1)}, u32[]{:S(2)}, u32[]{:S(2)}) %collective-permute-start.24) | collective-permute-done | bytes 73760 | tf_op jit(solution)/shard_map/ppermute | solution.py:397
  132.2 0.0 collective-permute-done.23
  132.2 0.7 add_add_fusion.gram_in
  132.8 8.6 %last.1 = (f32[288,256]{1,0:T(8,128)}, f32[1,48]{1,0:T(1,128)}) custom-call(f32[144,128]{1,0:T(8,128)} %add_add_fusion.gram_in, f32[48,96]{1,0:T(8,128)} %get-tuple-element.36.coeff_in, f32[2,96,96]{2,1,0:T(8,128)} %get-tuple-element.37.state_in, f32[288,256]{1,0:T(8,128)} %bitcast.11, f32[288,128]{1,0:T(8,128)} %get-tuple-element.33.refs_11_.res_low, ...), custom_call_target="tpu_custom_call" | custom-call | tf_op jit(solution)/shard_map/last/pallas_call | solution.py:426
  (19 shorter events, 0.1 us)
Async XLA Ops:
  0.6 7.6 %copy-start = (f32[48,6,256]{2,0,1:T(8,128)S(1)}, f32[48,6,256]{2,0,1:T(8,128)}, u32[]{:S(2)}) copy-start(f32[48,6,256]{2,0,1:T(8,128)} %param.4) | copy-start | bytes 884740
  4.5 21.7 %collective-permute-start.2 = (f32[584,128]{1,0:T(8,128)}, f32[584,128]{1,0:T(8,128)S(1)}, u32[]{:S(2)}, u32[]{:S(2)}) collective-permute-start(f32[584,128]{1,0:T(8,128)} %get-tuple-element.22), channel_id=1, source_target_pairs={{0,1},{1,2},{2,3},{3,4},{4,5},{5,6},{6,7},{7,8},{8,9},{9,10},{10,1... | collective-permute-start | bytes 897032 | tf_op jit(solution)/shard_map/ppermute | solution.py:413
  6.9 19.3 %collective-permute-start.3 = (f32[584,128]{1,0:T(8,128)}, f32[584,128]{1,0:T(8,128)S(1)}, u32[]{:S(2)}, u32[]{:S(2)}) collective-permute-start(f32[584,128]{1,0:T(8,128)} %get-tuple-element.23), channel_id=1, source_target_pairs={{1,0},{2,1},{3,2},{4,3},{5,4},{6,5},{7,6},{8,7},{9,8},{10,9},{11,1... | collective-permute-start | bytes 897032 | tf_op jit(solution)/shard_map/ppermute | solution.py:414
  8.3 7.1 %collective-permute-start.1 = (f32[288,128]{1,0:T(8,128)S(1)}, f32[288,128]{1,0:T(8,128)S(1)}, u32[]{:S(2)}, u32[]{:S(2)}) collective-permute-start(f32[288,128]{1,0:T(8,128)S(1)} %get-tuple-element.42), channel_id=1, source_target_pairs={{1,0},{2,1},{3,2},{4,3},{5,4},{6,5},{7,6},{8,7},{9,8},{10,9},{11,1... | collective-permute-start | bytes 442376 | tf_op jit(solution)/shard_map/ppermute | solution.py:414
  9.6 6.8 %collective-permute-start = (f32[288,128]{1,0:T(8,128)S(1)}, f32[288,128]{1,0:T(8,128)S(1)}, u32[]{:S(2)}, u32[]{:S(2)}) collective-permute-start(f32[288,128]{1,0:T(8,128)S(1)} %get-tuple-element.43), channel_id=1, source_target_pairs={{0,1},{1,2},{2,3},{3,4},{4,5},{5,6},{6,7},{7,8},{8,9},{9,10},{10,1... | collective-permute-start | bytes 442376 | tf_op jit(solution)/shard_map/ppermute | solution.py:413
  15.4 1.0 copy-start.3
  16.3 0.7 copy-start.4
  26.2 0.7 copy-start.5
  26.9 0.7 copy-start.6
  35.5 11.0 %collective-permute-start.6 = (f32[48,128]{1,0:T(8,128)}, f32[48,128]{1,0:T(8,128)S(1)}, u32[]{:S(2)}, u32[]{:S(2)}) collective-permute-start(f32[48,128]{1,0:T(8,128)} %get-tuple-element.24), channel_id=1, source_target_pairs={{0,3},{1,2},{2,1},{3,0},{4,7},{5,6},{6,5},{7,4},{8,11},{9,10},{10,... | collective-permute-start | bytes 73736 | tf_op jit(solution)/shard_map/ppermute | solution.py:397
  41.4 5.1 %collective-permute-start.5 = (f32[48,128]{1,0:T(8,128)}, f32[48,128]{1,0:T(8,128)S(1)}, u32[]{:S(2)}, u32[]{:S(2)}) collective-permute-start(f32[48,128]{1,0:T(8,128)} %get-tuple-element.24), channel_id=1, source_target_pairs={{0,2},{1,3},{2,0},{3,1},{4,6},{5,7},{6,4},{7,5},{8,10},{9,11},{10,... | collective-permute-start | bytes 73736 | tf_op jit(solution)/shard_map/ppermute | solution.py:397
  42.8 3.8 %collective-permute-start.4 = (f32[48,128]{1,0:T(8,128)}, f32[48,128]{1,0:T(8,128)S(1)}, u32[]{:S(2)}, u32[]{:S(2)}) collective-permute-start(f32[48,128]{1,0:T(8,128)} %get-tuple-element.24), channel_id=1, source_target_pairs={{0,1},{1,0},{2,3},{3,2},{4,5},{5,4},{6,7},{7,6},{8,9},{9,8},{10,11... | collective-permute-start | bytes 73736 | tf_op jit(solution)/shard_map/ppermute | solution.py:397
  42.9 16.4 %collective-permute-start.10 = (f32[576,128]{1,0:T(8,128)}, f32[576,128]{1,0:T(8,128)S(1)}, u32[]{:S(2)}, u32[]{:S(2)}) collective-permute-start(f32[576,128]{1,0:T(8,128)} %get-tuple-element.26.refs_2_), channel_id=1, source_target_pairs={{0,1},{1,2},{2,3},{3,4},{4,5},{5,6},{6,7},{7,8},{8,9},{9,10},{10,1... | collective-permute-start | bytes 884744 | tf_op jit(solution)/shard_map/ppermute | solution.py:413
  45.2 14.1 %collective-permute-start.11 = (f32[576,128]{1,0:T(8,128)}, f32[576,128]{1,0:T(8,128)S(1)}, u32[]{:S(2)}, u32[]{:S(2)}) collective-permute-start(f32[576,128]{1,0:T(8,128)} %get-tuple-element.27.refs_1_), channel_id=1, source_target_pairs={{1,0},{2,1},{3,2},{4,3},{5,4},{6,5},{7,6},{8,7},{9,8},{10,9},{11,1... | collective-permute-start | bytes 884744 | tf_op jit(solution)/shard_map/ppermute | solution.py:414
  47.3 11.4 %collective-permute-start.9 = (f32[48,128]{1,0:T(8,128)S(1)}, f32[48,128]{1,0:T(8,128)S(1)}, u32[]{:S(2)}, u32[]{:S(2)}) collective-permute-start(f32[48,128]{1,0:T(8,128)S(1)} %add_add_fusion.5), channel_id=1, source_target_pairs={{0,12},{1,13},{2,14},{3,15},{4,8},{5,9},{6,10},{7,11},{8,4},{9,5},... | collective-permute-start | bytes 73736 | tf_op jit(solution)/shard_map/ppermute | solution.py:397
  53.7 5.0 %collective-permute-start.8 = (f32[48,128]{1,0:T(8,128)S(1)}, f32[48,128]{1,0:T(8,128)S(1)}, u32[]{:S(2)}, u32[]{:S(2)}) collective-permute-start(f32[48,128]{1,0:T(8,128)S(1)} %add_add_fusion.5), channel_id=1, source_target_pairs={{0,8},{1,9},{2,10},{3,11},{4,12},{5,13},{6,14},{7,15},{8,0},{9,1},... | collective-permute-start | bytes 73736 | tf_op jit(solution)/shard_map/ppermute | solution.py:397
  53.7 5.0 %collective-permute-start.7 = (f32[48,128]{1,0:T(8,128)S(1)}, f32[48,128]{1,0:T(8,128)S(1)}, u32[]{:S(2)}, u32[]{:S(2)}) collective-permute-start(f32[48,128]{1,0:T(8,128)S(1)} %add_add_fusion.5), channel_id=1, source_target_pairs={{0,4},{1,5},{2,6},{3,7},{4,0},{5,1},{6,2},{7,3},{8,12},{9,13},{10,... | collective-permute-start | bytes 73736 | tf_op jit(solution)/shard_map/ppermute | solution.py:397
  59.3 0.7 copy-start.1
  59.3 0.8 copy-start.2
  76.4 5.3 %collective-permute-start.14 = (f32[96,128]{1,0:T(8,128)}, f32[96,128]{1,0:T(8,128)S(1)}, u32[]{:S(2)}, u32[]{:S(2)}) collective-permute-start(f32[96,128]{1,0:T(8,128)} %get-tuple-element.29), channel_id=1, source_target_pairs={{0,3},{1,2},{2,1},{3,0},{4,7},{5,6},{6,5},{7,4},{8,11},{9,10},{10,... | collective-permute-start | bytes 147464 | tf_op jit(solution)/shard_map/ppermute | solution.py:397
  76.5 5.3 %collective-permute-start.13 = (f32[96,128]{1,0:T(8,128)}, f32[96,128]{1,0:T(8,128)S(1)}, u32[]{:S(2)}, u32[]{:S(2)}) collective-permute-start(f32[96,128]{1,0:T(8,128)} %get-tuple-element.29), channel_id=1, source_target_pairs={{0,2},{1,3},{2,0},{3,1},{4,6},{5,7},{6,4},{7,5},{8,10},{9,11},{10,... | collective-permute-start | bytes 147464 | tf_op jit(solution)/shard_map/ppermute | solution.py:397
  76.5 5.2 %collective-permute-start.12 = (f32[96,128]{1,0:T(8,128)}, f32[96,128]{1,0:T(8,128)S(1)}, u32[]{:S(2)}, u32[]{:S(2)}) collective-permute-start(f32[96,128]{1,0:T(8,128)} %get-tuple-element.29), channel_id=1, source_target_pairs={{0,1},{1,0},{2,3},{3,2},{4,5},{5,4},{6,7},{7,6},{8,9},{9,8},{10,11... | collective-permute-start | bytes 147464 | tf_op jit(solution)/shard_map/ppermute | solution.py:397
  78.3 17.4 %collective-permute-start.18 = (f32[576,128]{1,0:T(8,128)}, f32[576,128]{1,0:T(8,128)S(1)}, u32[]{:S(2)}, u32[]{:S(2)}) collective-permute-start(f32[576,128]{1,0:T(8,128)} %get-tuple-element.31.refs_6_), channel_id=1, source_target_pairs={{0,1},{1,2},{2,3},{3,4},{4,5},{5,6},{6,7},{7,8},{8,9},{9,10},{10,1... | collective-permute-start | bytes 884744 | tf_op jit(solution)/shard_map/ppermute | solution.py:413
  80.2 15.4 %collective-permute-start.19 = (f32[576,128]{1,0:T(8,128)}, f32[576,128]{1,0:T(8,128)S(1)}, u32[]{:S(2)}, u32[]{:S(2)}) collective-permute-start(f32[576,128]{1,0:T(8,128)} %get-tuple-element.32.refs_5_), channel_id=1, source_target_pairs={{1,0},{2,1},{3,2},{4,3},{5,4},{6,5},{7,6},{8,7},{9,8},{10,9},{11,1... | collective-permute-start | bytes 884744 | tf_op jit(solution)/shard_map/ppermute | solution.py:414
  82.6 10.5 %collective-permute-start.17 = (f32[96,128]{1,0:T(8,128)S(1)}, f32[96,128]{1,0:T(8,128)S(1)}, u32[]{:S(2)}, u32[]{:S(2)}) collective-permute-start(f32[96,128]{1,0:T(8,128)S(1)} %add_add_fusion.3), channel_id=1, source_target_pairs={{0,12},{1,13},{2,14},{3,15},{4,8},{5,9},{6,10},{7,11},{8,4},{9,5},... | collective-permute-start | bytes 147464 | tf_op jit(solution)/shard_map/ppermute | solution.py:397
  87.1 8.0 %collective-permute-start.16 = (f32[96,128]{1,0:T(8,128)S(1)}, f32[96,128]{1,0:T(8,128)S(1)}, u32[]{:S(2)}, u32[]{:S(2)}) collective-permute-start(f32[96,128]{1,0:T(8,128)S(1)} %add_add_fusion.3), channel_id=1, source_target_pairs={{0,8},{1,9},{2,10},{3,11},{4,12},{5,13},{6,14},{7,15},{8,0},{9,1},... | collective-permute-start | bytes 147464 | tf_op jit(solution)/shard_map/ppermute | solution.py:397
  88.2 6.9 %collective-permute-start.15 = (f32[96,128]{1,0:T(8,128)S(1)}, f32[96,128]{1,0:T(8,128)S(1)}, u32[]{:S(2)}, u32[]{:S(2)}) collective-permute-start(f32[96,128]{1,0:T(8,128)S(1)} %add_add_fusion.3), channel_id=1, source_target_pairs={{0,4},{1,5},{2,6},{3,7},{4,0},{5,1},{6,2},{7,3},{8,12},{9,13},{10,... | collective-permute-start | bytes 147464 | tf_op jit(solution)/shard_map/ppermute | solution.py:397
  95.7 0.7 copy-start.7
  95.7 0.8 copy-start.8
  117.2 4.2 %collective-permute-start.22 = (f32[144,128]{1,0:T(8,128)}, f32[144,128]{1,0:T(8,128)S(1)}, u32[]{:S(2)}, u32[]{:S(2)}) collective-permute-start(f32[144,128]{1,0:T(8,128)} %get-tuple-element.35), channel_id=1, source_target_pairs={{0,3},{1,2},{2,1},{3,0},{4,7},{5,6},{6,5},{7,4},{8,11},{9,10},{10,... | collective-permute-start | bytes 221192 | tf_op jit(solution)/shard_map/ppermute | solution.py:397
  117.2 5.4 %collective-permute-start.21 = (f32[144,128]{1,0:T(8,128)}, f32[144,128]{1,0:T(8,128)S(1)}, u32[]{:S(2)}, u32[]{:S(2)}) collective-permute-start(f32[144,128]{1,0:T(8,128)} %get-tuple-element.35), channel_id=1, source_target_pairs={{0,2},{1,3},{2,0},{3,1},{4,6},{5,7},{6,4},{7,5},{8,10},{9,11},{10,... | collective-permute-start | bytes 221192 | tf_op jit(solution)/shard_map/ppermute | solution.py:397
  117.3 5.3 %collective-permute-start.20 = (f32[144,128]{1,0:T(8,128)}, f32[144,128]{1,0:T(8,128)S(1)}, u32[]{:S(2)}, u32[]{:S(2)}) collective-permute-start(f32[144,128]{1,0:T(8,128)} %get-tuple-element.35), channel_id=1, source_target_pairs={{0,1},{1,0},{2,3},{3,2},{4,5},{5,4},{6,7},{7,6},{8,9},{9,8},{10,11... | collective-permute-start | bytes 221192 | tf_op jit(solution)/shard_map/ppermute | solution.py:397
  123.6 7.1 %collective-permute-start.25 = (f32[144,128]{1,0:T(8,128)S(1)}, f32[144,128]{1,0:T(8,128)S(1)}, u32[]{:S(2)}, u32[]{:S(2)}) collective-permute-start(f32[144,128]{1,0:T(8,128)S(1)} %add_add_fusion.1), channel_id=1, source_target_pairs={{0,12},{1,13},{2,14},{3,15},{4,8},{5,9},{6,10},{7,11},{8,4},{9,5},... | collective-permute-start | bytes 221192 | tf_op jit(solution)/shard_map/ppermute | solution.py:397
  123.7 8.5 %collective-permute-start.24 = (f32[144,128]{1,0:T(8,128)S(1)}, f32[144,128]{1,0:T(8,128)S(1)}, u32[]{:S(2)}, u32[]{:S(2)}) collective-permute-start(f32[144,128]{1,0:T(8,128)S(1)} %add_add_fusion.1), channel_id=1, source_target_pairs={{0,8},{1,9},{2,10},{3,11},{4,12},{5,13},{6,14},{7,15},{8,0},{9,1},... | collective-permute-start | bytes 221192 | tf_op jit(solution)/shard_map/ppermute | solution.py:397
  125.1 7.1 %collective-permute-start.23 = (f32[144,128]{1,0:T(8,128)S(1)}, f32[144,128]{1,0:T(8,128)S(1)}, u32[]{:S(2)}, u32[]{:S(2)}) collective-permute-start(f32[144,128]{1,0:T(8,128)S(1)} %add_add_fusion.1), channel_id=1, source_target_pairs={{0,4},{1,5},{2,6},{3,7},{4,0},{5,1},{6,2},{7,3},{8,12},{9,13},{10,... | collective-permute-start | bytes 221192 | tf_op jit(solution)/shard_map/ppermute | solution.py:397

commit v3 on v2

v3 whole, which is shorter than its diff:
```python
import functools

import jax
import jax.numpy as jnp
from jax import lax
from jax.experimental import pallas as pl
from jax.experimental.pallas import tpu as pltpu
from jax.sharding import PartitionSpec as P

HALO = 64
LANES = 128
SUB = 8
CORNERS = 4
F32 = jnp.float32
BF16 = jnp.bfloat16

NN = (((1,), (0,)), ((), ()))
NT = (((1,), (1,)), ((), ()))
TN = (((0,), (0,)), ((), ()))


def split(value):
    high = value.astype(BF16)
    return high, (value - high.astype(F32)).astype(BF16)


def dot1(left, right, dims):
    return lax.dot_general(left, right, dims, preferred_element_type=F32)


def dot3(left, right, dims=NN):
    left_high, left_low = split(left)
    right_high, right_low = split(right)
    return dot1(left_high, right_high, dims) + (
        dot1(left_high, right_low, dims) + dot1(left_low, right_high, dims)
    )


def dotf(left, right, dims=NN):
    return lax.dot_general(
        left, right, dims, precision=lax.Precision.HIGHEST, preferred_element_type=F32
    )


def symmetric(matrix):
    return 0.5 * (matrix + matrix.T)


def whole(row):
    return jnp.broadcast_to(row,(SUB,row.shape[1]))
def eliminate(matrix, others, modes):
    tiles = modes // SUB
    chunks = []
    for other in others:
        for start in range(0, other.shape[1], LANES):
            chunks.append(other[:, start : start + LANES])
    unit = 1.0 / matrix[:1, :1]
    matrix = matrix * unit
    root = jnp.sqrt(jnp.broadcast_to(unit, (SUB, LANES)))
    left = [matrix[SUB * t : SUB * (t + 1), :] for t in range(tiles)]
    rest = [[chunk[SUB * t : SUB * (t + 1), :] for t in range(tiles)] for chunk in chunks]
    line = lax.broadcasted_iota(jnp.int32, (SUB, LANES), 0)
    outs = [[] for _ in chunks]
    for g in range(tiles):
        cols = [
            [jnp.broadcast_to(left[t][:, SUB * g + j : SUB * g + j + 1], (SUB, LANES)) for t in range(g, tiles)]
            for j in range(SUB)
        ]
        head = jnp.ones((SUB, LANES), F32)
        cross = jnp.zeros((SUB, LANES), F32)
        area = jnp.ones((SUB, LANES), F32)
        for s in range(0, SUB, 2):
            a = whole(cols[s][0][s : s + 1, :])
            b = whole(cols[s][0][s + 1 : s + 2, :])
            d = whole(cols[s + 1][0][s + 1 : s + 2, :])
            det = a * d - b * b
            inverse = 1.0 / det
            mine = (line // 2) == (s // 2)
            head = jnp.where(mine, a, head)
            cross = jnp.where(mine, b, cross)
            area = jnp.where(mine, det, area)
            p, q, r = d * inverse, b * inverse, a * inverse
            first, second = [], []
            for n, (x, y) in enumerate(zip(cols[s], cols[s + 1])):
                f0 = x * p - y * q
                f1 = y * r - x * q
                if n == 0:
                    f0 = jnp.where(line > s + 1, f0, 0.0)
                    f1 = jnp.where(line > s + 1, f1, 0.0)
                first.append(f0)
                second.append(f1)
            for j in range(s + 2, SUB):
                r0 = whole(cols[j][0][s : s + 1, :])
                r1 = whole(cols[j][0][s + 1 : s + 2, :])
                cols[j] = [c - (f0 * r0 + f1 * r1) for c, f0, f1 in zip(cols[j], first, second)]
            for group in ([left] if g + 1 < tiles else []) + rest:
                width = group[g].shape[1]
                r0 = whole(group[g][s : s + 1, :])
                r1 = whole(group[g][s + 1 : s + 2, :])
                for n, t in enumerate(range(g, tiles)):
                    if n == 0 and s + 2 == SUB:
                        continue
                    group[t] = group[t] - (first[n][:, :width] * r0 + second[n][:, :width] * r1)
        odd = (line % 2) == 1
        scale = lax.rsqrt(jnp.where(odd, area * head, head)) * root
        own = jnp.where(odd, head * scale, scale)
        mix = jnp.where(odd, cross * scale, 0.0)
        for i, group in enumerate(rest):
            width = group[g].shape[1]
            above = jnp.concatenate([group[g][SUB - 1 :, :], group[g][: SUB - 1, :]], axis=0)
            outs[i].append(own[:, :width] * group[g] - mix[:, :width] * above)
    joined = [jnp.concatenate(parts, axis=0) for parts in outs]
    results, at = [], 0
    for other in others:
        count = -(-other.shape[1] // LANES)
        part = joined[at : at + count]
        results.append(part[0] if count == 1 else jnp.concatenate(part, axis=1))
        at += count
    return results


def eye(modes):
    row = lax.broadcasted_iota(jnp.int32, (modes, modes), 0)
    col = lax.broadcasted_iota(jnp.int32, (modes, modes), 1)
    return (row == col).astype(F32)


def store_lanes(ref, value):
    rows, width = value.shape
    ref[0:rows, 0:width] = value


def chosen_nodes(nodes, base, window):
    place = lax.broadcasted_iota(jnp.int32, (window, LANES), 0) + base
    parts = [(place == nodes[a : a + 1, :]).astype(F32).astype(BF16) for a in range(nodes.shape[0])]
    return jnp.concatenate(parts, axis=1)


def pick(halves, chosen, base, picked):
    window = chosen.shape[0]
    picked[...] = dot1(halves[0][:, base : base + window], chosen, NN) + dot1(
        halves[1][:, base : base + window], chosen, NN
    )


def multiply(dims, entries, groups, picked, high, low):
    comps, modes = dims

    def one(step, unused):
        comp = step // groups
        group = step % groups
        totals = [jnp.zeros((modes, LANES), F32) for _ in range(4)]
        for j in range(comps * CORNERS):
            start = (j // CORNERS) * modes
            value = picked[start : start + modes, (j % CORNERS) * LANES : (j % CORNERS + 1) * LANES]
            for q in range(2):
                for m in range(2):
                    totals[2 * q + m] = totals[2 * q + m] + entries(comp, group, q, m, j) * value
        for q in range(2):
            for m in range(2):
                upper, lower = split(totals[2 * q + m])
                row = pl.multiple_of((comp * 2 + m) * modes, 16)
                col = pl.multiple_of((group * 2 + q) * LANES, LANES)
                high[pl.ds(row, modes), pl.ds(col, LANES)] = upper
                low[pl.ds(row, modes), pl.ds(col, LANES)] = lower
        return unused

    lax.fori_loop(0, comps * groups, one, 0)


def place_sums(high, low, target):
    return dot1(high, target, NT) + dot1(low, target, NT)


def all_products(dims, ext, stiffness, mass, edges, connect, edge_nodes, picked, high, low, out):
    comps, modes = dims
    halves = split(ext)
    own_nodes = connect[...] + (LANES - HALO)
    for number in range(2):
        lane = number * LANES
        chosen = chosen_nodes(own_nodes[:, lane : lane + LANES], lane, 3 * LANES)
        pick(halves, chosen, lane, picked)

        def entries(comp, group, q, m, j):
            matrix = mass if m else stiffness
            return matrix[comp * CORNERS + group * 2 + q, j : j + 1, lane : lane + LANES]

        multiply(dims, entries, CORNERS // 2, picked, high, low)
        total = place_sums(high[...], low[...], chosen[LANES - lane : 3 * LANES - lane, :])
        if number == 0:
            out[...] = total
        else:
            out[...] += total
    nodes = edge_nodes[...]
    pick(halves, chosen_nodes(nodes[:CORNERS], 0, 4 * LANES), 0, picked)
    multiply(dims, lambda comp, group, q, m, j: edges[m, q * comps + comp, j : j + 1, :], 1, picked, high, low)
    first = lax.broadcasted_iota(jnp.int32, (1, LANES), 1) < HALO
    reached = jnp.concatenate(
        [jnp.where(first, nodes[3:4], nodes[2:3]), jnp.where(first, nodes[1:2], -1)], axis=0
    )
    target = chosen_nodes(reached, LANES, 2 * LANES)
    out[...] += place_sums(high[:, : 2 * LANES], low[:, : 2 * LANES], target)


def grams(basis, products, dims):
    comps, modes = dims
    total = None
    for c in range(comps):
        left = jnp.concatenate([part[c * modes : (c + 1) * modes, :] for part in basis], axis=0)
        right = products[c * 2 * modes : (c + 1) * 2 * modes, :]
        term = dot3(left, right, NT)
        total = term if total is None else total + term
    return total


def by_side(first_case, second_case):
    odd = lax.rem(lax.axis_index("sub"), 2)
    pl.when(odd == 0)(first_case)
    pl.when(odd == 1)(second_case)


def start_all(pairs, sems, first=0):
    copies = [pltpu.make_async_copy(a, b, sems.at[first + i]) for i, (a, b) in enumerate(pairs)]
    for copy in copies:
        copy.start()
    return copies


def start_sides(from_a, from_b, below, above, sems, first):
    by_side(
        lambda: start_all([(from_b, below), (from_a, above)], sems, first) and None,
        lambda: start_all([(from_a, below), (from_b, above)], sems, first) and None,
    )
    return [pltpu.make_async_copy(a, b, sems.at[first + i]) for i, (a, b) in enumerate([(from_a, below), (from_b, above)])]


def pack_kernel(dims, block, connect, stiffness, mass, side_a, side_b, high_stiff, high_mass, low_stiff, low_mass, sems):
    comps, modes = dims
    size = comps * CORNERS
    upper, lower = pl.ds(LANES, LANES), pl.ds(0, LANES)
    copies = start_all(
        [
            (stiffness.at[:, 3, :, upper], high_stiff.at[0]),
            (stiffness.at[:, 1, :, upper], high_stiff.at[1]),
            (mass.at[:, 3, :, upper], high_mass.at[0]),
            (mass.at[:, 1, :, upper], high_mass.at[1]),
            (stiffness.at[:, 2, :, lower], low_stiff),
            (mass.at[:, 2, :, lower], low_mass),
        ],
        sems,
    )
    links = connect[...].astype(F32)
    pad = jnp.zeros((SUB - CORNERS, LANES), F32)
    rows = comps * size
    first = lax.broadcasted_iota(jnp.int32, (rows, LANES), 1) < HALO
    top = 2 * rows
    for copy in copies:
        copy.wait()

    def fill(up, down):
        for slot in range(2):
            up[slot * rows : (slot + 1) * rows, :] = jnp.where(
                first, pltpu.roll(high_stiff[slot].reshape(rows, LANES), HALO, 1), high_mass[slot].reshape(rows, LANES)
            )
        down[:rows, :] = jnp.where(
            first, low_stiff[...].reshape(rows, LANES), pltpu.roll(low_mass[...].reshape(rows, LANES), HALO, 1)
        )
        down[rows:top, :] = jnp.zeros((rows, LANES), F32)
        up[top : top + SUB, :] = jnp.concatenate([pltpu.roll(links[:, LANES:], HALO, 1), pad], axis=0)
        down[top : top + SUB, :] = jnp.concatenate([links[:, :LANES], pad], axis=0)
        up[top + SUB :, :] = block[:, LANES:]
        down[top + SUB :, :] = block[:, :LANES]

    by_side(lambda: fill(side_a, side_b), lambda: fill(side_b, side_a))


def store_sides(out, side_a, side_b):
    def put(low, high):
        low[...] = out[:, :LANES]
        high[...] = out[:, LANES:]

    by_side(lambda: put(side_b, side_a), lambda: put(side_a, side_b))


def first_kernel(dims, block, connect, from_a, from_b, stiff_in, mass_in, edges, edge_nodes, side_a, side_b, gram, picked, high, low, out, below, above, stiffness, mass, sems):
    comps, modes = dims
    size = comps * CORNERS
    rows = comps * size
    top = 2 * rows
    sides = start_sides(from_a, from_b, below, above, sems, 0)
    copies = start_all([(stiff_in, stiffness), (mass_in, mass)], sems, 2)
    first = lax.broadcasted_iota(jnp.int32, (rows, LANES), 1) < HALO
    for copy in sides:
        copy.wait()
    for slot in range(2):
        lower = below[slot * rows : (slot + 1) * rows, :]
        upper = above[slot * rows : (slot + 1) * rows, :]
        rest = jnp.zeros((rows, LANES), F32)
        here = slice(slot * comps, (slot + 1) * comps)
        edges[0, here] = jnp.where(first, lower, rest if slot else pltpu.roll(upper, HALO, 1)).reshape(comps, size, LANES)
        edges[1, here] = jnp.where(first, pltpu.roll(lower, HALO, 1), rest if slot else upper).reshape(comps, size, LANES)
    count = connect.shape[1]
    before = below[top : top + SUB, :] + (LANES - HALO - count)
    after = pltpu.roll(above[top : top + SUB, :], HALO, 1) + (LANES - HALO + count)
    edge_nodes[...] = jnp.where(first[:SUB], before, after).astype(jnp.int32)
    ext = jnp.concatenate([below[top + SUB :, :], block[...], above[top + SUB :, :]], axis=1)
    for copy in copies:
        copy.wait()
    all_products(dims, ext, stiffness, mass, edges, connect, edge_nodes, picked, high, low, out)
    store_sides(out, side_a, side_b)
    store_lanes(gram, grams([block[...]], out[...], dims))


def second_kernel(dims, gram_in, connect, edge_nodes, block, from_a, from_b, own_a, own_b, stiff_in, mass_in, edges_in, residual, side_a, side_b, gram, state, picked, high, low, out, below, above, lower, upper, stiffness, mass, edges, sems):
    comps, modes = dims
    tiles = (below, lower, upper, above)
    copies = start_sides(from_a, from_b, below, above, sems, 0)
    copies += start_sides(own_a, own_b, lower, upper, sems, 2)
    others = start_all([(stiff_in, stiffness), (mass_in, mass), (edges_in, edges)], sems, 4)
    reduced = gram_in[...]
    stiff_gram = symmetric(reduced[:, :modes])
    mass_gram = symmetric(reduced[:, modes : 2 * modes])
    unit = eye(modes)
    (inverse,) = eliminate(mass_gram, [unit], modes)
    (stiff_root,) = eliminate(stiff_gram, [unit], modes)
    ratio = dotf(stiff_gram, dotf(inverse, inverse, TN))
    state[0] = inverse
    state[1] = dotf(stiff_root, stiff_root, TN)
    state[2] = mass_gram
    ratio_high, ratio_low = split(ratio)
    for copy in copies:
        copy.wait()
    pieces = []
    for c in range(comps):
        row = c * 2 * modes
        left = jnp.concatenate([part[row : row + modes, :] for part in tiles], axis=1)
        right_high, right_low = split(jnp.concatenate([part[row + modes : row + 2 * modes, :] for part in tiles], axis=1))
        pieces.append(
            left - (dot1(ratio_high, right_high, NN) + (dot1(ratio_high, right_low, NN) + dot1(ratio_low, right_high, NN)))
        )
    ext = jnp.concatenate(pieces, axis=0)
    for copy in others:
        copy.wait()
    residual[...] = ext[:, LANES : 3 * LANES]
    all_products(dims, ext, stiffness, mass, edges, connect, edge_nodes, picked, high, low, out)
    store_sides(out, side_a, side_b)
    store_lanes(gram, grams([block[...], residual[...]], out[...], dims))


def small_step(reduced, solver, mass_old, start, modes):
    rows = reduced.shape[0]
    old = rows - modes
    turned = reduced.T
    cross = reduced[:old, :modes]
    corner = symmetric(reduced[old:, :modes])
    mass_cross = reduced[:old, modes : 2 * modes]
    mass_corner = symmetric(reduced[old:, modes : 2 * modes])
    mass_turned = turned[modes : 2 * modes, :old]
    mass_all = jnp.concatenate(
        [
            jnp.concatenate([mass_old, mass_cross], axis=1),
            jnp.concatenate([mass_turned, mass_corner], axis=1),
        ],
        axis=0,
    )
    unit = eye(modes)
    carried = dotf(turned[:modes, :old], solver)
    schur = symmetric(corner - dotf(carried, cross))
    root = jnp.concatenate(eliminate(schur, [-carried, unit], modes), axis=1)
    wide = jnp.concatenate(
        [
            jnp.concatenate([solver, jnp.zeros((old, modes), F32)], axis=1),
            jnp.zeros((modes, rows), F32),
        ],
        axis=0,
    )
    solver = wide + dotf(root, root, TN)
    pushed = dotf(start, mass_all[: start.shape[1], :])
    solved = dotf(pushed, solver)
    again = dotf(solved, mass_all)
    (pushed,) = eliminate(symmetric(dotf(solved, again, NT)), [again], modes)
    solved = dotf(pushed, solver)
    again = dotf(solved, mass_all)
    normal = symmetric(dotf(solved, again, NT))
    energy = dotf(solved, pushed, NT)
    coeff, half, root = eliminate(normal, [solved, energy, unit], modes)
    return coeff, half, root, solver, mass_all


def third_kernel(dims, gram_in, state_in, connect, edge_nodes, block, residual, from_a, from_b, own_a, own_b, more_a, more_b, new_a, new_b, stiff_in, mass_in, edges_in, new, gram, coeff_out, state, picked, high, low, out, below, above, lower, upper, new_below, new_above, new_lower, new_upper, stiffness, mass, edges, sems):
    comps, modes = dims
    tiles = ((below, new_below), (lower, new_lower), (upper, new_upper), (above, new_above))
    copies = start_sides(from_a, from_b, below, above, sems, 0)
    copies += start_sides(own_a, own_b, lower, upper, sems, 2)
    copies += start_sides(more_a, more_b, new_below, new_above, sems, 4)
    copies += start_sides(new_a, new_b, new_lower, new_upper, sems, 6)
    others = start_all([(stiff_in, stiffness), (mass_in, mass), (edges_in, edges)], sems, 8)
    coeff, half, root, solver, mass_all = small_step(gram_in[...], state_in[1], state_in[2], state_in[0], modes)
    rayleigh = symmetric(dotf(half, root, NT))
    coeff_out[...] = coeff
    state[0] = solver
    state[1] = mass_all
    bent = dotf(rayleigh, coeff)
    mixed = jnp.concatenate([coeff[:, :modes], -bent[:, :modes], coeff[:, modes:], -bent[:, modes:]], axis=1)
    mixed_high, mixed_low = split(mixed)
    for copy in copies:
        copy.wait()
    pieces = []
    for c in range(comps):
        rows = slice(c * 2 * modes, (c + 1) * 2 * modes)
        right = jnp.concatenate(
            [jnp.concatenate([part[rows, :] for part in parts], axis=0) for parts in tiles], axis=1
        )
        right_high, right_low = split(right)
        pieces.append(dot1(mixed_high, right_high, NN) + (dot1(mixed_high, right_low, NN) + dot1(mixed_low, right_high, NN)))
    ext = jnp.concatenate(pieces, axis=0)
    for copy in others:
        copy.wait()
    new[...] = ext[:, LANES : 3 * LANES]
    all_products(dims, ext, stiffness, mass, edges, connect, edge_nodes, picked, high, low, out)
    store_lanes(gram, grams([block[...], residual[...], new[...]], out[...], dims))


def last_kernel(dims, gram_in, coeff_in, state_in, block, residual, new, modes_out, ritz_out):
    comps, modes = dims
    coeff, half, root, solver, mass_all = small_step(gram_in[...], state_in[0], state_in[1], coeff_in[...], modes)
    ritz_out[...] = jnp.sum(dotf(half, root, NT) * eye(modes), axis=0, keepdims=True)
    coeff_high, coeff_low = split(coeff)
    for c in range(comps):
        rows = slice(c * modes, (c + 1) * modes)
        right_high, right_low = split(jnp.concatenate([part[rows, :] for part in (block, residual, new)], axis=0))
        modes_out[rows, :] = dot1(coeff_high, right_high, NN) + (
            dot1(coeff_high, right_low, NN) + dot1(coeff_low, right_high, NN)
        )


def total_over(value, axis):
    count = lax.axis_size(axis)
    if count & (count - 1):
        return lax.psum(value, axis)

    def from_partner(part, bits):
        return lax.ppermute(part, axis, [(i, i ^ bits) for i in range(count)])

    stride = 1
    while stride < count:
        if 4 * stride <= count:
            one, two, three = (from_partner(value, k * stride) for k in (1, 2, 3))
            value = (value + one) + (two + three)
            stride *= 4
        else:
            value = value + from_partner(value, stride)
            stride *= 2
    return value


def exchange(side_a, side_b, axis):
    count = lax.axis_size(axis)

    def swap(value, start):
        pairs = [(i, i + 1) for i in range(start, count - 1, 2)]
        return lax.ppermute(value, axis, pairs + [(b, a) for a, b in pairs])

    return swap(side_a, 0), swap(side_b, 1)


VMEM = pl.BlockSpec(memory_space=pltpu.VMEM)
HBM = pl.BlockSpec(memory_space=pltpu.HBM)


def call(kernel, dims, name, outs, scratch, operands, remote):
    shapes = tuple(jax.ShapeDtypeStruct(shape, dtype) for shape, dtype in outs)
    return pl.pallas_call(
        functools.partial(kernel, dims),
        out_shape=shapes,
        in_specs=[VMEM] * len(operands) + [HBM] * len(remote),
        out_specs=tuple(VMEM for _ in shapes),
        scratch_shapes=scratch,
        name=name,
    )(*operands, *remote)


def room(*arrays):
    return [pltpu.VMEM(x.shape, x.dtype) for x in arrays]


def body(modes_start, stiffness, mass, connect):
    modes, comps, count = modes_start.shape
    size = comps * CORNERS
    dims = (comps, modes)
    rows = comps * modes
    work = [
        pltpu.VMEM((rows, CORNERS * LANES), F32),
        pltpu.VMEM((2 * rows, CORNERS * LANES), BF16),
        pltpu.VMEM((2 * rows, CORNERS * LANES), BF16),
        pltpu.VMEM((2 * rows, count), F32),
    ]
    wide = ((rows, count), F32)
    side = ((2 * rows, LANES), F32)
    packed = ((2 * comps * size + SUB + rows, LANES), F32)
    edge = pltpu.VMEM((comps, size, LANES), F32)
    edges_pair = pltpu.VMEM((2, comps, size, LANES), F32)
    sems = pltpu.SemaphoreType.DMA
    block = modes_start.transpose(1, 0, 2).reshape(rows, count)

    by_corner = [x.reshape(comps, CORNERS, size, count) for x in (stiffness, mass)]
    side_a, side_b = call(
        pack_kernel,
        dims,
        "pack",
        [packed, packed],
        [edges_pair, edges_pair, edge, edge, sems((6,))],
        (block, connect),
        by_corner,
    )
    from_a, from_b = exchange(side_a, side_b, "sub")
    edges, edge_nodes, p_a, p_b, gram = call(
        first_kernel,
        dims,
        "first",
        [((2, 2 * comps, size, LANES), F32), ((SUB, LANES), jnp.int32), side, side, ((modes, LANES), F32)],
        work + room(from_a, from_b, stiffness, mass) + [sems((4,))],
        (block, connect),
        (from_a, from_b, stiffness, mass),
    )
    gram = total_over(gram, "sub")
    p_from_a, p_from_b = exchange(p_a, p_b, "sub")
    p = (p_from_a, p_from_b, p_a, p_b)
    residual, q_a, q_b, gram, state = call(
        second_kernel,
        dims,
        "second",
        [wide, side, side, ((2 * modes, LANES), F32), ((3, modes, modes), F32)],
        work + room(*p, stiffness, mass, edges) + [sems((7,))],
        (gram, connect, edge_nodes, block),
        (*p, stiffness, mass, edges),
    )
    gram = total_over(gram, "sub")
    q_from_a, q_from_b = exchange(q_a, q_b, "sub")
    q = (q_from_a, q_from_b, q_a, q_b)
    new, gram, coeff, state = call(
        third_kernel,
        dims,
        "third",
        [wide, ((3 * modes, LANES), F32), ((modes, 2 * modes), F32), ((2, 2 * modes, 2 * modes), F32)],
        work + room(*p, *q, stiffness, mass, edges) + [sems((11,))],
        (gram, state, connect, edge_nodes, block, residual),
        (*p, *q, stiffness, mass, edges),
    )
    gram = total_over(gram, "sub")
    result, ritz = call(
        last_kernel,
        dims,
        "last",
        [wide, ((1, modes), F32)],
        [],
        (gram, coeff, state, block, residual, new),
        (),
    )
    return result.reshape(comps, modes, count).transpose(1, 0, 2), ritz.reshape(modes)


def solution(mesh):
    in_specs = (
        P(None, None, ("groups", "sub")),
        P(None, None, ("groups", "sub")),
        P(None, None, ("groups", "sub")),
        P(None, ("groups", "sub")),
    )
    out_specs = (P(None, None, ("groups", "sub")), P("groups"))
    return jax.shard_map(body, mesh=mesh, in_specs=in_specs, out_specs=out_specs, check_vma=False)
```

time: 142 us -> 122 us (0.86)
  starting transfers between devices: 46 us -> 33.8 us
  Pallas kernels: 66.4 us -> 57.9 us
  waiting for transfers between devices: 19.9 us -> 21.7 us
    ppermute x8 -> x6, starting transfers between devices: 17.7 us -> 3.21 us  [swap(): return lax.ppermute(value, axis, pairs + [(b, a) for a, b in pairs])]
    pallas_call x6 -> x5, Pallas kernels: 66.4 us -> 57.9 us  [call(): pl.pallas_call(functools.partial(kernel, dims), out_shape=shapes, in_spec...]
    ppermute x18, starting transfers between devices: 28.3 us -> 30.6 us  [from_partner(): return lax.ppermute(part, axis, [(i, i ^ bits) for i in range(count)])]
    ppermute x18, waiting for transfers between devices: 18.9 us -> 21 us  [from_partner(): return lax.ppermute(part, axis, [(i, i ^ bits) for i in range(count)])]
    unnamed x18 -> x12, local copies, waits for them, and re-layouts: 3.75 us -> 3.05 us
  transfers between devices with their start and end apart: 26 -> 24, of which waited for: 8 -> 11; matrix products, arithmetic and copies ran while one was open for 2% -> 2% of each run, Pallas kernels for 7% -> 0%
where the time goes in v3:
time: 122 us
  Pallas kernels  57.9 us (47%)
  starting transfers between devices  33.8 us (28%)
  waiting for transfers between devices  21.7 us (18%)
  other arithmetic  4.37 us (4%)
  local copies, waits for them, and re-layouts  3.05 us (2%)
    pallas_call x5, Pallas kernels, call(): pl.pallas_call(functools.partial(kernel, dims), out_shape=shapes, in_spec...  57.9 us
    ppermute x18, starting transfers between devices, from_partner(): return lax.ppermute(part, axis, [(i, i ^ bits) for i in range(count)])  30.6 us
    ppermute x18, waiting for transfers between devices, from_partner(): return lax.ppermute(part, axis, [(i, i ^ bits) for i in range(count)])  21 us
    add x6, other arithmetic, total_over(): value = value + one + (two + three)  4.37 us
    ppermute x6, starting transfers between devices, swap(): return lax.ppermute(value, axis, pairs + [(b, a) for a, b in pairs])  3.21 us
    unnamed x12, local copies, waits for them, and re-layouts  3.05 us
  transfers between devices with their start and end apart: 24, of which 11 were waited for; matrix products, arithmetic and copies ran while one was open for 2% of the time, Pallas kernels for 0%

profile of v3, /device:TPU:0, one launch (start us, length us, event | category | flops | bytes accessed | tf_op | source)
XLA Modules:
  0.0 121.6 jit_solution(8261306717509641288)
XLA Ops:
  0.6 3.0 %pack.1 = (f32[584,128]{1,0:T(8,128)}, f32[584,128]{1,0:T(8,128)}) custom-call(f32[288,256]{1,0:T(8,128)} %bitcast.11, s32[4,256]{1,0:T(4,128)} %connect.7, f32[6,4,24,256]{3,2,1,0:T(8,128)} %bitcast.9, f32[6,4,24,256]{3,2,1,0:T(8,128)} %bitcast.10), custom_call_target="tpu_custom_call" | custom-call | tf_op jit(solution)/shard_map/pack/pallas_call | solution.py:473
  3.7 0.6 collective-permute-start
  4.2 0.7 collective-permute-start.1
  4.9 0.7 collective-permute-done.from_a
  5.7 0.0 collective-permute-done.1.from_b
  5.7 0.7 copy-done.2
  6.4 0.7 copy-done.3
  7.1 12.2 %first.1 = (f32[2,12,24,128]{3,2,1,0:T(8,128)}, s32[8,128]{1,0:T(8,128)}, f32[576,128]{1,0:T(8,128)}, f32[576,128]{1,0:T(8,128)}, f32[48,128]{1,0:T(8,128)}) custom-call(f32[288,256]{1,0:T(8,128)} %bitcast.12, s32[4,256]{1,0:T(4,128)} %connect.7, f32[584,128]{1,0:T(8,128)} %copy-done.2, f32[584,128]{1,0:T(8,128)} %copy-done.3, f32[24,24,256]{2,1,0:T(8,128)} %stiff_in.5, ...), custom_call_target="tpu_custom_call" | custom-call | tf_op jit(solution)/shard_map/first/pallas_call | solution.py:473
  19.3 9.9 %collective-permute-start.4 = (f32[48,128]{1,0:T(8,128)}, f32[48,128]{1,0:T(8,128)S(1)}, u32[]{:S(2)}, u32[]{:S(2)}) collective-permute-start(f32[48,128]{1,0:T(8,128)} %get-tuple-element.22), channel_id=1, source_target_pairs={{0,3},{1,2},{2,1},{3,0},{4,7},{5,6},{6,5},{7,4},{8,11},{9,10},{10,... | collective-permute-start | bytes 73736 | tf_op jit(solution)/shard_map/ppermute | solution.py:443
  29.2 2.2 %collective-permute-start.3 = (f32[48,128]{1,0:T(8,128)}, f32[48,128]{1,0:T(8,128)S(1)}, u32[]{:S(2)}, u32[]{:S(2)}) collective-permute-start(f32[48,128]{1,0:T(8,128)} %get-tuple-element.22), channel_id=1, source_target_pairs={{0,2},{1,3},{2,0},{3,1},{4,6},{5,7},{6,4},{7,5},{8,10},{9,11},{10,... | collective-permute-start | bytes 73736 | tf_op jit(solution)/shard_map/ppermute | solution.py:443
  31.3 0.0 collective-permute-start.2
  31.4 0.5 collective-permute-start.8
  31.8 0.7 collective-permute-start.9
  32.5 0.0 collective-permute-done.4
  32.5 1.0 collective-permute-done.3
  33.5 0.0 collective-permute-done.2
  33.5 0.7 add_add_fusion.5
  34.3 5.1 %collective-permute-start.7 = (f32[48,128]{1,0:T(8,128)S(1)}, f32[48,128]{1,0:T(8,128)S(1)}, u32[]{:S(2)}, u32[]{:S(2)}) collective-permute-start(f32[48,128]{1,0:T(8,128)S(1)} %add_add_fusion.5), channel_id=1, source_target_pairs={{0,12},{1,13},{2,14},{3,15},{4,8},{5,9},{6,10},{7,11},{8,4},{9,5},... | collective-permute-start | bytes 73736 | tf_op jit(solution)/shard_map/ppermute | solution.py:443
  39.4 0.0 collective-permute-start.6
  39.4 0.6 collective-permute-start.5
  40.0 4.5 %collective-permute-done.7 = f32[48,128]{1,0:T(8,128)S(1)} collective-permute-done((f32[48,128]{1,0:T(8,128)S(1)}, f32[48,128]{1,0:T(8,128)S(1)}, u32[]{:S(2)}, u32[]{:S(2)}) %collective-permute-start.7) | collective-permute-done | bytes 24608 | tf_op jit(solution)/shard_map/ppermute | solution.py:443
  44.5 0.0 collective-permute-done.6
  44.5 0.0 collective-permute-done.5
  44.5 0.6 add_add_fusion.4.gram_in
  45.1 0.0 collective-permute-done.8.from_a
  45.1 0.0 collective-permute-done.9.from_b
  45.2 0.7 copy-done
  45.8 0.1 copy-done.1
  46.0 14.9 %second.1 = (f32[288,256]{1,0:T(8,128)}, f32[576,128]{1,0:T(8,128)}, f32[576,128]{1,0:T(8,128)}, f32[96,128]{1,0:T(8,128)}, f32[3,48,48]{2,1,0:T(8,128)}) custom-call(f32[48,128]{1,0:T(8,128)} %add_add_fusion.4.gram_in, s32[4,256]{1,0:T(4,128)} %connect.7, s32[8,128]{1,0:T(8,128)} %get-tuple-element.23.edge_nodes, f32[288,256]{1,0:T(8,128)} %bitcast.13, ...), custom_call_target="tpu_custom_call" | custom-call | tf_op jit(solution)/shard_map/second/pallas_call | solution.py:473
  60.9 0.1 collective-permute-start.12
  60.9 0.6 collective-permute-start.11
  61.5 1.3 %collective-permute-start.10 = (f32[96,128]{1,0:T(8,128)}, f32[96,128]{1,0:T(8,128)S(1)}, u32[]{:S(2)}, u32[]{:S(2)}) collective-permute-start(f32[96,128]{1,0:T(8,128)} %get-tuple-element.27), channel_id=1, source_target_pairs={{0,1},{1,0},{2,3},{3,2},{4,5},{5,4},{6,7},{7,6},{8,9},{9,8},{10,11... | collective-permute-start | bytes 147464 | tf_op jit(solution)/shard_map/ppermute | solution.py:443
  62.8 0.0 collective-permute-start.16
  62.8 0.8 collective-permute-start.17
  63.7 1.0 collective-permute-done.12
  64.7 1.1 collective-permute-done.11
  65.7 0.0 collective-permute-done.10
  65.7 0.8 add_add_fusion.3
  66.5 2.8 %collective-permute-start.15 = (f32[96,128]{1,0:T(8,128)S(1)}, f32[96,128]{1,0:T(8,128)S(1)}, u32[]{:S(2)}, u32[]{:S(2)}) collective-permute-start(f32[96,128]{1,0:T(8,128)S(1)} %add_add_fusion.3), channel_id=1, source_target_pairs={{0,12},{1,13},{2,14},{3,15},{4,8},{5,9},{6,10},{7,11},{8,4},{9,5},... | collective-permute-start | bytes 147464 | tf_op jit(solution)/shard_map/ppermute | solution.py:443
  69.3 0.0 collective-permute-start.14
  69.3 1.6 %collective-permute-start.13 = (f32[96,128]{1,0:T(8,128)S(1)}, f32[96,128]{1,0:T(8,128)S(1)}, u32[]{:S(2)}, u32[]{:S(2)}) collective-permute-start(f32[96,128]{1,0:T(8,128)S(1)} %add_add_fusion.3), channel_id=1, source_target_pairs={{0,4},{1,5},{2,6},{3,7},{4,0},{5,1},{6,2},{7,3},{8,12},{9,13},{10,... | collective-permute-start | bytes 147464 | tf_op jit(solution)/shard_map/ppermute | solution.py:443
  71.0 4.4 %collective-permute-done.15 = f32[96,128]{1,0:T(8,128)S(1)} collective-permute-done((f32[96,128]{1,0:T(8,128)S(1)}, f32[96,128]{1,0:T(8,128)S(1)}, u32[]{:S(2)}, u32[]{:S(2)}) %collective-permute-start.15) | collective-permute-done | bytes 49184 | tf_op jit(solution)/shard_map/ppermute | solution.py:443
  75.4 0.6 collective-permute-done.14
  76.0 0.0 collective-permute-done.13
  76.0 0.6 add_add_fusion.2.gram_in
  76.6 0.0 collective-permute-done.16.more_a
  76.6 0.7 copy-done.4
  77.3 0.1 copy-done.5
  77.4 19.4 %third.1 = (f32[288,256]{1,0:T(8,128)}, f32[144,128]{1,0:T(8,128)}, f32[48,96]{1,0:T(8,128)}, f32[2,96,96]{2,1,0:T(8,128)}) custom-call(f32[96,128]{1,0:T(8,128)} %add_add_fusion.2.gram_in, f32[3,48,48]{2,1,0:T(8,128)} %get-tuple-element.28.state_in, s32[4,256]{1,0:T(4,128)} %connect.7, s32[8,128]{1,0:T(8,128)} %get-tuple-element.23.edge_nodes, ...), custom_call_target="tpu_custom_call" | custom-call | tf_op jit(solution)/shard_map/third/pallas_call | solution.py:473
  96.8 0.1 collective-permute-start.20
  96.9 0.1 collective-permute-start.19
  96.9 1.8 %collective-permute-start.18 = (f32[144,128]{1,0:T(8,128)}, f32[144,128]{1,0:T(8,128)S(1)}, u32[]{:S(2)}, u32[]{:S(2)}) collective-permute-start(f32[144,128]{1,0:T(8,128)} %get-tuple-element.32), channel_id=1, source_target_pairs={{0,1},{1,0},{2,3},{3,2},{4,5},{5,4},{6,7},{7,6},{8,9},{9,8},{10,11... | collective-permute-start | bytes 221192 | tf_op jit(solution)/shard_map/ppermute | solution.py:443
  98.7 2.3 %collective-permute-done.20 = f32[144,128]{1,0:T(8,128)S(1)} collective-permute-done((f32[144,128]{1,0:T(8,128)}, f32[144,128]{1,0:T(8,128)S(1)}, u32[]{:S(2)}, u32[]{:S(2)}) %collective-permute-start.20) | collective-permute-done | bytes 73760 | tf_op jit(solution)/shard_map/ppermute | solution.py:443
  101.0 1.3 %collective-permute-done.19 = f32[144,128]{1,0:T(8,128)S(1)} collective-permute-done((f32[144,128]{1,0:T(8,128)}, f32[144,128]{1,0:T(8,128)S(1)}, u32[]{:S(2)}, u32[]{:S(2)}) %collective-permute-start.19) | collective-permute-done | bytes 73760 | tf_op jit(solution)/shard_map/ppermute | solution.py:443
  102.3 0.0 collective-permute-done.18
  102.3 0.9 add_add_fusion.1
  103.2 2.0 %collective-permute-start.23 = (f32[144,128]{1,0:T(8,128)S(1)}, f32[144,128]{1,0:T(8,128)S(1)}, u32[]{:S(2)}, u32[]{:S(2)}) collective-permute-start(f32[144,128]{1,0:T(8,128)S(1)} %add_add_fusion.1), channel_id=1, source_target_pairs={{0,12},{1,13},{2,14},{3,15},{4,8},{5,9},{6,10},{7,11},{8,4},{9,5},... | collective-permute-start | bytes 221192 | tf_op jit(solution)/shard_map/ppermute | solution.py:443
  105.2 0.0 collective-permute-start.22
  105.2 2.4 %collective-permute-start.21 = (f32[144,128]{1,0:T(8,128)S(1)}, f32[144,128]{1,0:T(8,128)S(1)}, u32[]{:S(2)}, u32[]{:S(2)}) collective-permute-start(f32[144,128]{1,0:T(8,128)S(1)} %add_add_fusion.1), channel_id=1, source_target_pairs={{0,4},{1,5},{2,6},{3,7},{4,0},{5,1},{6,2},{7,3},{8,12},{9,13},{10,... | collective-permute-start | bytes 221192 | tf_op jit(solution)/shard_map/ppermute | solution.py:443
  107.6 2.6 %collective-permute-done.23 = f32[144,128]{1,0:T(8,128)S(1)} collective-permute-done((f32[144,128]{1,0:T(8,128)S(1)}, f32[144,128]{1,0:T(8,128)S(1)}, u32[]{:S(2)}, u32[]{:S(2)}) %collective-permute-start.23) | collective-permute-done | bytes 73760 | tf_op jit(solution)/shard_map/ppermute | solution.py:443
  110.2 2.3 %collective-permute-done.22 = f32[144,128]{1,0:T(8,128)S(1)} collective-permute-done((f32[144,128]{1,0:T(8,128)S(1)}, f32[144,128]{1,0:T(8,128)S(1)}, u32[]{:S(2)}, u32[]{:S(2)}) %collective-permute-start.22) | collective-permute-done | bytes 73760 | tf_op jit(solution)/shard_map/ppermute | solution.py:443
  112.5 0.0 collective-permute-done.21
  112.5 0.7 add_add_fusion.gram_in
  113.2 8.4 %last.1 = (f32[288,256]{1,0:T(8,128)}, f32[1,48]{1,0:T(1,128)}) custom-call(f32[144,128]{1,0:T(8,128)} %add_add_fusion.gram_in, f32[48,96]{1,0:T(8,128)} %get-tuple-element.33.coeff_in, f32[2,96,96]{2,1,0:T(8,128)} %get-tuple-element.34.state_in, f32[288,256]{1,0:T(8,128)} %bitcast.15, f32[288,256]{1,0:T(8,128)} %get-tuple-element.29.residual, ...), custom_call_target="tpu_custom_call" | custom-call | tf_op jit(solution)/shard_map/last/pallas_call | solution.py:473
  (7 shorter events, 0.0 us)
Async XLA Ops:
  3.7 2.0 %collective-permute-start = (f32[584,128]{1,0:T(8,128)}, f32[584,128]{1,0:T(8,128)S(1)}, u32[]{:S(2)}, u32[]{:S(2)}) collective-permute-start(f32[584,128]{1,0:T(8,128)} %get-tuple-element.20), channel_id=1, source_target_pairs={{0,1},{2,3},{4,5},{6,7},{8,9},{10,11},{12,13},{14,15},{1,0},{3,2},... | collective-permute-start | bytes 897032 | tf_op jit(solution)/shard_map/ppermute | solution.py:462
  4.2 1.4 %collective-permute-start.1 = (f32[584,128]{1,0:T(8,128)}, f32[584,128]{1,0:T(8,128)S(1)}, u32[]{:S(2)}, u32[]{:S(2)}) collective-permute-start(f32[584,128]{1,0:T(8,128)} %get-tuple-element.21), channel_id=1, source_target_pairs={{1,2},{3,4},{5,6},{7,8},{9,10},{11,12},{13,14},{2,1},{4,3},{6,5},{... | collective-permute-start | bytes 897032 | tf_op jit(solution)/shard_map/ppermute | solution.py:462
  5.7 0.7 copy-start.2
  6.4 0.7 copy-start.3
  19.3 13.2 %collective-permute-start.4 = (f32[48,128]{1,0:T(8,128)}, f32[48,128]{1,0:T(8,128)S(1)}, u32[]{:S(2)}, u32[]{:S(2)}) collective-permute-start(f32[48,128]{1,0:T(8,128)} %get-tuple-element.22), channel_id=1, source_target_pairs={{0,3},{1,2},{2,1},{3,0},{4,7},{5,6},{6,5},{7,4},{8,11},{9,10},{10,... | collective-permute-start | bytes 73736 | tf_op jit(solution)/shard_map/ppermute | solution.py:443
  29.2 4.4 %collective-permute-start.3 = (f32[48,128]{1,0:T(8,128)}, f32[48,128]{1,0:T(8,128)S(1)}, u32[]{:S(2)}, u32[]{:S(2)}) collective-permute-start(f32[48,128]{1,0:T(8,128)} %get-tuple-element.22), channel_id=1, source_target_pairs={{0,2},{1,3},{2,0},{3,1},{4,6},{5,7},{6,4},{7,5},{8,10},{9,11},{10,... | collective-permute-start | bytes 73736 | tf_op jit(solution)/shard_map/ppermute | solution.py:443
  31.3 2.2 %collective-permute-start.2 = (f32[48,128]{1,0:T(8,128)}, f32[48,128]{1,0:T(8,128)S(1)}, u32[]{:S(2)}, u32[]{:S(2)}) collective-permute-start(f32[48,128]{1,0:T(8,128)} %get-tuple-element.22), channel_id=1, source_target_pairs={{0,1},{1,0},{2,3},{3,2},{4,5},{5,4},{6,7},{7,6},{8,9},{9,8},{10,11... | collective-permute-start | bytes 73736 | tf_op jit(solution)/shard_map/ppermute | solution.py:443
  31.4 13.8 %collective-permute-start.8 = (f32[576,128]{1,0:T(8,128)}, f32[576,128]{1,0:T(8,128)S(1)}, u32[]{:S(2)}, u32[]{:S(2)}) collective-permute-start(f32[576,128]{1,0:T(8,128)} %get-tuple-element.24.own_a), channel_id=1, source_target_pairs={{0,1},{2,3},{4,5},{6,7},{8,9},{10,11},{12,13},{14,15},{1,0},{3,2},... | collective-permute-start | bytes 884744 | tf_op jit(solution)/shard_map/ppermute | solution.py:462
  31.8 13.3 %collective-permute-start.9 = (f32[576,128]{1,0:T(8,128)}, f32[576,128]{1,0:T(8,128)S(1)}, u32[]{:S(2)}, u32[]{:S(2)}) collective-permute-start(f32[576,128]{1,0:T(8,128)} %get-tuple-element.25.own_b), channel_id=1, source_target_pairs={{1,2},{3,4},{5,6},{7,8},{9,10},{11,12},{13,14},{2,1},{4,3},{6,5},{... | collective-permute-start | bytes 884744 | tf_op jit(solution)/shard_map/ppermute | solution.py:462
  34.3 10.2 %collective-permute-start.7 = (f32[48,128]{1,0:T(8,128)S(1)}, f32[48,128]{1,0:T(8,128)S(1)}, u32[]{:S(2)}, u32[]{:S(2)}) collective-permute-start(f32[48,128]{1,0:T(8,128)S(1)} %add_add_fusion.5), channel_id=1, source_target_pairs={{0,12},{1,13},{2,14},{3,15},{4,8},{5,9},{6,10},{7,11},{8,4},{9,5},... | collective-permute-start | bytes 73736 | tf_op jit(solution)/shard_map/ppermute | solution.py:443
  39.4 5.1 %collective-permute-start.6 = (f32[48,128]{1,0:T(8,128)S(1)}, f32[48,128]{1,0:T(8,128)S(1)}, u32[]{:S(2)}, u32[]{:S(2)}) collective-permute-start(f32[48,128]{1,0:T(8,128)S(1)} %add_add_fusion.5), channel_id=1, source_target_pairs={{0,8},{1,9},{2,10},{3,11},{4,12},{5,13},{6,14},{7,15},{8,0},{9,1},... | collective-permute-start | bytes 73736 | tf_op jit(solution)/shard_map/ppermute | solution.py:443
  39.4 5.1 %collective-permute-start.5 = (f32[48,128]{1,0:T(8,128)S(1)}, f32[48,128]{1,0:T(8,128)S(1)}, u32[]{:S(2)}, u32[]{:S(2)}) collective-permute-start(f32[48,128]{1,0:T(8,128)S(1)} %add_add_fusion.5), channel_id=1, source_target_pairs={{0,4},{1,5},{2,6},{3,7},{4,0},{5,1},{6,2},{7,3},{8,12},{9,13},{10,... | collective-permute-start | bytes 73736 | tf_op jit(solution)/shard_map/ppermute | solution.py:443
  45.1 0.7 copy-start
  45.1 0.8 copy-start.1
  60.9 3.8 %collective-permute-start.12 = (f32[96,128]{1,0:T(8,128)}, f32[96,128]{1,0:T(8,128)S(1)}, u32[]{:S(2)}, u32[]{:S(2)}) collective-permute-start(f32[96,128]{1,0:T(8,128)} %get-tuple-element.27), channel_id=1, source_target_pairs={{0,3},{1,2},{2,1},{3,0},{4,7},{5,6},{6,5},{7,4},{8,11},{9,10},{10,... | collective-permute-start | bytes 147464 | tf_op jit(solution)/shard_map/ppermute | solution.py:443
  60.9 4.8 %collective-permute-start.11 = (f32[96,128]{1,0:T(8,128)}, f32[96,128]{1,0:T(8,128)S(1)}, u32[]{:S(2)}, u32[]{:S(2)}) collective-permute-start(f32[96,128]{1,0:T(8,128)} %get-tuple-element.27), channel_id=1, source_target_pairs={{0,2},{1,3},{2,0},{3,1},{4,6},{5,7},{6,4},{7,5},{8,10},{9,11},{10,... | collective-permute-start | bytes 147464 | tf_op jit(solution)/shard_map/ppermute | solution.py:443
  61.5 4.2 %collective-permute-start.10 = (f32[96,128]{1,0:T(8,128)}, f32[96,128]{1,0:T(8,128)S(1)}, u32[]{:S(2)}, u32[]{:S(2)}) collective-permute-start(f32[96,128]{1,0:T(8,128)} %get-tuple-element.27), channel_id=1, source_target_pairs={{0,1},{1,0},{2,3},{3,2},{4,5},{5,4},{6,7},{7,6},{8,9},{9,8},{10,11... | collective-permute-start | bytes 147464 | tf_op jit(solution)/shard_map/ppermute | solution.py:443
  62.8 13.8 %collective-permute-start.16 = (f32[576,128]{1,0:T(8,128)}, f32[576,128]{1,0:T(8,128)S(1)}, u32[]{:S(2)}, u32[]{:S(2)}) collective-permute-start(f32[576,128]{1,0:T(8,128)} %get-tuple-element.30.new_a), channel_id=1, source_target_pairs={{0,1},{2,3},{4,5},{6,7},{8,9},{10,11},{12,13},{14,15},{1,0},{3,2},... | collective-permute-start | bytes 884744 | tf_op jit(solution)/shard_map/ppermute | solution.py:462
  62.8 13.8 %collective-permute-start.17 = (f32[576,128]{1,0:T(8,128)}, f32[576,128]{1,0:T(8,128)S(1)}, u32[]{:S(2)}, u32[]{:S(2)}) collective-permute-start(f32[576,128]{1,0:T(8,128)} %get-tuple-element.31.new_b), channel_id=1, source_target_pairs={{1,2},{3,4},{5,6},{7,8},{9,10},{11,12},{13,14},{2,1},{4,3},{6,5},{... | collective-permute-start | bytes 884744 | tf_op jit(solution)/shard_map/ppermute | solution.py:462
  66.5 8.9 %collective-permute-start.15 = (f32[96,128]{1,0:T(8,128)S(1)}, f32[96,128]{1,0:T(8,128)S(1)}, u32[]{:S(2)}, u32[]{:S(2)}) collective-permute-start(f32[96,128]{1,0:T(8,128)S(1)} %add_add_fusion.3), channel_id=1, source_target_pairs={{0,12},{1,13},{2,14},{3,15},{4,8},{5,9},{6,10},{7,11},{8,4},{9,5},... | collective-permute-start | bytes 147464 | tf_op jit(solution)/shard_map/ppermute | solution.py:443
  69.3 6.6 %collective-permute-start.14 = (f32[96,128]{1,0:T(8,128)S(1)}, f32[96,128]{1,0:T(8,128)S(1)}, u32[]{:S(2)}, u32[]{:S(2)}) collective-permute-start(f32[96,128]{1,0:T(8,128)S(1)} %add_add_fusion.3), channel_id=1, source_target_pairs={{0,8},{1,9},{2,10},{3,11},{4,12},{5,13},{6,14},{7,15},{8,0},{9,1},... | collective-permute-start | bytes 147464 | tf_op jit(solution)/shard_map/ppermute | solution.py:443
  69.3 6.6 %collective-permute-start.13 = (f32[96,128]{1,0:T(8,128)S(1)}, f32[96,128]{1,0:T(8,128)S(1)}, u32[]{:S(2)}, u32[]{:S(2)}) collective-permute-start(f32[96,128]{1,0:T(8,128)S(1)} %add_add_fusion.3), channel_id=1, source_target_pairs={{0,4},{1,5},{2,6},{3,7},{4,0},{5,1},{6,2},{7,3},{8,12},{9,13},{10,... | collective-permute-start | bytes 147464 | tf_op jit(solution)/shard_map/ppermute | solution.py:443
  76.6 0.7 copy-start.4
  76.6 0.8 copy-start.5
  96.8 4.2 %collective-permute-start.20 = (f32[144,128]{1,0:T(8,128)}, f32[144,128]{1,0:T(8,128)S(1)}, u32[]{:S(2)}, u32[]{:S(2)}) collective-permute-start(f32[144,128]{1,0:T(8,128)} %get-tuple-element.32), channel_id=1, source_target_pairs={{0,3},{1,2},{2,1},{3,0},{4,7},{5,6},{6,5},{7,4},{8,11},{9,10},{10,... | collective-permute-start | bytes 221192 | tf_op jit(solution)/shard_map/ppermute | solution.py:443
  96.9 5.4 %collective-permute-start.19 = (f32[144,128]{1,0:T(8,128)}, f32[144,128]{1,0:T(8,128)S(1)}, u32[]{:S(2)}, u32[]{:S(2)}) collective-permute-start(f32[144,128]{1,0:T(8,128)} %get-tuple-element.32), channel_id=1, source_target_pairs={{0,2},{1,3},{2,0},{3,1},{4,6},{5,7},{6,4},{7,5},{8,10},{9,11},{10,... | collective-permute-start | bytes 221192 | tf_op jit(solution)/shard_map/ppermute | solution.py:443
  96.9 5.3 %collective-permute-start.18 = (f32[144,128]{1,0:T(8,128)}, f32[144,128]{1,0:T(8,128)S(1)}, u32[]{:S(2)}, u32[]{:S(2)}) collective-permute-start(f32[144,128]{1,0:T(8,128)} %get-tuple-element.32), channel_id=1, source_target_pairs={{0,1},{1,0},{2,3},{3,2},{4,5},{5,4},{6,7},{7,6},{8,9},{9,8},{10,11... | collective-permute-start | bytes 221192 | tf_op jit(solution)/shard_map/ppermute | solution.py:443
  103.2 7.0 %collective-permute-start.23 = (f32[144,128]{1,0:T(8,128)S(1)}, f32[144,128]{1,0:T(8,128)S(1)}, u32[]{:S(2)}, u32[]{:S(2)}) collective-permute-start(f32[144,128]{1,0:T(8,128)S(1)} %add_add_fusion.1), channel_id=1, source_target_pairs={{0,12},{1,13},{2,14},{3,15},{4,8},{5,9},{6,10},{7,11},{8,4},{9,5},... | collective-permute-start | bytes 221192 | tf_op jit(solution)/shard_map/ppermute | solution.py:443
  105.2 7.3 %collective-permute-start.22 = (f32[144,128]{1,0:T(8,128)S(1)}, f32[144,128]{1,0:T(8,128)S(1)}, u32[]{:S(2)}, u32[]{:S(2)}) collective-permute-start(f32[144,128]{1,0:T(8,128)S(1)} %add_add_fusion.1), channel_id=1, source_target_pairs={{0,8},{1,9},{2,10},{3,11},{4,12},{5,13},{6,14},{7,15},{8,0},{9,1},... | collective-permute-start | bytes 221192 | tf_op jit(solution)/shard_map/ppermute | solution.py:443
  105.2 7.3 %collective-permute-start.21 = (f32[144,128]{1,0:T(8,128)S(1)}, f32[144,128]{1,0:T(8,128)S(1)}, u32[]{:S(2)}, u32[]{:S(2)}) collective-permute-start(f32[144,128]{1,0:T(8,128)S(1)} %add_add_fusion.1), channel_id=1, source_target_pairs={{0,4},{1,5},{2,6},{3,7},{4,0},{5,1},{6,2},{7,3},{8,12},{9,13},{10,... | collective-permute-start | bytes 221192 | tf_op jit(solution)/shard_map/ppermute | solution.py:443

commit v4 on v3

--- a/solution.py
+++ b/solution.py
@@ -7,6 +7,7 @@
 from jax.experimental.pallas import tpu as pltpu
 from jax.sharding import PartitionSpec as P
 
+
 HALO = 64
 LANES = 128
 SUB = 8
@@ -48,6 +49,8 @@
 
 def whole(row):
     return jnp.broadcast_to(row,(SUB,row.shape[1]))
+
+
 def eliminate(matrix, others, modes):
     tiles = modes // SUB
     chunks = []
@@ -165,7 +168,7 @@
                 low[pl.ds(row, modes), pl.ds(col, LANES)] = lower
         return unused
 
-    lax.fori_loop(0, comps * groups, one, 0)
+    lax.fori_loop(0, comps * groups, one, 0, unroll=2)
 
 
 def place_sums(high, low, target):
@@ -173,8 +176,12 @@
 
 
 def all_products(dims, ext, stiffness, mass, edges, connect, edge_nodes, picked, high, low, out):
-    comps, modes = dims
     halves = split(ext)
+    own_products(dims, halves, stiffness, mass, connect, picked, high, low, out)
+    edge_products(dims, halves, edges, edge_nodes, picked, high, low, out)
+
+
+def own_products(dims, halves, stiffness, mass, connect, picked, high, low, out):
     own_nodes = connect[...] + (LANES - HALO)
     for number in range(2):
         lane = number * LANES
@@ -191,6 +198,10 @@
             out[...] = total
         else:
             out[...] += total
+
+
+def edge_products(dims, halves, edges, edge_nodes, picked, high, low, out):
+    comps, _ = dims
     nodes = edge_nodes[...]
     pick(halves, chosen_nodes(nodes[:CORNERS], 0, 4 * LANES), 0, picked)
     multiply(dims, lambda comp, group, q, m, j: edges[m, q * comps + comp, j : j + 1, :], 1, picked, high, low)
@@ -234,44 +245,38 @@
     return [pltpu.make_async_copy(a, b, sems.at[first + i]) for i, (a, b) in enumerate([(from_a, below), (from_b, above)])]
 
 
-def pack_kernel(dims, block, connect, stiffness, mass, side_a, side_b, high_stiff, high_mass, low_stiff, low_mass, sems):
-    comps, modes = dims
+def node_kernel(dims, block_in, block, node_a, node_b, sems):
+    for copy in start_all([(block_in, block)], sems):
+        copy.wait()
+    store_sides(block, node_a, node_b)
+
+
+def pack_kernel(dims, connect_in, stiff_in, mass_in, connect, stiffness, mass, edge_a, edge_b, sems):
+    comps, _ = dims
     size = comps * CORNERS
-    upper, lower = pl.ds(LANES, LANES), pl.ds(0, LANES)
-    copies = start_all(
-        [
-            (stiffness.at[:, 3, :, upper], high_stiff.at[0]),
-            (stiffness.at[:, 1, :, upper], high_stiff.at[1]),
-            (mass.at[:, 3, :, upper], high_mass.at[0]),
-            (mass.at[:, 1, :, upper], high_mass.at[1]),
-            (stiffness.at[:, 2, :, lower], low_stiff),
-            (mass.at[:, 2, :, lower], low_mass),
-        ],
-        sems,
-    )
-    links = connect[...].astype(F32)
+    copies = start_all([(connect_in, connect), (stiff_in, stiffness), (mass_in, mass)], sems)
     pad = jnp.zeros((SUB - CORNERS, LANES), F32)
     rows = comps * size
     first = lax.broadcasted_iota(jnp.int32, (rows, LANES), 1) < HALO
     top = 2 * rows
     for copy in copies:
         copy.wait()
+    links = connect[...].astype(F32)
+
+    def corner(matrix, which, lane):
+        return jnp.concatenate([matrix[c * CORNERS + which, :, lane : lane + LANES] for c in range(comps)], axis=0)
 
     def fill(up, down):
-        for slot in range(2):
+        for slot, which in enumerate((3, 1)):
             up[slot * rows : (slot + 1) * rows, :] = jnp.where(
-                first, pltpu.roll(high_stiff[slot].reshape(rows, LANES), HALO, 1), high_mass[slot].reshape(rows, LANES)
+                first, pltpu.roll(corner(stiffness, which, LANES), HALO, 1), corner(mass, which, LANES)
             )
-        down[:rows, :] = jnp.where(
-            first, low_stiff[...].reshape(rows, LANES), pltpu.roll(low_mass[...].reshape(rows, LANES), HALO, 1)
-        )
+        down[:rows, :] = jnp.where(first, corner(stiffness, 2, 0), pltpu.roll(corner(mass, 2, 0), HALO, 1))
         down[rows:top, :] = jnp.zeros((rows, LANES), F32)
-        up[top : top + SUB, :] = jnp.concatenate([pltpu.roll(links[:, LANES:], HALO, 1), pad], axis=0)
-        down[top : top + SUB, :] = jnp.concatenate([links[:, :LANES], pad], axis=0)
-        up[top + SUB :, :] = block[:, LANES:]
-        down[top + SUB :, :] = block[:, :LANES]
-
-    by_side(lambda: fill(side_a, side_b), lambda: fill(side_b, side_a))
+        up[top:, :] = jnp.concatenate([pltpu.roll(links[:, LANES:], HALO, 1), pad], axis=0)
+        down[top:, :] = jnp.concatenate([links[:, :LANES], pad], axis=0)
+
+    by_side(lambda: fill(edge_a, edge_b), lambda: fill(edge_b, edge_a))
 
 
 def store_sides(out, side_a, side_b):
@@ -282,15 +287,25 @@
     by_side(lambda: put(side_b, side_a), lambda: put(side_a, side_b))
 
 
-def first_kernel(dims, block, connect, from_a, from_b, stiff_in, mass_in, edges, edge_nodes, side_a, side_b, gram, picked, high, low, out, below, above, stiffness, mass, sems):
-    comps, modes = dims
+def first_kernel(dims, block, connect, stiffness, mass, from_a, from_b, ext, out, picked, high, low, sems):
+    below, above = ext.at[:, :LANES], ext.at[:, 3 * LANES :]
+    copies = start_sides(from_a, from_b, below, above, sems, 0)
+    ext[:, LANES : 3 * LANES] = block[...]
+    for copy in copies:
+        copy.wait()
+    own_products(dims, split(ext[...]), stiffness, mass, connect, picked, high, low, out)
+
+
+def edge_kernel(dims, block, connect, ext, part, from_a, from_b, edges, edge_nodes, side_a, side_b, gram, picked, high, low, out, below, above, sems):
+    comps, _ = dims
     size = comps * CORNERS
     rows = comps * size
     top = 2 * rows
-    sides = start_sides(from_a, from_b, below, above, sems, 0)
-    copies = start_all([(stiff_in, stiffness), (mass_in, mass)], sems, 2)
+    copies = start_sides(from_a, from_b, below, above, sems, 0)
     first = lax.broadcasted_iota(jnp.int32, (rows, LANES), 1) < HALO
-    for copy in sides:
+    halves = split(ext[...])
+    out[...] = part[...]
+    for copy in copies:
         copy.wait()
     for slot in range(2):
         lower = below[slot * rows : (slot + 1) * rows, :]
@@ -300,23 +315,19 @@
         edges[0, here] = jnp.where(first, lower, rest if slot else pltpu.roll(upper, HALO, 1)).reshape(comps, size, LANES)
         edges[1, here] = jnp.where(first, pltpu.roll(lower, HALO, 1), rest if slot else upper).reshape(comps, size, LANES)
     count = connect.shape[1]
-    before = below[top : top + SUB, :] + (LANES - HALO - count)
-    after = pltpu.roll(above[top : top + SUB, :], HALO, 1) + (LANES - HALO + count)
+    before = below[top:, :] + (LANES - HALO - count)
+    after = pltpu.roll(above[top:, :], HALO, 1) + (LANES - HALO + count)
     edge_nodes[...] = jnp.where(first[:SUB], before, after).astype(jnp.int32)
-    ext = jnp.concatenate([below[top + SUB :, :], block[...], above[top + SUB :, :]], axis=1)
-    for copy in copies:
-        copy.wait()
-    all_products(dims, ext, stiffness, mass, edges, connect, edge_nodes, picked, high, low, out)
+    edge_products(dims, halves, edges, edge_nodes, picked, high, low, out)
     store_sides(out, side_a, side_b)
     store_lanes(gram, grams([block[...]], out[...], dims))
 
 
-def second_kernel(dims, gram_in, connect, edge_nodes, block, from_a, from_b, own_a, own_b, stiff_in, mass_in, edges_in, residual, side_a, side_b, gram, state, picked, high, low, out, below, above, lower, upper, stiffness, mass, edges, sems):
+def second_kernel(dims, gram_in, connect, edge_nodes, block, stiffness, mass, edges, from_a, from_b, own_a, own_b, residual, side_a, side_b, gram, state, picked, high, low, out, below, above, lower, upper, sems):
     comps, modes = dims
     tiles = (below, lower, upper, above)
     copies = start_sides(from_a, from_b, below, above, sems, 0)
     copies += start_sides(own_a, own_b, lower, upper, sems, 2)
-    others = start_all([(stiff_in, stiffness), (mass_in, mass), (edges_in, edges)], sems, 4)
     reduced = gram_in[...]
     stiff_gram = symmetric(reduced[:, :modes])
     mass_gram = symmetric(reduced[:, modes : 2 * modes])
@@ -339,8 +350,6 @@
             left - (dot1(ratio_high, right_high, NN) + (dot1(ratio_high, right_low, NN) + dot1(ratio_low, right_high, NN)))
         )
     ext = jnp.concatenate(pieces, axis=0)
-    for copy in others:
-        copy.wait()
     residual[...] = ext[:, LANES : 3 * LANES]
     all_products(dims, ext, stiffness, mass, edges, connect, edge_nodes, picked, high, low, out)
     store_sides(out, side_a, side_b)
@@ -387,14 +396,13 @@
     return coeff, half, root, solver, mass_all
 
 
-def third_kernel(dims, gram_in, state_in, connect, edge_nodes, block, residual, from_a, from_b, own_a, own_b, more_a, more_b, new_a, new_b, stiff_in, mass_in, edges_in, new, gram, coeff_out, state, picked, high, low, out, below, above, lower, upper, new_below, new_above, new_lower, new_upper, stiffness, mass, edges, sems):
+def third_kernel(dims, gram_in, state_in, connect, edge_nodes, block, residual, stiffness, mass, edges, from_a, from_b, own_a, own_b, more_a, more_b, new_a, new_b, new, gram, coeff_out, state, picked, high, low, out, below, above, lower, upper, new_below, new_above, new_lower, new_upper, sems):
     comps, modes = dims
     tiles = ((below, new_below), (lower, new_lower), (upper, new_upper), (above, new_above))
     copies = start_sides(from_a, from_b, below, above, sems, 0)
     copies += start_sides(own_a, own_b, lower, upper, sems, 2)
     copies += start_sides(more_a, more_b, new_below, new_above, sems, 4)
     copies += start_sides(new_a, new_b, new_lower, new_upper, sems, 6)
-    others = start_all([(stiff_in, stiffness), (mass_in, mass), (edges_in, edges)], sems, 8)
     coeff, half, root, solver, mass_all = small_step(gram_in[...], state_in[1], state_in[2], state_in[0], modes)
     rayleigh = symmetric(dotf(half, root, NT))
     coeff_out[...] = coeff
@@ -414,8 +422,6 @@
         right_high, right_low = split(right)
         pieces.append(dot1(mixed_high, right_high, NN) + (dot1(mixed_high, right_low, NN) + dot1(mixed_low, right_high, NN)))
     ext = jnp.concatenate(pieces, axis=0)
-    for copy in others:
-        copy.wait()
     new[...] = ext[:, LANES : 3 * LANES]
     all_products(dims, ext, stiffness, mass, edges, connect, edge_nodes, picked, high, low, out)
     store_lanes(gram, grams([block[...], residual[...], new[...]], out[...], dims))
@@ -423,7 +429,7 @@
 
 def last_kernel(dims, gram_in, coeff_in, state_in, block, residual, new, modes_out, ritz_out):
     comps, modes = dims
-    coeff, half, root, solver, mass_all = small_step(gram_in[...], state_in[0], state_in[1], coeff_in[...], modes)
+    coeff, half, root, _, _ = small_step(gram_in[...], state_in[0], state_in[1], coeff_in[...], modes)
     ritz_out[...] = jnp.sum(dotf(half, root, NT) * eye(modes), axis=0, keepdims=True)
     coeff_high, coeff_low = split(coeff)
     for c in range(comps):
@@ -461,23 +467,26 @@
         pairs = [(i, i + 1) for i in range(start, count - 1, 2)]
         return lax.ppermute(value, axis, pairs + [(b, a) for a, b in pairs])
 
-    return swap(side_a, 0), swap(side_b, 1)
+    from_a = swap(side_a, 0)
+    from_b = swap(side_b, 1)
+    return from_a, from_b
 
 
 VMEM = pl.BlockSpec(memory_space=pltpu.VMEM)
 HBM = pl.BlockSpec(memory_space=pltpu.HBM)
 
 
-def call(kernel, dims, name, outs, scratch, operands, remote):
-    shapes = tuple(jax.ShapeDtypeStruct(shape, dtype) for shape, dtype in outs)
+def call(kernel, dims, outs, scratch, operands, remote):
+    shapes = tuple(kind(shape, dtype) for kind, shape, dtype in outs)
+    operands = [pltpu.with_memory_space_constraint(x, pltpu.VMEM) for x in operands]
     return pl.pallas_call(
         functools.partial(kernel, dims),
         out_shape=shapes,
         in_specs=[VMEM] * len(operands) + [HBM] * len(remote),
         out_specs=tuple(VMEM for _ in shapes),
         scratch_shapes=scratch,
-        name=name,
-    )(*operands, *remote)
+        compiler_params=pltpu.CompilerParams(vmem_limit_bytes=24 << 20),
+    )(*operands, *[pltpu.with_memory_space_constraint(x, pltpu.HBM) for x in remote])
 
 
 def room(*arrays):
@@ -495,33 +504,40 @@
         pltpu.VMEM((2 * rows, CORNERS * LANES), BF16),
         pltpu.VMEM((2 * rows, count), F32),
     ]
-    wide = ((rows, count), F32)
-    side = ((2 * rows, LANES), F32)
-    packed = ((2 * comps * size + SUB + rows, LANES), F32)
-    edge = pltpu.VMEM((comps, size, LANES), F32)
-    edges_pair = pltpu.VMEM((2, comps, size, LANES), F32)
+    near, far = pltpu.VMEM, jax.ShapeDtypeStruct
+    wide = (near, (rows, count), F32)
+    side = (near, (2 * rows, LANES), F32)
+    node = (near, (rows, LANES), F32)
+    packed = (near, (2 * comps * size + SUB, LANES), F32)
     sems = pltpu.SemaphoreType.DMA
     block = modes_start.transpose(1, 0, 2).reshape(rows, count)
 
-    by_corner = [x.reshape(comps, CORNERS, size, count) for x in (stiffness, mass)]
-    side_a, side_b = call(
+    block, node_a, node_b = call(node_kernel, dims, [wide, node, node], [sems((1,))], (), (block,))
+    node_from = exchange(node_a, node_b, "sub")
+    link, stiff_near, mass_near, edge_a, edge_b = call(
         pack_kernel,
         dims,
-        "pack",
-        [packed, packed],
-        [edges_pair, edges_pair, edge, edge, sems((6,))],
-        (block, connect),
-        by_corner,
-    )
-    from_a, from_b = exchange(side_a, side_b, "sub")
-    edges, edge_nodes, p_a, p_b, gram = call(
+        [(near, connect.shape, connect.dtype), (near, stiffness.shape, F32), (near, mass.shape, F32), packed, packed],
+        [sems((3,))],
+        (),
+        (connect, stiffness, mass),
+    )
+    edge_from = exchange(edge_a, edge_b, "sub")
+    ext, part = call(
         first_kernel,
         dims,
-        "first",
-        [((2, 2 * comps, size, LANES), F32), ((SUB, LANES), jnp.int32), side, side, ((modes, LANES), F32)],
-        work + room(from_a, from_b, stiffness, mass) + [sems((4,))],
-        (block, connect),
-        (from_a, from_b, stiffness, mass),
+        [(near, (rows, 2 * count), F32), (near, (2 * rows, count), F32)],
+        work[:3] + [sems((2,))],
+        (block, link, stiff_near, mass_near, *node_from),
+        (),
+    )
+    edges, edge_nodes, p_a, p_b, gram = call(
+        edge_kernel,
+        dims,
+        [(near, (2, 2 * comps, size, LANES), F32), (near, (SUB, LANES), jnp.int32), side, side, (near, (modes, LANES), F32)],
+        work + room(*edge_from) + [sems((2,))],
+        (block, link, ext, part, *edge_from),
+        (),
     )
     gram = total_over(gram, "sub")
     p_from_a, p_from_b = exchange(p_a, p_b, "sub")
@@ -529,11 +545,10 @@
     residual, q_a, q_b, gram, state = call(
         second_kernel,
         dims,
-        "second",
-        [wide, side, side, ((2 * modes, LANES), F32), ((3, modes, modes), F32)],
-        work + room(*p, stiffness, mass, edges) + [sems((7,))],
-        (gram, connect, edge_nodes, block),
-        (*p, stiffness, mass, edges),
+        [wide, side, side, (near, (2 * modes, LANES), F32), (near, (3, modes, modes), F32)],
+        work + room(*p) + [sems((4,))],
+        (gram, link, edge_nodes, block, stiff_near, mass_near, edges, *p),
+        (),
     )
     gram = total_over(gram, "sub")
     q_from_a, q_from_b = exchange(q_a, q_b, "sub")
@@ -541,18 +556,16 @@
     new, gram, coeff, state = call(
         third_kernel,
         dims,
-        "third",
-        [wide, ((3 * modes, LANES), F32), ((modes, 2 * modes), F32), ((2, 2 * modes, 2 * modes), F32)],
-        work + room(*p, *q, stiffness, mass, edges) + [sems((11,))],
-        (gram, state, connect, edge_nodes, block, residual),
-        (*p, *q, stiffness, mass, edges),
+        [wide, (near, (3 * modes, LANES), F32), (near, (modes, 2 * modes), F32), (near, (2, 2 * modes, 2 * modes), F32)],
+        work + room(*p, *q) + [sems((8,))],
+        (gram, state, link, edge_nodes, block, residual, stiff_near, mass_near, edges, *p, *q),
+        (),
     )
     gram = total_over(gram, "sub")
     result, ritz = call(
         last_kernel,
         dims,
-        "last",
-        [wide, ((1, modes), F32)],
+        [(far, (rows, count), F32), (far, (1, modes), F32)],
         [],
         (gram, coeff, state, block, residual, new),
         (),

time: 122 us -> 107 us (0.88)
  Pallas kernels: 57.9 us -> 48.5 us
  other arithmetic: 4.37 us -> 0.08 us
  local copies, waits for them, and re-layouts: 3.05 us -> 0 us
  waiting for transfers between devices: 21.7 us -> 23.3 us
    pallas_call x5 -> x7, Pallas kernels: 57.9 us -> 48.5 us  [call(): pl.pallas_call(functools.partial(kernel, dims), out_shape=shapes, in_spec...]
    ppermute x6 -> x8, starting transfers between devices: 3.21 us -> 7.63 us  [swap(): return lax.ppermute(value, axis, pairs + [(b, a) for a, b in pairs])]
    add x6, other arithmetic: 4.37 us -> 0.08 us  [total_over(): value = value + one + (two + three)]
    ppermute x18, starting transfers between devices: 30.6 us -> 26.5 us  [from_partner(): return lax.ppermute(part, axis, [(i, i ^ bits) for i in range(count)])]
    unnamed x12 -> x0, local copies, waits for them, and re-layouts: 3.05 us -> none
    ppermute x18, waiting for transfers between devices: 21 us -> 23 us  [from_partner(): return lax.ppermute(part, axis, [(i, i ^ bits) for i in range(count)])]
  transfers between devices with their start and end apart: 24 -> 26, of which waited for: 11 -> 11; matrix products, arithmetic and copies ran while one was open for 2% -> 0% of each run, Pallas kernels for 0% -> 7%
where the time goes in v4:
time: 107 us
  Pallas kernels  48.5 us (45%)
  starting transfers between devices  34.1 us (32%)
  waiting for transfers between devices  23.3 us (22%)
    pallas_call x7, Pallas kernels, call(): pl.pallas_call(functools.partial(kernel, dims), out_shape=shapes, in_spec...  48.5 us
    ppermute x18, starting transfers between devices, from_partner(): return lax.ppermute(part, axis, [(i, i ^ bits) for i in range(count)])  26.5 us
    ppermute x18, waiting for transfers between devices, from_partner(): return lax.ppermute(part, axis, [(i, i ^ bits) for i in range(count)])  23 us
    ppermute x8, starting transfers between devices, swap(): return lax.ppermute(value, axis, pairs + [(b, a) for a, b in pairs])  7.63 us
  transfers between devices with their start and end apart: 26, of which 11 were waited for; matrix products, arithmetic and copies ran while one was open for 0% of the time, Pallas kernels for 7%

profile of v4, /device:TPU:0, one launch (start us, length us, event | category | flops | bytes accessed | tf_op | source)
XLA Modules:
  0.0 106.8 jit_solution(15664869672747525839)
XLA Ops:
  0.6 1.4 %shard_map.60 = (s32[4,256]{1,0:T(4,128)S(1)}, f32[24,24,256]{2,1,0:T(8,128)S(1)}, f32[24,24,256]{2,1,0:T(8,128)S(1)}, f32[296,128]{1,0:T(8,128)S(1)}, f32[296,128]{1,0:T(8,128)S(1)}) custom-call(s32[4,256]{1,0:T(4,128)} %connect_in.1, f32[24,24,256]{2,1,0:T(8,128)} %stiff_in.1, f32[24,24,256]{2,1,0:T(8,128)} %mass_in.1), custom_call_target="tpu_custom_call" | custom-call | tf_op jit(solution)/shard_map/pallas_call | solution.py:482
  2.1 0.6 collective-permute-start.2
  2.6 0.7 collective-permute-start.3
  3.3 1.0 shard_map.59
  4.3 3.9 %collective-permute-start = (f32[288,128]{1,0:T(8,128)S(1)}, f32[288,128]{1,0:T(8,128)S(1)}, u32[]{:S(2)}, u32[]{:S(2)}) collective-permute-start(f32[288,128]{1,0:T(8,128)S(1)} %get-tuple-element.32), channel_id=1, source_target_pairs={{0,1},{2,3},{4,5},{6,7},{8,9},{10,11},{12,13},{14,15},{1,0},{3,2},... | collective-permute-start | bytes 442376 | tf_op jit(solution)/shard_map/ppermute | solution.py:468
  8.2 0.7 collective-permute-start.1
  8.9 0.3 collective-permute-done.from_a
  9.2 0.0 collective-permute-done.1.from_b
  9.2 6.8 %shard_map.61 = (f32[288,512]{1,0:T(8,128)S(1)}, f32[576,256]{1,0:T(8,128)S(1)}) custom-call(f32[288,256]{1,0:T(8,128)S(1)} %get-tuple-element.28.block, s32[4,256]{1,0:T(4,128)S(1)} %get-tuple-element.29.connect, f32[24,24,256]{2,1,0:T(8,128)S(1)} %get-tuple-element.30.stiffness, f32[24,24,256]{2,1,0:T(8,128)S(1)} %get-tuple-element.31.mass, ...), custom_call_target="tpu_custom_call" | custom-call | tf_op jit(solution)/shard_map/pallas_call | solution.py:482
  16.0 0.0 collective-permute-done.2.from_a
  16.1 0.0 collective-permute-done.3.from_b
  16.1 3.5 %shard_map.62 = (f32[2,12,24,128]{3,2,1,0:T(8,128)S(1)}, s32[8,128]{1,0:T(8,128)S(1)}, f32[576,128]{1,0:T(8,128)S(1)}, f32[576,128]{1,0:T(8,128)S(1)}, f32[48,128]{1,0:T(8,128)S(1)}) custom-call(f32[288,256]{1,0:T(8,128)S(1)} %get-tuple-element.28.block, s32[4,256]{1,0:T(4,128)S(1)} %get-tuple-element.29.connect, f32[288,512]{1,0:T(8,128)S(1)} %get-tuple-element.34.ext, ...), custom_call_target="tpu_custom_call" | custom-call | tf_op jit(solution)/shard_map/pallas_call | solution.py:482
  19.6 7.7 %collective-permute-start.6 = (f32[48,128]{1,0:T(8,128)S(1)}, f32[48,128]{1,0:T(8,128)S(1)}, u32[]{:S(2)}, u32[]{:S(2)}) collective-permute-start(f32[48,128]{1,0:T(8,128)S(1)} %get-tuple-element.38), channel_id=1, source_target_pairs={{0,3},{1,2},{2,1},{3,0},{4,7},{5,6},{6,5},{7,4},{8,11},{9,10},{10,... | collective-permute-start | bytes 73736 | tf_op jit(solution)/shard_map/ppermute | solution.py:449
  27.2 1.0 collective-permute-start.5
  28.2 0.0 collective-permute-start.4
  28.3 0.5 collective-permute-start.10
  28.8 0.7 collective-permute-start.11
  29.4 0.0 collective-permute-done.6
  29.4 1.8 %collective-permute-done.5 = f32[48,128]{1,0:T(8,128)S(1)} collective-permute-done((f32[48,128]{1,0:T(8,128)S(1)}, f32[48,128]{1,0:T(8,128)S(1)}, u32[]{:S(2)}, u32[]{:S(2)}) %collective-permute-start.5) | collective-permute-done | bytes 24608 | tf_op jit(solution)/shard_map/ppermute | solution.py:449
  31.2 0.0 collective-permute-done.4
  31.3 4.4 %collective-permute-start.9 = (f32[48,128]{1,0:T(8,128)S(1)}, f32[48,128]{1,0:T(8,128)S(1)}, u32[]{:S(2)}, u32[]{:S(2)}) collective-permute-start(f32[48,128]{1,0:T(8,128)S(1)} %add_add_fusion.5), channel_id=1, source_target_pairs={{0,12},{1,13},{2,14},{3,15},{4,8},{5,9},{6,10},{7,11},{8,4},{9,5},... | collective-permute-start | bytes 73736 | tf_op jit(solution)/shard_map/ppermute | solution.py:449
  35.7 0.0 collective-permute-start.8
  35.7 0.6 collective-permute-start.7
  36.3 4.7 %collective-permute-done.9 = f32[48,128]{1,0:T(8,128)S(1)} collective-permute-done((f32[48,128]{1,0:T(8,128)S(1)}, f32[48,128]{1,0:T(8,128)S(1)}, u32[]{:S(2)}, u32[]{:S(2)}) %collective-permute-start.9) | collective-permute-done | bytes 24608 | tf_op jit(solution)/shard_map/ppermute | solution.py:449
  41.0 0.0 collective-permute-done.8
  41.0 0.0 collective-permute-done.7
  41.0 0.0 collective-permute-done.10.from_a
  41.0 0.0 collective-permute-done.11.from_b
  41.0 12.1 %shard_map.63 = (f32[288,256]{1,0:T(8,128)S(1)}, f32[576,128]{1,0:T(8,128)S(1)}, f32[576,128]{1,0:T(8,128)S(1)}, f32[96,128]{1,0:T(8,128)S(1)}, f32[3,48,48]{2,1,0:T(8,128)S(1)}) custom-call(f32[48,128]{1,0:T(8,128)S(1)} %add_add_fusion.4.gram_in, s32[4,256]{1,0:T(4,128)S(1)} %get-tuple-element.29.connect, s32[8,128]{1,0:T(8,128)S(1)} %get-tuple-element.39.edge_nodes, ...), custom_call_target="tpu_custom_call" | custom-call | tf_op jit(solution)/shard_map/pallas_call | solution.py:482
  53.2 0.1 collective-permute-start.14
  53.2 0.2 collective-permute-start.13
  53.5 1.6 %collective-permute-start.12 = (f32[96,128]{1,0:T(8,128)S(1)}, f32[96,128]{1,0:T(8,128)S(1)}, u32[]{:S(2)}, u32[]{:S(2)}) collective-permute-start(f32[96,128]{1,0:T(8,128)S(1)} %get-tuple-element.43), channel_id=1, source_target_pairs={{0,1},{1,0},{2,3},{3,2},{4,5},{5,4},{6,7},{7,6},{8,9},{9,8},{10,11... | collective-permute-start | bytes 147464 | tf_op jit(solution)/shard_map/ppermute | solution.py:449
  55.1 0.0 collective-permute-start.18
  55.1 0.7 collective-permute-start.19
  55.8 1.0 collective-permute-done.14
  56.7 1.1 collective-permute-done.13
  57.8 0.0 collective-permute-done.12
  57.8 3.1 %collective-permute-start.17 = (f32[96,128]{1,0:T(8,128)S(1)}, f32[96,128]{1,0:T(8,128)S(1)}, u32[]{:S(2)}, u32[]{:S(2)}) collective-permute-start(f32[96,128]{1,0:T(8,128)S(1)} %add_add_fusion.3), channel_id=1, source_target_pairs={{0,12},{1,13},{2,14},{3,15},{4,8},{5,9},{6,10},{7,11},{8,4},{9,5},... | collective-permute-start | bytes 147464 | tf_op jit(solution)/shard_map/ppermute | solution.py:449
  60.9 0.0 collective-permute-start.16
  60.9 1.4 %collective-permute-start.15 = (f32[96,128]{1,0:T(8,128)S(1)}, f32[96,128]{1,0:T(8,128)S(1)}, u32[]{:S(2)}, u32[]{:S(2)}) collective-permute-start(f32[96,128]{1,0:T(8,128)S(1)} %add_add_fusion.3), channel_id=1, source_target_pairs={{0,4},{1,5},{2,6},{3,7},{4,0},{5,1},{6,2},{7,3},{8,12},{9,13},{10,... | collective-permute-start | bytes 147464 | tf_op jit(solution)/shard_map/ppermute | solution.py:449
  62.3 5.4 %collective-permute-done.17 = f32[96,128]{1,0:T(8,128)S(1)} collective-permute-done((f32[96,128]{1,0:T(8,128)S(1)}, f32[96,128]{1,0:T(8,128)S(1)}, u32[]{:S(2)}, u32[]{:S(2)}) %collective-permute-start.17) | collective-permute-done | bytes 49184 | tf_op jit(solution)/shard_map/ppermute | solution.py:449
  67.6 0.8 collective-permute-done.16
  68.5 0.0 collective-permute-done.15
  68.5 0.0 collective-permute-done.18.more_a
  68.5 0.0 collective-permute-done.19.more_b
  68.5 16.5 %shard_map.64 = (f32[288,256]{1,0:T(8,128)S(1)}, f32[144,128]{1,0:T(8,128)S(1)}, f32[48,96]{1,0:T(8,128)S(1)}, f32[2,96,96]{2,1,0:T(8,128)S(1)}) custom-call(f32[96,128]{1,0:T(8,128)S(1)} %add_add_fusion.2.gram_in, f32[3,48,48]{2,1,0:T(8,128)S(1)} %get-tuple-element.44.state_in, s32[4,256]{1,0:T(4,128)S(1)} %get-tuple-element.29.connect, ...), custom_call_target="tpu_custom_call" | custom-call | tf_op jit(solution)/shard_map/pallas_call | solution.py:482
  85.0 0.1 collective-permute-start.22
  85.1 0.1 collective-permute-start.21
  85.1 1.8 %collective-permute-start.20 = (f32[144,128]{1,0:T(8,128)S(1)}, f32[144,128]{1,0:T(8,128)S(1)}, u32[]{:S(2)}, u32[]{:S(2)}) collective-permute-start(f32[144,128]{1,0:T(8,128)S(1)} %get-tuple-element.48), channel_id=1, source_target_pairs={{0,1},{1,0},{2,3},{3,2},{4,5},{5,4},{6,7},{7,6},{8,9},{9,8},{10,11... | collective-permute-start | bytes 221192 | tf_op jit(solution)/shard_map/ppermute | solution.py:449
  86.9 2.0 %collective-permute-done.22 = f32[144,128]{1,0:T(8,128)S(1)} collective-permute-done((f32[144,128]{1,0:T(8,128)S(1)}, f32[144,128]{1,0:T(8,128)S(1)}, u32[]{:S(2)}, u32[]{:S(2)}) %collective-permute-start.22) | collective-permute-done | bytes 73760 | tf_op jit(solution)/shard_map/ppermute | solution.py:449
  89.0 1.3 %collective-permute-done.21 = f32[144,128]{1,0:T(8,128)S(1)} collective-permute-done((f32[144,128]{1,0:T(8,128)S(1)}, f32[144,128]{1,0:T(8,128)S(1)}, u32[]{:S(2)}, u32[]{:S(2)}) %collective-permute-start.21) | collective-permute-done | bytes 73760 | tf_op jit(solution)/shard_map/ppermute | solution.py:449
  90.3 0.0 collective-permute-done.20
  90.3 2.1 %collective-permute-start.25 = (f32[144,128]{1,0:T(8,128)S(1)}, f32[144,128]{1,0:T(8,128)S(1)}, u32[]{:S(2)}, u32[]{:S(2)}) collective-permute-start(f32[144,128]{1,0:T(8,128)S(1)} %add_add_fusion.1), channel_id=1, source_target_pairs={{0,12},{1,13},{2,14},{3,15},{4,8},{5,9},{6,10},{7,11},{8,4},{9,5},... | collective-permute-start | bytes 221192 | tf_op jit(solution)/shard_map/ppermute | solution.py:449
  92.4 0.0 collective-permute-start.24
  92.4 2.4 %collective-permute-start.23 = (f32[144,128]{1,0:T(8,128)S(1)}, f32[144,128]{1,0:T(8,128)S(1)}, u32[]{:S(2)}, u32[]{:S(2)}) collective-permute-start(f32[144,128]{1,0:T(8,128)S(1)} %add_add_fusion.1), channel_id=1, source_target_pairs={{0,4},{1,5},{2,6},{3,7},{4,0},{5,1},{6,2},{7,3},{8,12},{9,13},{10,... | collective-permute-start | bytes 221192 | tf_op jit(solution)/shard_map/ppermute | solution.py:449
  94.8 2.6 %collective-permute-done.25 = f32[144,128]{1,0:T(8,128)S(1)} collective-permute-done((f32[144,128]{1,0:T(8,128)S(1)}, f32[144,128]{1,0:T(8,128)S(1)}, u32[]{:S(2)}, u32[]{:S(2)}) %collective-permute-start.25) | collective-permute-done | bytes 73760 | tf_op jit(solution)/shard_map/ppermute | solution.py:449
  97.3 2.3 %collective-permute-done.24 = f32[144,128]{1,0:T(8,128)S(1)} collective-permute-done((f32[144,128]{1,0:T(8,128)S(1)}, f32[144,128]{1,0:T(8,128)S(1)}, u32[]{:S(2)}, u32[]{:S(2)}) %collective-permute-start.24) | collective-permute-done | bytes 73760 | tf_op jit(solution)/shard_map/ppermute | solution.py:449
  99.6 0.0 collective-permute-done.23
  99.6 7.2 %shard_map.65 = (f32[288,256]{1,0:T(8,128)}, f32[1,48]{1,0:T(1,128)}) custom-call(f32[144,128]{1,0:T(8,128)S(1)} %add_add_fusion.gram_in, f32[48,96]{1,0:T(8,128)S(1)} %get-tuple-element.49.coeff_in, f32[2,96,96]{2,1,0:T(8,128)S(1)} %get-tuple-element.50.state_in, f32[288,256]{1,0:T(8,128)S(1)} %get-tuple-element.28.block, ...), custom_call_target="tpu_custom_call" | custom-call | tf_op jit(solution)/shard_map/pallas_call | solution.py:482
  (6 shorter events, 0.1 us)
Async XLA Ops:
  2.1 14.0 %collective-permute-start.2 = (f32[296,128]{1,0:T(8,128)S(1)}, f32[296,128]{1,0:T(8,128)S(1)}, u32[]{:S(2)}, u32[]{:S(2)}) collective-permute-start(f32[296,128]{1,0:T(8,128)S(1)} %get-tuple-element.36), channel_id=1, source_target_pairs={{0,1},{2,3},{4,5},{6,7},{8,9},{10,11},{12,13},{14,15},{1,0},{3,2},... | collective-permute-start | bytes 454664 | tf_op jit(solution)/shard_map/ppermute | solution.py:468
  2.6 13.4 %collective-permute-start.3 = (f32[296,128]{1,0:T(8,128)S(1)}, f32[296,128]{1,0:T(8,128)S(1)}, u32[]{:S(2)}, u32[]{:S(2)}) collective-permute-start(f32[296,128]{1,0:T(8,128)S(1)} %get-tuple-element.37), channel_id=1, source_target_pairs={{1,2},{3,4},{5,6},{7,8},{9,10},{11,12},{13,14},{2,1},{4,3},{6,5},{... | collective-permute-start | bytes 454664 | tf_op jit(solution)/shard_map/ppermute | solution.py:468
  4.3 5.0 %collective-permute-start = (f32[288,128]{1,0:T(8,128)S(1)}, f32[288,128]{1,0:T(8,128)S(1)}, u32[]{:S(2)}, u32[]{:S(2)}) collective-permute-start(f32[288,128]{1,0:T(8,128)S(1)} %get-tuple-element.32), channel_id=1, source_target_pairs={{0,1},{2,3},{4,5},{6,7},{8,9},{10,11},{12,13},{14,15},{1,0},{3,2},... | collective-permute-start | bytes 442376 | tf_op jit(solution)/shard_map/ppermute | solution.py:468
  8.2 1.0 collective-permute-start.1
  19.6 9.9 %collective-permute-start.6 = (f32[48,128]{1,0:T(8,128)S(1)}, f32[48,128]{1,0:T(8,128)S(1)}, u32[]{:S(2)}, u32[]{:S(2)}) collective-permute-start(f32[48,128]{1,0:T(8,128)S(1)} %get-tuple-element.38), channel_id=1, source_target_pairs={{0,3},{1,2},{2,1},{3,0},{4,7},{5,6},{6,5},{7,4},{8,11},{9,10},{10,... | collective-permute-start | bytes 73736 | tf_op jit(solution)/shard_map/ppermute | solution.py:449
  27.2 4.0 %collective-permute-start.5 = (f32[48,128]{1,0:T(8,128)S(1)}, f32[48,128]{1,0:T(8,128)S(1)}, u32[]{:S(2)}, u32[]{:S(2)}) collective-permute-start(f32[48,128]{1,0:T(8,128)S(1)} %get-tuple-element.38), channel_id=1, source_target_pairs={{0,2},{1,3},{2,0},{3,1},{4,6},{5,7},{6,4},{7,5},{8,10},{9,11},{10,... | collective-permute-start | bytes 73736 | tf_op jit(solution)/shard_map/ppermute | solution.py:449
  28.2 3.0 %collective-permute-start.4 = (f32[48,128]{1,0:T(8,128)S(1)}, f32[48,128]{1,0:T(8,128)S(1)}, u32[]{:S(2)}, u32[]{:S(2)}) collective-permute-start(f32[48,128]{1,0:T(8,128)S(1)} %get-tuple-element.38), channel_id=1, source_target_pairs={{0,1},{1,0},{2,3},{3,2},{4,5},{5,4},{6,7},{7,6},{8,9},{9,8},{10,11... | collective-permute-start | bytes 73736 | tf_op jit(solution)/shard_map/ppermute | solution.py:449
  28.3 12.7 %collective-permute-start.10 = (f32[576,128]{1,0:T(8,128)S(1)}, f32[576,128]{1,0:T(8,128)S(1)}, u32[]{:S(2)}, u32[]{:S(2)}) collective-permute-start(f32[576,128]{1,0:T(8,128)S(1)} %get-tuple-element.41.own_a), channel_id=1, source_target_pairs={{0,1},{2,3},{4,5},{6,7},{8,9},{10,11},{12,13},{14,15},{1,0},{3,2},... | collective-permute-start | bytes 884744 | tf_op jit(solution)/shard_map/ppermute | solution.py:468
  28.8 12.3 %collective-permute-start.11 = (f32[576,128]{1,0:T(8,128)S(1)}, f32[576,128]{1,0:T(8,128)S(1)}, u32[]{:S(2)}, u32[]{:S(2)}) collective-permute-start(f32[576,128]{1,0:T(8,128)S(1)} %get-tuple-element.42.own_b), channel_id=1, source_target_pairs={{1,2},{3,4},{5,6},{7,8},{9,10},{11,12},{13,14},{2,1},{4,3},{6,5},{... | collective-permute-start | bytes 884744 | tf_op jit(solution)/shard_map/ppermute | solution.py:468
  31.3 9.7 %collective-permute-start.9 = (f32[48,128]{1,0:T(8,128)S(1)}, f32[48,128]{1,0:T(8,128)S(1)}, u32[]{:S(2)}, u32[]{:S(2)}) collective-permute-start(f32[48,128]{1,0:T(8,128)S(1)} %add_add_fusion.5), channel_id=1, source_target_pairs={{0,12},{1,13},{2,14},{3,15},{4,8},{5,9},{6,10},{7,11},{8,4},{9,5},... | collective-permute-start | bytes 73736 | tf_op jit(solution)/shard_map/ppermute | solution.py:449
  35.7 5.4 %collective-permute-start.8 = (f32[48,128]{1,0:T(8,128)S(1)}, f32[48,128]{1,0:T(8,128)S(1)}, u32[]{:S(2)}, u32[]{:S(2)}) collective-permute-start(f32[48,128]{1,0:T(8,128)S(1)} %add_add_fusion.5), channel_id=1, source_target_pairs={{0,8},{1,9},{2,10},{3,11},{4,12},{5,13},{6,14},{7,15},{8,0},{9,1},... | collective-permute-start | bytes 73736 | tf_op jit(solution)/shard_map/ppermute | solution.py:449
  35.7 5.4 %collective-permute-start.7 = (f32[48,128]{1,0:T(8,128)S(1)}, f32[48,128]{1,0:T(8,128)S(1)}, u32[]{:S(2)}, u32[]{:S(2)}) collective-permute-start(f32[48,128]{1,0:T(8,128)S(1)} %add_add_fusion.5), channel_id=1, source_target_pairs={{0,4},{1,5},{2,6},{3,7},{4,0},{5,1},{6,2},{7,3},{8,12},{9,13},{10,... | collective-permute-start | bytes 73736 | tf_op jit(solution)/shard_map/ppermute | solution.py:449
  53.2 3.6 %collective-permute-start.14 = (f32[96,128]{1,0:T(8,128)S(1)}, f32[96,128]{1,0:T(8,128)S(1)}, u32[]{:S(2)}, u32[]{:S(2)}) collective-permute-start(f32[96,128]{1,0:T(8,128)S(1)} %get-tuple-element.43), channel_id=1, source_target_pairs={{0,3},{1,2},{2,1},{3,0},{4,7},{5,6},{6,5},{7,4},{8,11},{9,10},{10,... | collective-permute-start | bytes 147464 | tf_op jit(solution)/shard_map/ppermute | solution.py:449
  53.2 4.6 %collective-permute-start.13 = (f32[96,128]{1,0:T(8,128)S(1)}, f32[96,128]{1,0:T(8,128)S(1)}, u32[]{:S(2)}, u32[]{:S(2)}) collective-permute-start(f32[96,128]{1,0:T(8,128)S(1)} %get-tuple-element.43), channel_id=1, source_target_pairs={{0,2},{1,3},{2,0},{3,1},{4,6},{5,7},{6,4},{7,5},{8,10},{9,11},{10,... | collective-permute-start | bytes 147464 | tf_op jit(solution)/shard_map/ppermute | solution.py:449
  53.5 4.3 %collective-permute-start.12 = (f32[96,128]{1,0:T(8,128)S(1)}, f32[96,128]{1,0:T(8,128)S(1)}, u32[]{:S(2)}, u32[]{:S(2)}) collective-permute-start(f32[96,128]{1,0:T(8,128)S(1)} %get-tuple-element.43), channel_id=1, source_target_pairs={{0,1},{1,0},{2,3},{3,2},{4,5},{5,4},{6,7},{7,6},{8,9},{9,8},{10,11... | collective-permute-start | bytes 147464 | tf_op jit(solution)/shard_map/ppermute | solution.py:449
  55.1 13.4 %collective-permute-start.18 = (f32[576,128]{1,0:T(8,128)S(1)}, f32[576,128]{1,0:T(8,128)S(1)}, u32[]{:S(2)}, u32[]{:S(2)}) collective-permute-start(f32[576,128]{1,0:T(8,128)S(1)} %get-tuple-element.46.new_a), channel_id=1, source_target_pairs={{0,1},{2,3},{4,5},{6,7},{8,9},{10,11},{12,13},{14,15},{1,0},{3,2},... | collective-permute-start | bytes 884744 | tf_op jit(solution)/shard_map/ppermute | solution.py:468
  55.1 13.4 %collective-permute-start.19 = (f32[576,128]{1,0:T(8,128)S(1)}, f32[576,128]{1,0:T(8,128)S(1)}, u32[]{:S(2)}, u32[]{:S(2)}) collective-permute-start(f32[576,128]{1,0:T(8,128)S(1)} %get-tuple-element.47.new_b), channel_id=1, source_target_pairs={{1,2},{3,4},{5,6},{7,8},{9,10},{11,12},{13,14},{2,1},{4,3},{6,5},{... | collective-permute-start | bytes 884744 | tf_op jit(solution)/shard_map/ppermute | solution.py:468
  57.8 9.8 %collective-permute-start.17 = (f32[96,128]{1,0:T(8,128)S(1)}, f32[96,128]{1,0:T(8,128)S(1)}, u32[]{:S(2)}, u32[]{:S(2)}) collective-permute-start(f32[96,128]{1,0:T(8,128)S(1)} %add_add_fusion.3), channel_id=1, source_target_pairs={{0,12},{1,13},{2,14},{3,15},{4,8},{5,9},{6,10},{7,11},{8,4},{9,5},... | collective-permute-start | bytes 147464 | tf_op jit(solution)/shard_map/ppermute | solution.py:449
  60.9 7.6 %collective-permute-start.16 = (f32[96,128]{1,0:T(8,128)S(1)}, f32[96,128]{1,0:T(8,128)S(1)}, u32[]{:S(2)}, u32[]{:S(2)}) collective-permute-start(f32[96,128]{1,0:T(8,128)S(1)} %add_add_fusion.3), channel_id=1, source_target_pairs={{0,8},{1,9},{2,10},{3,11},{4,12},{5,13},{6,14},{7,15},{8,0},{9,1},... | collective-permute-start | bytes 147464 | tf_op jit(solution)/shard_map/ppermute | solution.py:449
  60.9 7.6 %collective-permute-start.15 = (f32[96,128]{1,0:T(8,128)S(1)}, f32[96,128]{1,0:T(8,128)S(1)}, u32[]{:S(2)}, u32[]{:S(2)}) collective-permute-start(f32[96,128]{1,0:T(8,128)S(1)} %add_add_fusion.3), channel_id=1, source_target_pairs={{0,4},{1,5},{2,6},{3,7},{4,0},{5,1},{6,2},{7,3},{8,12},{9,13},{10,... | collective-permute-start | bytes 147464 | tf_op jit(solution)/shard_map/ppermute | solution.py:449
  85.0 4.0 %collective-permute-start.22 = (f32[144,128]{1,0:T(8,128)S(1)}, f32[144,128]{1,0:T(8,128)S(1)}, u32[]{:S(2)}, u32[]{:S(2)}) collective-permute-start(f32[144,128]{1,0:T(8,128)S(1)} %get-tuple-element.48), channel_id=1, source_target_pairs={{0,3},{1,2},{2,1},{3,0},{4,7},{5,6},{6,5},{7,4},{8,11},{9,10},{10,... | collective-permute-start | bytes 221192 | tf_op jit(solution)/shard_map/ppermute | solution.py:449
  85.1 5.2 %collective-permute-start.21 = (f32[144,128]{1,0:T(8,128)S(1)}, f32[144,128]{1,0:T(8,128)S(1)}, u32[]{:S(2)}, u32[]{:S(2)}) collective-permute-start(f32[144,128]{1,0:T(8,128)S(1)} %get-tuple-element.48), channel_id=1, source_target_pairs={{0,2},{1,3},{2,0},{3,1},{4,6},{5,7},{6,4},{7,5},{8,10},{9,11},{10,... | collective-permute-start | bytes 221192 | tf_op jit(solution)/shard_map/ppermute | solution.py:449
  85.1 5.1 %collective-permute-start.20 = (f32[144,128]{1,0:T(8,128)S(1)}, f32[144,128]{1,0:T(8,128)S(1)}, u32[]{:S(2)}, u32[]{:S(2)}) collective-permute-start(f32[144,128]{1,0:T(8,128)S(1)} %get-tuple-element.48), channel_id=1, source_target_pairs={{0,1},{1,0},{2,3},{3,2},{4,5},{5,4},{6,7},{7,6},{8,9},{9,8},{10,11... | collective-permute-start | bytes 221192 | tf_op jit(solution)/shard_map/ppermute | solution.py:449
  90.3 7.0 %collective-permute-start.25 = (f32[144,128]{1,0:T(8,128)S(1)}, f32[144,128]{1,0:T(8,128)S(1)}, u32[]{:S(2)}, u32[]{:S(2)}) collective-permute-start(f32[144,128]{1,0:T(8,128)S(1)} %add_add_fusion.1), channel_id=1, source_target_pairs={{0,12},{1,13},{2,14},{3,15},{4,8},{5,9},{6,10},{7,11},{8,4},{9,5},... | collective-permute-start | bytes 221192 | tf_op jit(solution)/shard_map/ppermute | solution.py:449
  92.4 7.2 %collective-permute-start.24 = (f32[144,128]{1,0:T(8,128)S(1)}, f32[144,128]{1,0:T(8,128)S(1)}, u32[]{:S(2)}, u32[]{:S(2)}) collective-permute-start(f32[144,128]{1,0:T(8,128)S(1)} %add_add_fusion.1), channel_id=1, source_target_pairs={{0,8},{1,9},{2,10},{3,11},{4,12},{5,13},{6,14},{7,15},{8,0},{9,1},... | collective-permute-start | bytes 221192 | tf_op jit(solution)/shard_map/ppermute | solution.py:449
  92.4 7.2 %collective-permute-start.23 = (f32[144,128]{1,0:T(8,128)S(1)}, f32[144,128]{1,0:T(8,128)S(1)}, u32[]{:S(2)}, u32[]{:S(2)}) collective-permute-start(f32[144,128]{1,0:T(8,128)S(1)} %add_add_fusion.1), channel_id=1, source_target_pairs={{0,4},{1,5},{2,6},{3,7},{4,0},{5,1},{6,2},{7,3},{8,12},{9,13},{10,... | collective-permute-start | bytes 221192 | tf_op jit(solution)/shard_map/ppermute | solution.py:449

commit v5 on v4

--- a/solution.py
+++ b/solution.py
@@ -133,6 +133,34 @@
     ref[0:rows, 0:width] = value
 
 
+def store_folded(ref, value, modes):
+    rows, width = value.shape
+    old = rows - modes
+    spare = LANES - width
+    corner, mass_corner = value[old:, :modes], value[old:, modes:]
+    row = lax.broadcasted_iota(jnp.int32, (modes, modes), 0)
+    col = lax.broadcasted_iota(jnp.int32, (modes, modes), 1)
+    both = jnp.where(row >= col, corner, mass_corner)
+    diagonal = jnp.sum(jnp.where(row == col, mass_corner, 0.0), axis=1, keepdims=True)
+    rest = jnp.zeros((modes, 2 * spare - modes - 1), F32)
+    second = jnp.concatenate([both[:, spare:], diagonal, rest], axis=1)
+    folded = jnp.concatenate([both[:, :spare], second], axis=0)
+    ref[...] = jnp.concatenate([value[:old, :], folded], axis=1)
+
+
+def unfold(value, modes):
+    width = 2 * modes
+    spare = LANES - width
+    both = jnp.concatenate([value[:modes, width:], value[modes : 2 * modes, width : width + modes - spare]], axis=1)
+    diagonal = value[modes : 2 * modes, width + modes - spare : width + modes - spare + 1]
+    row = lax.broadcasted_iota(jnp.int32, (modes, modes), 0)
+    col = lax.broadcasted_iota(jnp.int32, (modes, modes), 1)
+    turned = both.T
+    corner = jnp.where(row >= col, both, turned)
+    mass_corner = jnp.where(row < col, both, jnp.where(row > col, turned, diagonal))
+    return jnp.concatenate([value[:, :width], jnp.concatenate([corner, mass_corner], axis=1)], axis=0)
+
+
 def chosen_nodes(nodes, base, window):
     place = lax.broadcasted_iota(jnp.int32, (window, LANES), 0) + base
     parts = [(place == nodes[a : a + 1, :]).astype(F32).astype(BF16) for a in range(nodes.shape[0])]
@@ -146,43 +174,50 @@
     )
 
 
-def multiply(dims, entries, groups, picked, high, low):
+def multiply(dims, entries, groups, picked, high, low, marks, out):
     comps, modes = dims
-
-    def one(step, unused):
-        comp = step // groups
-        group = step % groups
-        totals = [jnp.zeros((modes, LANES), F32) for _ in range(4)]
-        for j in range(comps * CORNERS):
-            start = (j // CORNERS) * modes
-            value = picked[start : start + modes, (j % CORNERS) * LANES : (j % CORNERS + 1) * LANES]
+    pair = 2 * modes
+    width = groups * 2 * LANES
+    high[:pair, :] = jnp.zeros((pair, high.shape[1]), BF16)
+    low[:pair, :] = jnp.zeros((pair, low.shape[1]), BF16)
+
+    def place(comp):
+        rows = pl.ds(pl.multiple_of(comp * pair, pair), pair)
+        target = marks[:, :width]
+        out[rows, :] += dot1(high[rows, :width], target, NT) + dot1(low[rows, :width], target, NT)
+
+    def one(comp, unused):
+        place(comp)
+        for group in range(groups):
+            totals = [jnp.zeros((modes, LANES), F32) for _ in range(4)]
+            for j in range(comps * CORNERS):
+                start = (j // CORNERS) * modes
+                value = picked[start : start + modes, (j % CORNERS) * LANES : (j % CORNERS + 1) * LANES]
+                for q in range(2):
+                    for m in range(2):
+                        totals[2 * q + m] = totals[2 * q + m] + entries(comp, group, q, m, j) * value
             for q in range(2):
                 for m in range(2):
-                    totals[2 * q + m] = totals[2 * q + m] + entries(comp, group, q, m, j) * value
-        for q in range(2):
-            for m in range(2):
-                upper, lower = split(totals[2 * q + m])
-                row = pl.multiple_of((comp * 2 + m) * modes, 16)
-                col = pl.multiple_of((group * 2 + q) * LANES, LANES)
-                high[pl.ds(row, modes), pl.ds(col, LANES)] = upper
-                low[pl.ds(row, modes), pl.ds(col, LANES)] = lower
+                    upper, lower = split(totals[2 * q + m])
+                    rows = pl.ds(pl.multiple_of((comp + 1) * pair + m * modes, 16), modes)
+                    lanes = slice((group * 2 + q) * LANES, (group * 2 + q + 1) * LANES)
+                    high[rows, lanes] = upper
+                    low[rows, lanes] = lower
         return unused
 
-    lax.fori_loop(0, comps * groups, one, 0, unroll=2)
-
-
-def place_sums(high, low, target):
-    return dot1(high, target, NT) + dot1(low, target, NT)
-
-
-def all_products(dims, ext, stiffness, mass, edges, connect, edge_nodes, picked, high, low, out):
+    lax.fori_loop(0, comps, one, 0)
+    place(comps)
+
+
+def all_products(dims, ext, stiffness, mass, edges, connect, edge_nodes, picked, high, low, marks, out):
     halves = split(ext)
-    own_products(dims, halves, stiffness, mass, connect, picked, high, low, out)
-    edge_products(dims, halves, edges, edge_nodes, picked, high, low, out)
-
-
-def own_products(dims, halves, stiffness, mass, connect, picked, high, low, out):
+    own_products(dims, halves, stiffness, mass, connect, picked, high, low, marks, out)
+    edge_products(dims, halves, edges, edge_nodes, picked, high, low, marks, out)
+
+
+def own_products(dims, halves, stiffness, mass, connect, picked, high, low, marks, out):
     own_nodes = connect[...] + (LANES - HALO)
+    out[...] = jnp.zeros(out.shape, F32)
     for number in range(2):
         lane = number * LANES
         chosen = chosen_nodes(own_nodes[:, lane : lane + LANES], lane, 3 * LANES)
@@ -192,25 +227,24 @@
             matrix = mass if m else stiffness
             return matrix[comp * CORNERS + group * 2 + q, j : j + 1, lane : lane + LANES]
 
-        multiply(dims, entries, CORNERS // 2, picked, high, low)
-        total = place_sums(high[...], low[...], chosen[LANES - lane : 3 * LANES - lane, :])
-        if number == 0:
-            out[...] = total
-        else:
-            out[...] += total
-
-
-def edge_products(dims, halves, edges, edge_nodes, picked, high, low, out):
+        marks[...] = chosen[LANES - lane : 3 * LANES - lane, :]
+        multiply(dims, entries, CORNERS // 2, picked, high, low, marks, out)
+
+
+def edge_products(dims, halves, edges, edge_nodes, picked, high, low, marks, out):
     comps, _ = dims
     nodes = edge_nodes[...]
     pick(halves, chosen_nodes(nodes[:CORNERS], 0, 4 * LANES), 0, picked)
-    multiply(dims, lambda comp, group, q, m, j: edges[m, q * comps + comp, j : j + 1, :], 1, picked, high, low)
     first = lax.broadcasted_iota(jnp.int32, (1, LANES), 1) < HALO
     reached = jnp.concatenate(
         [jnp.where(first, nodes[3:4], nodes[2:3]), jnp.where(first, nodes[1:2], -1)], axis=0
     )
-    target = chosen_nodes(reached, LANES, 2 * LANES)
-    out[...] += place_sums(high[:, : 2 * LANES], low[:, : 2 * LANES], target)
+    marks[:, : 2 * LANES] = chosen_nodes(reached, LANES, 2 * LANES)
+    multiply(
+        dims,
+        lambda comp, group, q, m, j: edges[m, q * comps + comp, j : j + 1, :],
+        1, picked, high, low, marks, out,
+    )
 
 
 def grams(basis, products, dims):
@@ -287,24 +321,24 @@
     by_side(lambda: put(side_b, side_a), lambda: put(side_a, side_b))
 
 
-def first_kernel(dims, block, connect, stiffness, mass, from_a, from_b, ext, out, picked, high, low, sems):
+def first_kernel(dims, block, connect, stiffness, mass, from_a, from_b, ext, sums, picked, high, low, marks, sems):
     below, above = ext.at[:, :LANES], ext.at[:, 3 * LANES :]
     copies = start_sides(from_a, from_b, below, above, sems, 0)
     ext[:, LANES : 3 * LANES] = block[...]
     for copy in copies:
         copy.wait()
-    own_products(dims, split(ext[...]), stiffness, mass, connect, picked, high, low, out)
-
-
-def edge_kernel(dims, block, connect, ext, part, from_a, from_b, edges, edge_nodes, side_a, side_b, gram, picked, high, low, out, below, above, sems):
-    comps, _ = dims
+    own_products(dims, split(ext[...]), stiffness, mass, connect, picked, high, low, marks, sums)
+
+
+def edge_kernel(dims, block, connect, ext, part, from_a, from_b, edges, edge_nodes, side_a, side_b, gram, picked, high, low, marks, sums, below, above, sems):
+    comps, modes = dims
     size = comps * CORNERS
     rows = comps * size
     top = 2 * rows
     copies = start_sides(from_a, from_b, below, above, sems, 0)
     first = lax.broadcasted_iota(jnp.int32, (rows, LANES), 1) < HALO
     halves = split(ext[...])
-    out[...] = part[...]
+    sums[...] = part[...]
     for copy in copies:
         copy.wait()
     for slot in range(2):
@@ -318,12 +352,13 @@
     before = below[top:, :] + (LANES - HALO - count)
     after = pltpu.roll(above[top:, :], HALO, 1) + (LANES - HALO + count)
     edge_nodes[...] = jnp.where(first[:SUB], before, after).astype(jnp.int32)
-    edge_products(dims, halves, edges, edge_nodes, picked, high, low, out)
+    edge_products(dims, halves, edges, edge_nodes, picked, high, low, marks, sums)
+    out = sums.at[2 * modes :, :]
     store_sides(out, side_a, side_b)
     store_lanes(gram, grams([block[...]], out[...], dims))
 
 
-def second_kernel(dims, gram_in, connect, edge_nodes, block, stiffness, mass, edges, from_a, from_b, own_a, own_b, residual, side_a, side_b, gram, state, picked, high, low, out, below, above, lower, upper, sems):
+def second_kernel(dims, gram_in, connect, edge_nodes, block, stiffness, mass, edges, from_a, from_b, own_a, own_b, residual, side_a, side_b, gram, state, picked, high, low, marks, sums, below, above, lower, upper, sems):
     comps, modes = dims
     tiles = (below, lower, upper, above)
     copies = start_sides(from_a, from_b, below, above, sems, 0)
@@ -351,7 +386,8 @@
         )
     ext = jnp.concatenate(pieces, axis=0)
     residual[...] = ext[:, LANES : 3 * LANES]
-    all_products(dims, ext, stiffness, mass, edges, connect, edge_nodes, picked, high, low, out)
+    all_products(dims, ext, stiffness, mass, edges, connect, edge_nodes, picked, high, low, marks, sums)
+    out = sums.at[2 * modes :, :]
     store_sides(out, side_a, side_b)
     store_lanes(gram, grams([block[...], residual[...]], out[...], dims))
 
@@ -396,7 +432,7 @@
     return coeff, half, root, solver, mass_all
 
 
-def third_kernel(dims, gram_in, state_in, connect, edge_nodes, block, residual, stiffness, mass, edges, from_a, from_b, own_a, own_b, more_a, more_b, new_a, new_b, new, gram, coeff_out, state, picked, high, low, out, below, above, lower, upper, new_below, new_above, new_lower, new_upper, sems):
+def third_kernel(dims, gram_in, state_in, connect, edge_nodes, block, residual, stiffness, mass, edges, from_a, from_b, own_a, own_b, more_a, more_b, new_a, new_b, new, gram, coeff_out, state, picked, high, low, marks, sums, below, above, lower, upper, new_below, new_above, new_lower, new_upper, sems):
     comps, modes = dims
     tiles = ((below, new_below), (lower, new_lower), (upper, new_upper), (above, new_above))
     copies = start_sides(from_a, from_b, below, above, sems, 0)
@@ -423,13 +459,14 @@
         pieces.append(dot1(mixed_high, right_high, NN) + (dot1(mixed_high, right_low, NN) + dot1(mixed_low, right_high, NN)))
     ext = jnp.concatenate(pieces, axis=0)
     new[...] = ext[:, LANES : 3 * LANES]
-    all_products(dims, ext, stiffness, mass, edges, connect, edge_nodes, picked, high, low, out)
-    store_lanes(gram, grams([block[...], residual[...], new[...]], out[...], dims))
+    all_products(dims, ext, stiffness, mass, edges, connect, edge_nodes, picked, high, low, marks, sums)
+    out = sums.at[2 * modes :, :]
+    store_folded(gram, grams([block[...], residual[...], new[...]], out[...], dims), modes)
 
 
 def last_kernel(dims, gram_in, coeff_in, state_in, block, residual, new, modes_out, ritz_out):
     comps, modes = dims
-    coeff, half, root, _, _ = small_step(gram_in[...], state_in[0], state_in[1], coeff_in[...], modes)
+    coeff, half, root, _, _ = small_step(unfold(gram_in[...], modes), state_in[0], state_in[1], coeff_in[...], modes)
     ritz_out[...] = jnp.sum(dotf(half, root, NT) * eye(modes), axis=0, keepdims=True)
     coeff_high, coeff_low = split(coeff)
     for c in range(comps):
@@ -500,9 +537,10 @@
     rows = comps * modes
     work = [
         pltpu.VMEM((rows, CORNERS * LANES), F32),
-        pltpu.VMEM((2 * rows, CORNERS * LANES), BF16),
-        pltpu.VMEM((2 * rows, CORNERS * LANES), BF16),
-        pltpu.VMEM((2 * rows, count), F32),
+        pltpu.VMEM((2 * rows + 2 * modes, CORNERS * LANES), BF16),
+        pltpu.VMEM((2 * rows + 2 * modes, CORNERS * LANES), BF16),
+        pltpu.VMEM((count, CORNERS * LANES), BF16),
+        pltpu.VMEM((2 * rows + 2 * modes, count), F32),
     ]
     near, far = pltpu.VMEM, jax.ShapeDtypeStruct
     wide = (near, (rows, count), F32)
@@ -526,8 +564,8 @@
     ext, part = call(
         first_kernel,
         dims,
-        [(near, (rows, 2 * count), F32), (near, (2 * rows, count), F32)],
-        work[:3] + [sems((2,))],
+        [(near, (rows, 2 * count), F32), (near, (2 * rows + 2 * modes, count), F32)],
+        work[:4] + [sems((2,))],
         (block, link, stiff_near, mass_near, *node_from),
         (),
     )
@@ -556,7 +594,7 @@
     new, gram, coeff, state = call(
         third_kernel,
         dims,
-        [wide, (near, (3 * modes, LANES), F32), (near, (modes, 2 * modes), F32), (near, (2, 2 * modes, 2 * modes), F32)],
+        [wide, (near, (2 * modes, LANES), F32), (near, (modes, 2 * modes), F32), (near, (2, 2 * modes, 2 * modes), F32)],
         work + room(*p, *q) + [sems((8,))],
         (gram, state, link, edge_nodes, block, residual, stiff_near, mass_near, edges, *p, *q),
         (),

time: 107 us -> 105 us (0.981)
  waiting for transfers between devices: 23.3 us -> 21 us
    ppermute x18, waiting for transfers between devices: 23 us -> 20.7 us  [from_partner(): return lax.ppermute(part, axis, [(i, i ^ bits) for i in range(count)])]
where the time goes in v5:
time: 105 us
  Pallas kernels  48.8 us (46%)
  starting transfers between devices  34.1 us (32%)
  waiting for transfers between devices  21 us (20%)
    pallas_call x7, Pallas kernels, call(): pl.pallas_call(functools.partial(kernel, dims), out_shape=shapes, in_spec...  48.8 us
    ppermute x18, starting transfers between devices, from_partner(): return lax.ppermute(part, axis, [(i, i ^ bits) for i in range(count)])  26.5 us
    ppermute x18, waiting for transfers between devices, from_partner(): return lax.ppermute(part, axis, [(i, i ^ bits) for i in range(count)])  20.7 us
    ppermute x8, starting transfers between devices, swap(): return lax.ppermute(value, axis, pairs + [(b, a) for a, b in pairs])  7.63 us
  transfers between devices with their start and end apart: 26, of which 11 were waited for; matrix products, arithmetic and copies ran while one was open for 0% of the time, Pallas kernels for 7%

profile of v5, /device:TPU:0, one launch (start us, length us, event | category | flops | bytes accessed | tf_op | source)
XLA Modules:
  0.0 104.9 jit_solution(16560001126159739788)
XLA Ops:
  0.6 1.4 %shard_map.60 = (s32[4,256]{1,0:T(4,128)S(1)}, f32[24,24,256]{2,1,0:T(8,128)S(1)}, f32[24,24,256]{2,1,0:T(8,128)S(1)}, f32[296,128]{1,0:T(8,128)S(1)}, f32[296,128]{1,0:T(8,128)S(1)}) custom-call(s32[4,256]{1,0:T(4,128)} %connect_in.1, f32[24,24,256]{2,1,0:T(8,128)} %stiff_in.1, f32[24,24,256]{2,1,0:T(8,128)} %mass_in.1), custom_call_target="tpu_custom_call" | custom-call | tf_op jit(solution)/shard_map/pallas_call | solution.py:519
  2.1 0.6 collective-permute-start.2
  2.6 0.7 collective-permute-start.3
  3.3 1.0 shard_map.59
  4.3 3.9 %collective-permute-start = (f32[288,128]{1,0:T(8,128)S(1)}, f32[288,128]{1,0:T(8,128)S(1)}, u32[]{:S(2)}, u32[]{:S(2)}) collective-permute-start(f32[288,128]{1,0:T(8,128)S(1)} %get-tuple-element.32), channel_id=1, source_target_pairs={{0,1},{2,3},{4,5},{6,7},{8,9},{10,11},{12,13},{14,15},{1,0},{3,2},... | collective-permute-start | bytes 442376 | tf_op jit(solution)/shard_map/ppermute | solution.py:505
  8.2 0.7 collective-permute-start.1
  8.9 0.3 collective-permute-done.from_a
  9.2 0.0 collective-permute-done.1.from_b
  9.2 6.6 %shard_map.61 = (f32[288,512]{1,0:T(8,128)S(1)}, f32[672,256]{1,0:T(8,128)S(1)}) custom-call(f32[288,256]{1,0:T(8,128)S(1)} %get-tuple-element.28.block, s32[4,256]{1,0:T(4,128)S(1)} %get-tuple-element.29.connect, f32[24,24,256]{2,1,0:T(8,128)S(1)} %get-tuple-element.30.stiffness, f32[24,24,256]{2,1,0:T(8,128)S(1)} %get-tuple-element.31.mass, ...), custom_call_target="tpu_custom_call" | custom-call | tf_op jit(solution)/shard_map/pallas_call | solution.py:519
  15.8 0.0 collective-permute-done.2.from_a
  15.9 0.0 collective-permute-done.3.from_b
  15.9 3.3 %shard_map.62 = (f32[2,12,24,128]{3,2,1,0:T(8,128)S(1)}, s32[8,128]{1,0:T(8,128)S(1)}, f32[576,128]{1,0:T(8,128)S(1)}, f32[576,128]{1,0:T(8,128)S(1)}, f32[48,128]{1,0:T(8,128)S(1)}) custom-call(f32[288,256]{1,0:T(8,128)S(1)} %get-tuple-element.28.block, s32[4,256]{1,0:T(4,128)S(1)} %get-tuple-element.29.connect, f32[288,512]{1,0:T(8,128)S(1)} %get-tuple-element.34.ext, ...), custom_call_target="tpu_custom_call" | custom-call | tf_op jit(solution)/shard_map/pallas_call | solution.py:519
  19.2 7.7 %collective-permute-start.6 = (f32[48,128]{1,0:T(8,128)S(1)}, f32[48,128]{1,0:T(8,128)S(1)}, u32[]{:S(2)}, u32[]{:S(2)}) collective-permute-start(f32[48,128]{1,0:T(8,128)S(1)} %get-tuple-element.38), channel_id=1, source_target_pairs={{0,3},{1,2},{2,1},{3,0},{4,7},{5,6},{6,5},{7,4},{8,11},{9,10},{10,... | collective-permute-start | bytes 73736 | tf_op jit(solution)/shard_map/ppermute | solution.py:486
  26.9 1.0 collective-permute-start.5
  27.9 0.0 collective-permute-start.4
  27.9 0.5 collective-permute-start.10
  28.4 0.7 collective-permute-start.11
  29.1 0.0 collective-permute-done.6
  29.1 1.8 %collective-permute-done.5 = f32[48,128]{1,0:T(8,128)S(1)} collective-permute-done((f32[48,128]{1,0:T(8,128)S(1)}, f32[48,128]{1,0:T(8,128)S(1)}, u32[]{:S(2)}, u32[]{:S(2)}) %collective-permute-start.5) | collective-permute-done | bytes 24608 | tf_op jit(solution)/shard_map/ppermute | solution.py:486
  30.9 0.0 collective-permute-done.4
  30.9 4.4 %collective-permute-start.9 = (f32[48,128]{1,0:T(8,128)S(1)}, f32[48,128]{1,0:T(8,128)S(1)}, u32[]{:S(2)}, u32[]{:S(2)}) collective-permute-start(f32[48,128]{1,0:T(8,128)S(1)} %add_add_fusion.5), channel_id=1, source_target_pairs={{0,12},{1,13},{2,14},{3,15},{4,8},{5,9},{6,10},{7,11},{8,4},{9,5},... | collective-permute-start | bytes 73736 | tf_op jit(solution)/shard_map/ppermute | solution.py:486
  35.3 0.0 collective-permute-start.8
  35.3 0.6 collective-permute-start.7
  35.9 4.7 %collective-permute-done.9 = f32[48,128]{1,0:T(8,128)S(1)} collective-permute-done((f32[48,128]{1,0:T(8,128)S(1)}, f32[48,128]{1,0:T(8,128)S(1)}, u32[]{:S(2)}, u32[]{:S(2)}) %collective-permute-start.9) | collective-permute-done | bytes 24608 | tf_op jit(solution)/shard_map/ppermute | solution.py:486
  40.7 0.0 collective-permute-done.8
  40.7 0.0 collective-permute-done.7
  40.7 0.0 collective-permute-done.10.from_a
  40.7 0.0 collective-permute-done.11.from_b
  40.7 12.4 %shard_map.63 = (f32[288,256]{1,0:T(8,128)S(1)}, f32[576,128]{1,0:T(8,128)S(1)}, f32[576,128]{1,0:T(8,128)S(1)}, f32[96,128]{1,0:T(8,128)S(1)}, f32[3,48,48]{2,1,0:T(8,128)S(1)}) custom-call(f32[48,128]{1,0:T(8,128)S(1)} %add_add_fusion.4.gram_in, s32[4,256]{1,0:T(4,128)S(1)} %get-tuple-element.29.connect, s32[8,128]{1,0:T(8,128)S(1)} %get-tuple-element.39.edge_nodes, ...), custom_call_target="tpu_custom_call" | custom-call | tf_op jit(solution)/shard_map/pallas_call | solution.py:519
  53.1 0.1 collective-permute-start.14
  53.2 0.2 collective-permute-start.13
  53.4 1.6 %collective-permute-start.12 = (f32[96,128]{1,0:T(8,128)S(1)}, f32[96,128]{1,0:T(8,128)S(1)}, u32[]{:S(2)}, u32[]{:S(2)}) collective-permute-start(f32[96,128]{1,0:T(8,128)S(1)} %get-tuple-element.43), channel_id=1, source_target_pairs={{0,1},{1,0},{2,3},{3,2},{4,5},{5,4},{6,7},{7,6},{8,9},{9,8},{10,11... | collective-permute-start | bytes 147464 | tf_op jit(solution)/shard_map/ppermute | solution.py:486
  55.0 0.0 collective-permute-start.18
  55.0 0.7 collective-permute-start.19
  55.7 1.0 collective-permute-done.14
  56.7 1.1 %collective-permute-done.13 = f32[96,128]{1,0:T(8,128)S(1)} collective-permute-done((f32[96,128]{1,0:T(8,128)S(1)}, f32[96,128]{1,0:T(8,128)S(1)}, u32[]{:S(2)}, u32[]{:S(2)}) %collective-permute-start.13) | collective-permute-done | bytes 49184 | tf_op jit(solution)/shard_map/ppermute | solution.py:486
  57.7 0.0 collective-permute-done.12
  57.8 3.1 %collective-permute-start.17 = (f32[96,128]{1,0:T(8,128)S(1)}, f32[96,128]{1,0:T(8,128)S(1)}, u32[]{:S(2)}, u32[]{:S(2)}) collective-permute-start(f32[96,128]{1,0:T(8,128)S(1)} %add_add_fusion.3), channel_id=1, source_target_pairs={{0,12},{1,13},{2,14},{3,15},{4,8},{5,9},{6,10},{7,11},{8,4},{9,5},... | collective-permute-start | bytes 147464 | tf_op jit(solution)/shard_map/ppermute | solution.py:486
  60.8 0.0 collective-permute-start.16
  60.8 1.4 %collective-permute-start.15 = (f32[96,128]{1,0:T(8,128)S(1)}, f32[96,128]{1,0:T(8,128)S(1)}, u32[]{:S(2)}, u32[]{:S(2)}) collective-permute-start(f32[96,128]{1,0:T(8,128)S(1)} %add_add_fusion.3), channel_id=1, source_target_pairs={{0,4},{1,5},{2,6},{3,7},{4,0},{5,1},{6,2},{7,3},{8,12},{9,13},{10,... | collective-permute-start | bytes 147464 | tf_op jit(solution)/shard_map/ppermute | solution.py:486
  62.2 5.4 %collective-permute-done.17 = f32[96,128]{1,0:T(8,128)S(1)} collective-permute-done((f32[96,128]{1,0:T(8,128)S(1)}, f32[96,128]{1,0:T(8,128)S(1)}, u32[]{:S(2)}, u32[]{:S(2)}) %collective-permute-start.17) | collective-permute-done | bytes 49184 | tf_op jit(solution)/shard_map/ppermute | solution.py:486
  67.6 0.9 collective-permute-done.16
  68.4 0.0 collective-permute-done.15
  68.5 0.0 collective-permute-done.18.more_a
  68.5 0.0 collective-permute-done.19.more_b
  68.5 16.7 %shard_map.64 = (f32[288,256]{1,0:T(8,128)S(1)}, f32[96,128]{1,0:T(8,128)S(1)}, f32[48,96]{1,0:T(8,128)S(1)}, f32[2,96,96]{2,1,0:T(8,128)S(1)}) custom-call(f32[96,128]{1,0:T(8,128)S(1)} %add_add_fusion.2.gram_in, f32[3,48,48]{2,1,0:T(8,128)S(1)} %get-tuple-element.44.state_in, s32[4,256]{1,0:T(4,128)S(1)} %get-tuple-element.29.connect, ...), custom_call_target="tpu_custom_call" | custom-call | tf_op jit(solution)/shard_map/pallas_call | solution.py:519
  85.2 0.1 collective-permute-start.22
  85.2 0.1 collective-permute-start.21
  85.3 1.8 %collective-permute-start.20 = (f32[96,128]{1,0:T(8,128)S(1)}, f32[96,128]{1,0:T(8,128)S(1)}, u32[]{:S(2)}, u32[]{:S(2)}) collective-permute-start(f32[96,128]{1,0:T(8,128)S(1)} %get-tuple-element.48), channel_id=1, source_target_pairs={{0,1},{1,0},{2,3},{3,2},{4,5},{5,4},{6,7},{7,6},{8,9},{9,8},{10,11... | collective-permute-start | bytes 147464 | tf_op jit(solution)/shard_map/ppermute | solution.py:486
  87.1 1.7 %collective-permute-done.22 = f32[96,128]{1,0:T(8,128)S(1)} collective-permute-done((f32[96,128]{1,0:T(8,128)S(1)}, f32[96,128]{1,0:T(8,128)S(1)}, u32[]{:S(2)}, u32[]{:S(2)}) %collective-permute-start.22) | collective-permute-done | bytes 49184 | tf_op jit(solution)/shard_map/ppermute | solution.py:486
  88.7 1.1 %collective-permute-done.21 = f32[96,128]{1,0:T(8,128)S(1)} collective-permute-done((f32[96,128]{1,0:T(8,128)S(1)}, f32[96,128]{1,0:T(8,128)S(1)}, u32[]{:S(2)}, u32[]{:S(2)}) %collective-permute-start.21) | collective-permute-done | bytes 49184 | tf_op jit(solution)/shard_map/ppermute | solution.py:486
  89.8 0.0 collective-permute-done.20
  89.8 2.4 %collective-permute-start.25 = (f32[96,128]{1,0:T(8,128)S(1)}, f32[96,128]{1,0:T(8,128)S(1)}, u32[]{:S(2)}, u32[]{:S(2)}) collective-permute-start(f32[96,128]{1,0:T(8,128)S(1)} %add_add_fusion.1), channel_id=1, source_target_pairs={{0,12},{1,13},{2,14},{3,15},{4,8},{5,9},{6,10},{7,11},{8,4},{9,5},... | collective-permute-start | bytes 147464 | tf_op jit(solution)/shard_map/ppermute | solution.py:486
  92.2 0.0 collective-permute-start.24
  92.2 2.1 %collective-permute-start.23 = (f32[96,128]{1,0:T(8,128)S(1)}, f32[96,128]{1,0:T(8,128)S(1)}, u32[]{:S(2)}, u32[]{:S(2)}) collective-permute-start(f32[96,128]{1,0:T(8,128)S(1)} %add_add_fusion.1), channel_id=1, source_target_pairs={{0,4},{1,5},{2,6},{3,7},{4,0},{5,1},{6,2},{7,3},{8,12},{9,13},{10,... | collective-permute-start | bytes 147464 | tf_op jit(solution)/shard_map/ppermute | solution.py:486
  94.3 2.0 %collective-permute-done.25 = f32[96,128]{1,0:T(8,128)S(1)} collective-permute-done((f32[96,128]{1,0:T(8,128)S(1)}, f32[96,128]{1,0:T(8,128)S(1)}, u32[]{:S(2)}, u32[]{:S(2)}) %collective-permute-start.25) | collective-permute-done | bytes 49184 | tf_op jit(solution)/shard_map/ppermute | solution.py:486
  96.3 1.1 %collective-permute-done.24 = f32[96,128]{1,0:T(8,128)S(1)} collective-permute-done((f32[96,128]{1,0:T(8,128)S(1)}, f32[96,128]{1,0:T(8,128)S(1)}, u32[]{:S(2)}, u32[]{:S(2)}) %collective-permute-start.24) | collective-permute-done | bytes 49184 | tf_op jit(solution)/shard_map/ppermute | solution.py:486
  97.5 0.0 collective-permute-done.23
  97.5 7.4 %shard_map.65 = (f32[288,256]{1,0:T(8,128)}, f32[1,48]{1,0:T(1,128)}) custom-call(f32[96,128]{1,0:T(8,128)S(1)} %add_add_fusion.gram_in, f32[48,96]{1,0:T(8,128)S(1)} %get-tuple-element.49.coeff_in, f32[2,96,96]{2,1,0:T(8,128)S(1)} %get-tuple-element.50.state_in, f32[288,256]{1,0:T(8,128)S(1)} %get-tuple-element.28.block, ...), custom_call_target="tpu_custom_call" | custom-call | tf_op jit(solution)/shard_map/pallas_call | solution.py:519
  (6 shorter events, 0.1 us)
Async XLA Ops:
  2.1 13.8 %collective-permute-start.2 = (f32[296,128]{1,0:T(8,128)S(1)}, f32[296,128]{1,0:T(8,128)S(1)}, u32[]{:S(2)}, u32[]{:S(2)}) collective-permute-start(f32[296,128]{1,0:T(8,128)S(1)} %get-tuple-element.36), channel_id=1, source_target_pairs={{0,1},{2,3},{4,5},{6,7},{8,9},{10,11},{12,13},{14,15},{1,0},{3,2},... | collective-permute-start | bytes 454664 | tf_op jit(solution)/shard_map/ppermute | solution.py:505
  2.6 13.2 %collective-permute-start.3 = (f32[296,128]{1,0:T(8,128)S(1)}, f32[296,128]{1,0:T(8,128)S(1)}, u32[]{:S(2)}, u32[]{:S(2)}) collective-permute-start(f32[296,128]{1,0:T(8,128)S(1)} %get-tuple-element.37), channel_id=1, source_target_pairs={{1,2},{3,4},{5,6},{7,8},{9,10},{11,12},{13,14},{2,1},{4,3},{6,5},{... | collective-permute-start | bytes 454664 | tf_op jit(solution)/shard_map/ppermute | solution.py:505
  4.3 5.0 %collective-permute-start = (f32[288,128]{1,0:T(8,128)S(1)}, f32[288,128]{1,0:T(8,128)S(1)}, u32[]{:S(2)}, u32[]{:S(2)}) collective-permute-start(f32[288,128]{1,0:T(8,128)S(1)} %get-tuple-element.32), channel_id=1, source_target_pairs={{0,1},{2,3},{4,5},{6,7},{8,9},{10,11},{12,13},{14,15},{1,0},{3,2},... | collective-permute-start | bytes 442376 | tf_op jit(solution)/shard_map/ppermute | solution.py:505
  8.2 1.0 collective-permute-start.1
  19.2 9.9 %collective-permute-start.6 = (f32[48,128]{1,0:T(8,128)S(1)}, f32[48,128]{1,0:T(8,128)S(1)}, u32[]{:S(2)}, u32[]{:S(2)}) collective-permute-start(f32[48,128]{1,0:T(8,128)S(1)} %get-tuple-element.38), channel_id=1, source_target_pairs={{0,3},{1,2},{2,1},{3,0},{4,7},{5,6},{6,5},{7,4},{8,11},{9,10},{10,... | collective-permute-start | bytes 73736 | tf_op jit(solution)/shard_map/ppermute | solution.py:486
  26.9 4.0 %collective-permute-start.5 = (f32[48,128]{1,0:T(8,128)S(1)}, f32[48,128]{1,0:T(8,128)S(1)}, u32[]{:S(2)}, u32[]{:S(2)}) collective-permute-start(f32[48,128]{1,0:T(8,128)S(1)} %get-tuple-element.38), channel_id=1, source_target_pairs={{0,2},{1,3},{2,0},{3,1},{4,6},{5,7},{6,4},{7,5},{8,10},{9,11},{10,... | collective-permute-start | bytes 73736 | tf_op jit(solution)/shard_map/ppermute | solution.py:486
  27.9 3.0 %collective-permute-start.4 = (f32[48,128]{1,0:T(8,128)S(1)}, f32[48,128]{1,0:T(8,128)S(1)}, u32[]{:S(2)}, u32[]{:S(2)}) collective-permute-start(f32[48,128]{1,0:T(8,128)S(1)} %get-tuple-element.38), channel_id=1, source_target_pairs={{0,1},{1,0},{2,3},{3,2},{4,5},{5,4},{6,7},{7,6},{8,9},{9,8},{10,11... | collective-permute-start | bytes 73736 | tf_op jit(solution)/shard_map/ppermute | solution.py:486
  27.9 12.7 %collective-permute-start.10 = (f32[576,128]{1,0:T(8,128)S(1)}, f32[576,128]{1,0:T(8,128)S(1)}, u32[]{:S(2)}, u32[]{:S(2)}) collective-permute-start(f32[576,128]{1,0:T(8,128)S(1)} %get-tuple-element.41.own_a), channel_id=1, source_target_pairs={{0,1},{2,3},{4,5},{6,7},{8,9},{10,11},{12,13},{14,15},{1,0},{3,2},... | collective-permute-start | bytes 884744 | tf_op jit(solution)/shard_map/ppermute | solution.py:505
  28.4 12.3 %collective-permute-start.11 = (f32[576,128]{1,0:T(8,128)S(1)}, f32[576,128]{1,0:T(8,128)S(1)}, u32[]{:S(2)}, u32[]{:S(2)}) collective-permute-start(f32[576,128]{1,0:T(8,128)S(1)} %get-tuple-element.42.own_b), channel_id=1, source_target_pairs={{1,2},{3,4},{5,6},{7,8},{9,10},{11,12},{13,14},{2,1},{4,3},{6,5},{... | collective-permute-start | bytes 884744 | tf_op jit(solution)/shard_map/ppermute | solution.py:505
  30.9 9.7 %collective-permute-start.9 = (f32[48,128]{1,0:T(8,128)S(1)}, f32[48,128]{1,0:T(8,128)S(1)}, u32[]{:S(2)}, u32[]{:S(2)}) collective-permute-start(f32[48,128]{1,0:T(8,128)S(1)} %add_add_fusion.5), channel_id=1, source_target_pairs={{0,12},{1,13},{2,14},{3,15},{4,8},{5,9},{6,10},{7,11},{8,4},{9,5},... | collective-permute-start | bytes 73736 | tf_op jit(solution)/shard_map/ppermute | solution.py:486
  35.3 5.4 %collective-permute-start.8 = (f32[48,128]{1,0:T(8,128)S(1)}, f32[48,128]{1,0:T(8,128)S(1)}, u32[]{:S(2)}, u32[]{:S(2)}) collective-permute-start(f32[48,128]{1,0:T(8,128)S(1)} %add_add_fusion.5), channel_id=1, source_target_pairs={{0,8},{1,9},{2,10},{3,11},{4,12},{5,13},{6,14},{7,15},{8,0},{9,1},... | collective-permute-start | bytes 73736 | tf_op jit(solution)/shard_map/ppermute | solution.py:486
  35.3 5.4 %collective-permute-start.7 = (f32[48,128]{1,0:T(8,128)S(1)}, f32[48,128]{1,0:T(8,128)S(1)}, u32[]{:S(2)}, u32[]{:S(2)}) collective-permute-start(f32[48,128]{1,0:T(8,128)S(1)} %add_add_fusion.5), channel_id=1, source_target_pairs={{0,4},{1,5},{2,6},{3,7},{4,0},{5,1},{6,2},{7,3},{8,12},{9,13},{10,... | collective-permute-start | bytes 73736 | tf_op jit(solution)/shard_map/ppermute | solution.py:486
  53.1 3.6 %collective-permute-start.14 = (f32[96,128]{1,0:T(8,128)S(1)}, f32[96,128]{1,0:T(8,128)S(1)}, u32[]{:S(2)}, u32[]{:S(2)}) collective-permute-start(f32[96,128]{1,0:T(8,128)S(1)} %get-tuple-element.43), channel_id=1, source_target_pairs={{0,3},{1,2},{2,1},{3,0},{4,7},{5,6},{6,5},{7,4},{8,11},{9,10},{10,... | collective-permute-start | bytes 147464 | tf_op jit(solution)/shard_map/ppermute | solution.py:486
  53.2 4.6 %collective-permute-start.13 = (f32[96,128]{1,0:T(8,128)S(1)}, f32[96,128]{1,0:T(8,128)S(1)}, u32[]{:S(2)}, u32[]{:S(2)}) collective-permute-start(f32[96,128]{1,0:T(8,128)S(1)} %get-tuple-element.43), channel_id=1, source_target_pairs={{0,2},{1,3},{2,0},{3,1},{4,6},{5,7},{6,4},{7,5},{8,10},{9,11},{10,... | collective-permute-start | bytes 147464 | tf_op jit(solution)/shard_map/ppermute | solution.py:486
  53.4 4.3 %collective-permute-start.12 = (f32[96,128]{1,0:T(8,128)S(1)}, f32[96,128]{1,0:T(8,128)S(1)}, u32[]{:S(2)}, u32[]{:S(2)}) collective-permute-start(f32[96,128]{1,0:T(8,128)S(1)} %get-tuple-element.43), channel_id=1, source_target_pairs={{0,1},{1,0},{2,3},{3,2},{4,5},{5,4},{6,7},{7,6},{8,9},{9,8},{10,11... | collective-permute-start | bytes 147464 | tf_op jit(solution)/shard_map/ppermute | solution.py:486
  55.0 13.4 %collective-permute-start.18 = (f32[576,128]{1,0:T(8,128)S(1)}, f32[576,128]{1,0:T(8,128)S(1)}, u32[]{:S(2)}, u32[]{:S(2)}) collective-permute-start(f32[576,128]{1,0:T(8,128)S(1)} %get-tuple-element.46.new_a), channel_id=1, source_target_pairs={{0,1},{2,3},{4,5},{6,7},{8,9},{10,11},{12,13},{14,15},{1,0},{3,2},... | collective-permute-start | bytes 884744 | tf_op jit(solution)/shard_map/ppermute | solution.py:505
  55.0 13.4 %collective-permute-start.19 = (f32[576,128]{1,0:T(8,128)S(1)}, f32[576,128]{1,0:T(8,128)S(1)}, u32[]{:S(2)}, u32[]{:S(2)}) collective-permute-start(f32[576,128]{1,0:T(8,128)S(1)} %get-tuple-element.47.new_b), channel_id=1, source_target_pairs={{1,2},{3,4},{5,6},{7,8},{9,10},{11,12},{13,14},{2,1},{4,3},{6,5},{... | collective-permute-start | bytes 884744 | tf_op jit(solution)/shard_map/ppermute | solution.py:505
  57.8 9.8 %collective-permute-start.17 = (f32[96,128]{1,0:T(8,128)S(1)}, f32[96,128]{1,0:T(8,128)S(1)}, u32[]{:S(2)}, u32[]{:S(2)}) collective-permute-start(f32[96,128]{1,0:T(8,128)S(1)} %add_add_fusion.3), channel_id=1, source_target_pairs={{0,12},{1,13},{2,14},{3,15},{4,8},{5,9},{6,10},{7,11},{8,4},{9,5},... | collective-permute-start | bytes 147464 | tf_op jit(solution)/shard_map/ppermute | solution.py:486
  60.8 7.6 %collective-permute-start.16 = (f32[96,128]{1,0:T(8,128)S(1)}, f32[96,128]{1,0:T(8,128)S(1)}, u32[]{:S(2)}, u32[]{:S(2)}) collective-permute-start(f32[96,128]{1,0:T(8,128)S(1)} %add_add_fusion.3), channel_id=1, source_target_pairs={{0,8},{1,9},{2,10},{3,11},{4,12},{5,13},{6,14},{7,15},{8,0},{9,1},... | collective-permute-start | bytes 147464 | tf_op jit(solution)/shard_map/ppermute | solution.py:486
  60.8 7.6 %collective-permute-start.15 = (f32[96,128]{1,0:T(8,128)S(1)}, f32[96,128]{1,0:T(8,128)S(1)}, u32[]{:S(2)}, u32[]{:S(2)}) collective-permute-start(f32[96,128]{1,0:T(8,128)S(1)} %add_add_fusion.3), channel_id=1, source_target_pairs={{0,4},{1,5},{2,6},{3,7},{4,0},{5,1},{6,2},{7,3},{8,12},{9,13},{10,... | collective-permute-start | bytes 147464 | tf_op jit(solution)/shard_map/ppermute | solution.py:486
  85.2 3.6 %collective-permute-start.22 = (f32[96,128]{1,0:T(8,128)S(1)}, f32[96,128]{1,0:T(8,128)S(1)}, u32[]{:S(2)}, u32[]{:S(2)}) collective-permute-start(f32[96,128]{1,0:T(8,128)S(1)} %get-tuple-element.48), channel_id=1, source_target_pairs={{0,3},{1,2},{2,1},{3,0},{4,7},{5,6},{6,5},{7,4},{8,11},{9,10},{10,... | collective-permute-start | bytes 147464 | tf_op jit(solution)/shard_map/ppermute | solution.py:486
  85.2 4.6 %collective-permute-start.21 = (f32[96,128]{1,0:T(8,128)S(1)}, f32[96,128]{1,0:T(8,128)S(1)}, u32[]{:S(2)}, u32[]{:S(2)}) collective-permute-start(f32[96,128]{1,0:T(8,128)S(1)} %get-tuple-element.48), channel_id=1, source_target_pairs={{0,2},{1,3},{2,0},{3,1},{4,6},{5,7},{6,4},{7,5},{8,10},{9,11},{10,... | collective-permute-start | bytes 147464 | tf_op jit(solution)/shard_map/ppermute | solution.py:486
  85.3 4.5 %collective-permute-start.20 = (f32[96,128]{1,0:T(8,128)S(1)}, f32[96,128]{1,0:T(8,128)S(1)}, u32[]{:S(2)}, u32[]{:S(2)}) collective-permute-start(f32[96,128]{1,0:T(8,128)S(1)} %get-tuple-element.48), channel_id=1, source_target_pairs={{0,1},{1,0},{2,3},{3,2},{4,5},{5,4},{6,7},{7,6},{8,9},{9,8},{10,11... | collective-permute-start | bytes 147464 | tf_op jit(solution)/shard_map/ppermute | solution.py:486
  89.8 6.5 %collective-permute-start.25 = (f32[96,128]{1,0:T(8,128)S(1)}, f32[96,128]{1,0:T(8,128)S(1)}, u32[]{:S(2)}, u32[]{:S(2)}) collective-permute-start(f32[96,128]{1,0:T(8,128)S(1)} %add_add_fusion.1), channel_id=1, source_target_pairs={{0,12},{1,13},{2,14},{3,15},{4,8},{5,9},{6,10},{7,11},{8,4},{9,5},... | collective-permute-start | bytes 147464 | tf_op jit(solution)/shard_map/ppermute | solution.py:486
  92.2 5.3 %collective-permute-start.24 = (f32[96,128]{1,0:T(8,128)S(1)}, f32[96,128]{1,0:T(8,128)S(1)}, u32[]{:S(2)}, u32[]{:S(2)}) collective-permute-start(f32[96,128]{1,0:T(8,128)S(1)} %add_add_fusion.1), channel_id=1, source_target_pairs={{0,8},{1,9},{2,10},{3,11},{4,12},{5,13},{6,14},{7,15},{8,0},{9,1},... | collective-permute-start | bytes 147464 | tf_op jit(solution)/shard_map/ppermute | solution.py:486
  92.2 5.3 %collective-permute-start.23 = (f32[96,128]{1,0:T(8,128)S(1)}, f32[96,128]{1,0:T(8,128)S(1)}, u32[]{:S(2)}, u32[]{:S(2)}) collective-permute-start(f32[96,128]{1,0:T(8,128)S(1)} %add_add_fusion.1), channel_id=1, source_target_pairs={{0,4},{1,5},{2,6},{3,7},{4,0},{5,1},{6,2},{7,3},{8,12},{9,13},{10,... | collective-permute-start | bytes 147464 | tf_op jit(solution)/shard_map/ppermute | solution.py:486

commit v6 on v5

--- a/solution.py
+++ b/solution.py
@@ -133,32 +133,52 @@
     ref[0:rows, 0:width] = value
 
 
+def mirror(modes):
+    row = lax.broadcasted_iota(jnp.int32, (modes, modes), 0)
+    col = lax.broadcasted_iota(jnp.int32, (modes, modes), 1)
+    return row, col
+
+
 def store_folded(ref, value, modes):
     rows, width = value.shape
     old = rows - modes
     spare = LANES - width
     corner, mass_corner = value[old:, :modes], value[old:, modes:]
-    row = lax.broadcasted_iota(jnp.int32, (modes, modes), 0)
-    col = lax.broadcasted_iota(jnp.int32, (modes, modes), 1)
+    row, col = mirror(modes)
     both = jnp.where(row >= col, corner, mass_corner)
     diagonal = jnp.sum(jnp.where(row == col, mass_corner, 0.0), axis=1, keepdims=True)
-    rest = jnp.zeros((modes, 2 * spare - modes - 1), F32)
-    second = jnp.concatenate([both[:, spare:], diagonal, rest], axis=1)
-    folded = jnp.concatenate([both[:, :spare], second], axis=0)
-    ref[...] = jnp.concatenate([value[:old, :], folded], axis=1)
+    if old > modes:
+        rest = jnp.zeros((modes, 2 * spare - modes - 1), F32)
+        second = jnp.concatenate([both[:, spare:], diagonal, rest], axis=1)
+        folded = jnp.concatenate([both[:, :spare], second], axis=0)
+        ref[...] = jnp.concatenate([value[:old, :], folded], axis=1)
+    else:
+        ref[:old, :] = jnp.concatenate([value[:old, :], both[:, :spare]], axis=1)
+        other = jnp.concatenate([both[:, spare:], jnp.broadcast_to(diagonal, (modes, modes - spare))], axis=1)
+        turned = other.T
+        left = modes - spare
+        ref[old:, :modes] = turned[:left]
+        ref[old:, modes : 2 * modes] = turned[left:]
 
 
 def unfold(value, modes):
     width = 2 * modes
     spare = LANES - width
-    both = jnp.concatenate([value[:modes, width:], value[modes : 2 * modes, width : width + modes - spare]], axis=1)
-    diagonal = value[modes : 2 * modes, width + modes - spare : width + modes - spare + 1]
-    row = lax.broadcasted_iota(jnp.int32, (modes, modes), 0)
-    col = lax.broadcasted_iota(jnp.int32, (modes, modes), 1)
+    left = modes - spare
+    row, col = mirror(modes)
+    if value.shape[0] >= 2 * modes:
+        old = 2 * modes
+        both = jnp.concatenate([value[:modes, width:], value[modes:old, width : width + left]], axis=1)
+        diagonal = value[modes:old, width + left : width + left + 1]
+    else:
+        old = modes
+        back = jnp.concatenate([value[old:, :modes], value[old:, modes:width]], axis=0).T
+        both = jnp.concatenate([value[:old, width:], back[:, :left]], axis=1)
+        diagonal = back[:, left : left + 1]
     turned = both.T
     corner = jnp.where(row >= col, both, turned)
     mass_corner = jnp.where(row < col, both, jnp.where(row > col, turned, diagonal))
-    return jnp.concatenate([value[:, :width], jnp.concatenate([corner, mass_corner], axis=1)], axis=0)
+    return jnp.concatenate([value[:old, :width], jnp.concatenate([corner, mass_corner], axis=1)], axis=0)
 
 
 def chosen_nodes(nodes, base, window):
@@ -169,9 +189,10 @@
 
 def pick(halves, chosen, base, picked):
     window = chosen.shape[0]
-    picked[...] = dot1(halves[0][:, base : base + window], chosen, NN) + dot1(
-        halves[1][:, base : base + window], chosen, NN
-    )
+    rows = halves[0].shape[0]
+    both = jnp.concatenate([half[:, base : base + window] for half in halves], axis=0)
+    values = dot1(both, chosen, NN)
+    picked[...] = values[:rows] + values[rows:]
 
 
 def multiply(dims, entries, groups, picked, high, low, marks, out):
@@ -183,8 +204,9 @@
 
     def place(comp):
         rows = pl.ds(pl.multiple_of(comp * pair, pair), pair)
-        target = marks[:, :width]
-        out[rows, :] += dot1(high[rows, :width], target, NT) + dot1(low[rows, :width], target, NT)
+        both = jnp.concatenate([high[rows, :width], low[rows, :width]], axis=0)
+        sums = dot1(both, marks[:, :width], NT)
+        out[rows, :] += sums[:pair] + sums[pair:]
 
     def one(comp, unused):
         place(comp)
@@ -389,7 +411,7 @@
     all_products(dims, ext, stiffness, mass, edges, connect, edge_nodes, picked, high, low, marks, sums)
     out = sums.at[2 * modes :, :]
     store_sides(out, side_a, side_b)
-    store_lanes(gram, grams([block[...], residual[...]], out[...], dims))
+    store_folded(gram, grams([block[...], residual[...]], out[...], dims), modes)
 
 
 def small_step(reduced, solver, mass_old, start, modes):
@@ -411,7 +433,11 @@
     unit = eye(modes)
     carried = dotf(turned[:modes, :old], solver)
     schur = symmetric(corner - dotf(carried, cross))
-    root = jnp.concatenate(eliminate(schur, [-carried, unit], modes), axis=1)
+    pushed = dotf(start, mass_all[: start.shape[1], :])
+    behind = pushed[:, :old]
+    ahead = pushed[:, old:].T - dotf(carried, behind, NT)
+    left, right, along = eliminate(schur, [-carried, unit, ahead], modes)
+    root = jnp.concatenate([left, right], axis=1)
     wide = jnp.concatenate(
         [
             jnp.concatenate([solver, jnp.zeros((old, modes), F32)], axis=1),
@@ -419,9 +445,9 @@
         ],
         axis=0,
     )
+    base = jnp.concatenate([dotf(behind, solver), jnp.zeros((modes, modes), F32)], axis=1)
+    solved = base + dotf(along, root, TN)
     solver = wide + dotf(root, root, TN)
-    pushed = dotf(start, mass_all[: start.shape[1], :])
-    solved = dotf(pushed, solver)
     again = dotf(solved, mass_all)
     (pushed,) = eliminate(symmetric(dotf(solved, again, NT)), [again], modes)
     solved = dotf(pushed, solver)
@@ -439,7 +465,7 @@
     copies += start_sides(own_a, own_b, lower, upper, sems, 2)
     copies += start_sides(more_a, more_b, new_below, new_above, sems, 4)
     copies += start_sides(new_a, new_b, new_lower, new_upper, sems, 6)
-    coeff, half, root, solver, mass_all = small_step(gram_in[...], state_in[1], state_in[2], state_in[0], modes)
+    coeff, half, root, solver, mass_all = small_step(unfold(gram_in[...], modes), state_in[1], state_in[2], state_in[0], modes)
     rayleigh = symmetric(dotf(half, root, NT))
     coeff_out[...] = coeff
     state[0] = solver
@@ -583,7 +609,7 @@
     residual, q_a, q_b, gram, state = call(
         second_kernel,
         dims,
-        [wide, side, side, (near, (2 * modes, LANES), F32), (near, (3, modes, modes), F32)],
+        [wide, side, side, (near, (4 * modes - LANES, LANES), F32), (near, (3, modes, modes), F32)],
         work + room(*p) + [sems((4,))],
         (gram, link, edge_nodes, block, stiff_near, mass_near, edges, *p),
         (),

time: 105 us -> 103 us (0.981)
  waiting for transfers between devices: 21 us -> 19.9 us
    ppermute x18, waiting for transfers between devices: 20.7 us -> 19.5 us  [from_partner(): return lax.ppermute(part, axis, [(i, i ^ bits) for i in range(count)])]
  transfers between devices with their start and end apart: 26 -> 26, of which waited for: 11 -> 10; matrix products, arithmetic and copies ran while one was open for 0% -> 0% of each run, Pallas kernels for 7% -> 7%
where the time goes in v6:
time: 103 us
  Pallas kernels  48.4 us (47%)
  starting transfers between devices  34.1 us (33%)
  waiting for transfers between devices  19.9 us (19%)
    pallas_call x7, Pallas kernels, call(): pl.pallas_call(functools.partial(kernel, dims), out_shape=shapes, in_spec...  48.4 us
    ppermute x18, starting transfers between devices, from_partner(): return lax.ppermute(part, axis, [(i, i ^ bits) for i in range(count)])  26.5 us
    ppermute x18, waiting for transfers between devices, from_partner(): return lax.ppermute(part, axis, [(i, i ^ bits) for i in range(count)])  19.5 us
    ppermute x8, starting transfers between devices, swap(): return lax.ppermute(value, axis, pairs + [(b, a) for a, b in pairs])  7.63 us
  transfers between devices with their start and end apart: 26, of which 10 were waited for; matrix products, arithmetic and copies ran while one was open for 0% of the time, Pallas kernels for 7%

profile of v6, /device:TPU:0, one launch (start us, length us, event | category | flops | bytes accessed | tf_op | source)
XLA Modules:
  0.0 103.2 jit_solution(9397613472935092570)
XLA Ops:
  0.6 1.4 %shard_map.60 = (s32[4,256]{1,0:T(4,128)S(1)}, f32[24,24,256]{2,1,0:T(8,128)S(1)}, f32[24,24,256]{2,1,0:T(8,128)S(1)}, f32[296,128]{1,0:T(8,128)S(1)}, f32[296,128]{1,0:T(8,128)S(1)}) custom-call(s32[4,256]{1,0:T(4,128)} %connect_in.1, f32[24,24,256]{2,1,0:T(8,128)} %stiff_in.1, f32[24,24,256]{2,1,0:T(8,128)} %mass_in.1), custom_call_target="tpu_custom_call" | custom-call | tf_op jit(solution)/shard_map/pallas_call | solution.py:545
  2.1 0.6 collective-permute-start.2
  2.6 0.7 collective-permute-start.3
  3.3 1.0 shard_map.59
  4.3 3.9 %collective-permute-start = (f32[288,128]{1,0:T(8,128)S(1)}, f32[288,128]{1,0:T(8,128)S(1)}, u32[]{:S(2)}, u32[]{:S(2)}) collective-permute-start(f32[288,128]{1,0:T(8,128)S(1)} %get-tuple-element.32), channel_id=1, source_target_pairs={{0,1},{2,3},{4,5},{6,7},{8,9},{10,11},{12,13},{14,15},{1,0},{3,2},... | collective-permute-start | bytes 442376 | tf_op jit(solution)/shard_map/ppermute | solution.py:531
  8.2 0.7 collective-permute-start.1
  8.9 0.3 collective-permute-done.from_a
  9.2 0.0 collective-permute-done.1.from_b
  9.2 6.4 %shard_map.61 = (f32[288,512]{1,0:T(8,128)S(1)}, f32[672,256]{1,0:T(8,128)S(1)}) custom-call(f32[288,256]{1,0:T(8,128)S(1)} %get-tuple-element.28.block, s32[4,256]{1,0:T(4,128)S(1)} %get-tuple-element.29.connect, f32[24,24,256]{2,1,0:T(8,128)S(1)} %get-tuple-element.30.stiffness, f32[24,24,256]{2,1,0:T(8,128)S(1)} %get-tuple-element.31.mass, ...), custom_call_target="tpu_custom_call" | custom-call | tf_op jit(solution)/shard_map/pallas_call | solution.py:545
  15.7 0.0 collective-permute-done.2.from_a
  15.7 0.0 collective-permute-done.3.from_b
  15.7 3.2 %shard_map.62 = (f32[2,12,24,128]{3,2,1,0:T(8,128)S(1)}, s32[8,128]{1,0:T(8,128)S(1)}, f32[576,128]{1,0:T(8,128)S(1)}, f32[576,128]{1,0:T(8,128)S(1)}, f32[48,128]{1,0:T(8,128)S(1)}) custom-call(f32[288,256]{1,0:T(8,128)S(1)} %get-tuple-element.28.block, s32[4,256]{1,0:T(4,128)S(1)} %get-tuple-element.29.connect, f32[288,512]{1,0:T(8,128)S(1)} %get-tuple-element.34.ext, ...), custom_call_target="tpu_custom_call" | custom-call | tf_op jit(solution)/shard_map/pallas_call | solution.py:545
  19.0 7.7 %collective-permute-start.6 = (f32[48,128]{1,0:T(8,128)S(1)}, f32[48,128]{1,0:T(8,128)S(1)}, u32[]{:S(2)}, u32[]{:S(2)}) collective-permute-start(f32[48,128]{1,0:T(8,128)S(1)} %get-tuple-element.38), channel_id=1, source_target_pairs={{0,3},{1,2},{2,1},{3,0},{4,7},{5,6},{6,5},{7,4},{8,11},{9,10},{10,... | collective-permute-start | bytes 73736 | tf_op jit(solution)/shard_map/ppermute | solution.py:512
  26.6 1.0 collective-permute-start.5
  27.6 0.0 collective-permute-start.4
  27.7 0.5 collective-permute-start.10
  28.1 0.7 collective-permute-start.11
  28.8 0.0 collective-permute-done.6
  28.8 1.8 %collective-permute-done.5 = f32[48,128]{1,0:T(8,128)S(1)} collective-permute-done((f32[48,128]{1,0:T(8,128)S(1)}, f32[48,128]{1,0:T(8,128)S(1)}, u32[]{:S(2)}, u32[]{:S(2)}) %collective-permute-start.5) | collective-permute-done | bytes 24608 | tf_op jit(solution)/shard_map/ppermute | solution.py:512
  30.6 0.0 collective-permute-done.4
  30.6 4.4 %collective-permute-start.9 = (f32[48,128]{1,0:T(8,128)S(1)}, f32[48,128]{1,0:T(8,128)S(1)}, u32[]{:S(2)}, u32[]{:S(2)}) collective-permute-start(f32[48,128]{1,0:T(8,128)S(1)} %add_add_fusion.5), channel_id=1, source_target_pairs={{0,12},{1,13},{2,14},{3,15},{4,8},{5,9},{6,10},{7,11},{8,4},{9,5},... | collective-permute-start | bytes 73736 | tf_op jit(solution)/shard_map/ppermute | solution.py:512
  35.0 0.0 collective-permute-start.8
  35.0 0.6 collective-permute-start.7
  35.7 4.7 %collective-permute-done.9 = f32[48,128]{1,0:T(8,128)S(1)} collective-permute-done((f32[48,128]{1,0:T(8,128)S(1)}, f32[48,128]{1,0:T(8,128)S(1)}, u32[]{:S(2)}, u32[]{:S(2)}) %collective-permute-start.9) | collective-permute-done | bytes 24608 | tf_op jit(solution)/shard_map/ppermute | solution.py:512
  40.4 0.0 collective-permute-done.8
  40.4 0.0 collective-permute-done.7
  40.4 0.0 collective-permute-done.10.from_a
  40.4 0.0 collective-permute-done.11.from_b
  40.4 12.5 %shard_map.63 = (f32[288,256]{1,0:T(8,128)S(1)}, f32[576,128]{1,0:T(8,128)S(1)}, f32[576,128]{1,0:T(8,128)S(1)}, f32[64,128]{1,0:T(8,128)S(1)}, f32[3,48,48]{2,1,0:T(8,128)S(1)}) custom-call(f32[48,128]{1,0:T(8,128)S(1)} %add_add_fusion.4.gram_in, s32[4,256]{1,0:T(4,128)S(1)} %get-tuple-element.29.connect, s32[8,128]{1,0:T(8,128)S(1)} %get-tuple-element.39.edge_nodes, ...), custom_call_target="tpu_custom_call" | custom-call | tf_op jit(solution)/shard_map/pallas_call | solution.py:545
  53.0 0.1 collective-permute-start.14
  53.1 0.2 collective-permute-start.13
  53.3 1.6 %collective-permute-start.12 = (f32[64,128]{1,0:T(8,128)S(1)}, f32[64,128]{1,0:T(8,128)S(1)}, u32[]{:S(2)}, u32[]{:S(2)}) collective-permute-start(f32[64,128]{1,0:T(8,128)S(1)} %get-tuple-element.43), channel_id=1, source_target_pairs={{0,1},{1,0},{2,3},{3,2},{4,5},{5,4},{6,7},{7,6},{8,9},{9,8},{10,11... | collective-permute-start | bytes 98312 | tf_op jit(solution)/shard_map/ppermute | solution.py:512
  54.9 0.0 collective-permute-start.18
  54.9 0.7 collective-permute-start.19
  55.6 0.8 collective-permute-done.14
  56.4 0.7 collective-permute-done.13
  57.1 0.0 collective-permute-done.12
  57.1 3.6 %collective-permute-start.17 = (f32[64,128]{1,0:T(8,128)S(1)}, f32[64,128]{1,0:T(8,128)S(1)}, u32[]{:S(2)}, u32[]{:S(2)}) collective-permute-start(f32[64,128]{1,0:T(8,128)S(1)} %add_add_fusion.3), channel_id=1, source_target_pairs={{0,12},{1,13},{2,14},{3,15},{4,8},{5,9},{6,10},{7,11},{8,4},{9,5},... | collective-permute-start | bytes 98312 | tf_op jit(solution)/shard_map/ppermute | solution.py:512
  60.7 0.0 collective-permute-start.16
  60.7 0.9 collective-permute-start.15
  61.6 5.1 %collective-permute-done.17 = f32[64,128]{1,0:T(8,128)S(1)} collective-permute-done((f32[64,128]{1,0:T(8,128)S(1)}, f32[64,128]{1,0:T(8,128)S(1)}, u32[]{:S(2)}, u32[]{:S(2)}) %collective-permute-start.17) | collective-permute-done | bytes 32800 | tf_op jit(solution)/shard_map/ppermute | solution.py:512
  66.6 0.0 collective-permute-done.16
  66.6 0.0 collective-permute-done.15
  66.7 0.0 collective-permute-done.18.more_a
  66.7 0.0 collective-permute-done.19.more_b
  66.7 16.7 %shard_map.64 = (f32[288,256]{1,0:T(8,128)S(1)}, f32[96,128]{1,0:T(8,128)S(1)}, f32[48,96]{1,0:T(8,128)S(1)}, f32[2,96,96]{2,1,0:T(8,128)S(1)}) custom-call(f32[64,128]{1,0:T(8,128)S(1)} %add_add_fusion.2.gram_in, f32[3,48,48]{2,1,0:T(8,128)S(1)} %get-tuple-element.44.state_in, s32[4,256]{1,0:T(4,128)S(1)} %get-tuple-element.29.connect, ...), custom_call_target="tpu_custom_call" | custom-call | tf_op jit(solution)/shard_map/pallas_call | solution.py:545
  83.4 0.1 collective-permute-start.22
  83.4 0.2 collective-permute-start.21
  83.6 1.6 %collective-permute-start.20 = (f32[96,128]{1,0:T(8,128)S(1)}, f32[96,128]{1,0:T(8,128)S(1)}, u32[]{:S(2)}, u32[]{:S(2)}) collective-permute-start(f32[96,128]{1,0:T(8,128)S(1)} %get-tuple-element.48), channel_id=1, source_target_pairs={{0,1},{1,0},{2,3},{3,2},{4,5},{5,4},{6,7},{7,6},{8,9},{9,8},{10,11... | collective-permute-start | bytes 147464 | tf_op jit(solution)/shard_map/ppermute | solution.py:512
  85.3 1.7 %collective-permute-done.22 = f32[96,128]{1,0:T(8,128)S(1)} collective-permute-done((f32[96,128]{1,0:T(8,128)S(1)}, f32[96,128]{1,0:T(8,128)S(1)}, u32[]{:S(2)}, u32[]{:S(2)}) %collective-permute-start.22) | collective-permute-done | bytes 49184 | tf_op jit(solution)/shard_map/ppermute | solution.py:512
  86.9 1.1 %collective-permute-done.21 = f32[96,128]{1,0:T(8,128)S(1)} collective-permute-done((f32[96,128]{1,0:T(8,128)S(1)}, f32[96,128]{1,0:T(8,128)S(1)}, u32[]{:S(2)}, u32[]{:S(2)}) %collective-permute-start.21) | collective-permute-done | bytes 49184 | tf_op jit(solution)/shard_map/ppermute | solution.py:512
  88.0 0.0 collective-permute-done.20
  88.0 2.7 %collective-permute-start.25 = (f32[96,128]{1,0:T(8,128)S(1)}, f32[96,128]{1,0:T(8,128)S(1)}, u32[]{:S(2)}, u32[]{:S(2)}) collective-permute-start(f32[96,128]{1,0:T(8,128)S(1)} %add_add_fusion.1), channel_id=1, source_target_pairs={{0,12},{1,13},{2,14},{3,15},{4,8},{5,9},{6,10},{7,11},{8,4},{9,5},... | collective-permute-start | bytes 147464 | tf_op jit(solution)/shard_map/ppermute | solution.py:512
  90.7 0.3 collective-permute-start.24
  91.0 1.5 %collective-permute-start.23 = (f32[96,128]{1,0:T(8,128)S(1)}, f32[96,128]{1,0:T(8,128)S(1)}, u32[]{:S(2)}, u32[]{:S(2)}) collective-permute-start(f32[96,128]{1,0:T(8,128)S(1)} %add_add_fusion.1), channel_id=1, source_target_pairs={{0,4},{1,5},{2,6},{3,7},{4,0},{5,1},{6,2},{7,3},{8,12},{9,13},{10,... | collective-permute-start | bytes 147464 | tf_op jit(solution)/shard_map/ppermute | solution.py:512
  92.5 1.9 %collective-permute-done.25 = f32[96,128]{1,0:T(8,128)S(1)} collective-permute-done((f32[96,128]{1,0:T(8,128)S(1)}, f32[96,128]{1,0:T(8,128)S(1)}, u32[]{:S(2)}, u32[]{:S(2)}) %collective-permute-start.25) | collective-permute-done | bytes 49184 | tf_op jit(solution)/shard_map/ppermute | solution.py:512
  94.4 1.8 %collective-permute-done.24 = f32[96,128]{1,0:T(8,128)S(1)} collective-permute-done((f32[96,128]{1,0:T(8,128)S(1)}, f32[96,128]{1,0:T(8,128)S(1)}, u32[]{:S(2)}, u32[]{:S(2)}) %collective-permute-start.24) | collective-permute-done | bytes 49184 | tf_op jit(solution)/shard_map/ppermute | solution.py:512
  96.1 0.0 collective-permute-done.23
  96.2 7.1 %shard_map.65 = (f32[288,256]{1,0:T(8,128)}, f32[1,48]{1,0:T(1,128)}) custom-call(f32[96,128]{1,0:T(8,128)S(1)} %add_add_fusion.gram_in, f32[48,96]{1,0:T(8,128)S(1)} %get-tuple-element.49.coeff_in, f32[2,96,96]{2,1,0:T(8,128)S(1)} %get-tuple-element.50.state_in, f32[288,256]{1,0:T(8,128)S(1)} %get-tuple-element.28.block, ...), custom_call_target="tpu_custom_call" | custom-call | tf_op jit(solution)/shard_map/pallas_call | solution.py:545
  (6 shorter events, 0.1 us)
Async XLA Ops:
  2.1 13.6 %collective-permute-start.2 = (f32[296,128]{1,0:T(8,128)S(1)}, f32[296,128]{1,0:T(8,128)S(1)}, u32[]{:S(2)}, u32[]{:S(2)}) collective-permute-start(f32[296,128]{1,0:T(8,128)S(1)} %get-tuple-element.36), channel_id=1, source_target_pairs={{0,1},{2,3},{4,5},{6,7},{8,9},{10,11},{12,13},{14,15},{1,0},{3,2},... | collective-permute-start | bytes 454664 | tf_op jit(solution)/shard_map/ppermute | solution.py:531
  2.6 13.1 %collective-permute-start.3 = (f32[296,128]{1,0:T(8,128)S(1)}, f32[296,128]{1,0:T(8,128)S(1)}, u32[]{:S(2)}, u32[]{:S(2)}) collective-permute-start(f32[296,128]{1,0:T(8,128)S(1)} %get-tuple-element.37), channel_id=1, source_target_pairs={{1,2},{3,4},{5,6},{7,8},{9,10},{11,12},{13,14},{2,1},{4,3},{6,5},{... | collective-permute-start | bytes 454664 | tf_op jit(solution)/shard_map/ppermute | solution.py:531
  4.3 5.0 %collective-permute-start = (f32[288,128]{1,0:T(8,128)S(1)}, f32[288,128]{1,0:T(8,128)S(1)}, u32[]{:S(2)}, u32[]{:S(2)}) collective-permute-start(f32[288,128]{1,0:T(8,128)S(1)} %get-tuple-element.32), channel_id=1, source_target_pairs={{0,1},{2,3},{4,5},{6,7},{8,9},{10,11},{12,13},{14,15},{1,0},{3,2},... | collective-permute-start | bytes 442376 | tf_op jit(solution)/shard_map/ppermute | solution.py:531
  8.2 1.0 collective-permute-start.1
  19.0 9.9 %collective-permute-start.6 = (f32[48,128]{1,0:T(8,128)S(1)}, f32[48,128]{1,0:T(8,128)S(1)}, u32[]{:S(2)}, u32[]{:S(2)}) collective-permute-start(f32[48,128]{1,0:T(8,128)S(1)} %get-tuple-element.38), channel_id=1, source_target_pairs={{0,3},{1,2},{2,1},{3,0},{4,7},{5,6},{6,5},{7,4},{8,11},{9,10},{10,... | collective-permute-start | bytes 73736 | tf_op jit(solution)/shard_map/ppermute | solution.py:512
  26.6 4.0 %collective-permute-start.5 = (f32[48,128]{1,0:T(8,128)S(1)}, f32[48,128]{1,0:T(8,128)S(1)}, u32[]{:S(2)}, u32[]{:S(2)}) collective-permute-start(f32[48,128]{1,0:T(8,128)S(1)} %get-tuple-element.38), channel_id=1, source_target_pairs={{0,2},{1,3},{2,0},{3,1},{4,6},{5,7},{6,4},{7,5},{8,10},{9,11},{10,... | collective-permute-start | bytes 73736 | tf_op jit(solution)/shard_map/ppermute | solution.py:512
  27.6 3.0 %collective-permute-start.4 = (f32[48,128]{1,0:T(8,128)S(1)}, f32[48,128]{1,0:T(8,128)S(1)}, u32[]{:S(2)}, u32[]{:S(2)}) collective-permute-start(f32[48,128]{1,0:T(8,128)S(1)} %get-tuple-element.38), channel_id=1, source_target_pairs={{0,1},{1,0},{2,3},{3,2},{4,5},{5,4},{6,7},{7,6},{8,9},{9,8},{10,11... | collective-permute-start | bytes 73736 | tf_op jit(solution)/shard_map/ppermute | solution.py:512
  27.7 12.7 %collective-permute-start.10 = (f32[576,128]{1,0:T(8,128)S(1)}, f32[576,128]{1,0:T(8,128)S(1)}, u32[]{:S(2)}, u32[]{:S(2)}) collective-permute-start(f32[576,128]{1,0:T(8,128)S(1)} %get-tuple-element.41.own_a), channel_id=1, source_target_pairs={{0,1},{2,3},{4,5},{6,7},{8,9},{10,11},{12,13},{14,15},{1,0},{3,2},... | collective-permute-start | bytes 884744 | tf_op jit(solution)/shard_map/ppermute | solution.py:531
  28.1 12.3 %collective-permute-start.11 = (f32[576,128]{1,0:T(8,128)S(1)}, f32[576,128]{1,0:T(8,128)S(1)}, u32[]{:S(2)}, u32[]{:S(2)}) collective-permute-start(f32[576,128]{1,0:T(8,128)S(1)} %get-tuple-element.42.own_b), channel_id=1, source_target_pairs={{1,2},{3,4},{5,6},{7,8},{9,10},{11,12},{13,14},{2,1},{4,3},{6,5},{... | collective-permute-start | bytes 884744 | tf_op jit(solution)/shard_map/ppermute | solution.py:531
  30.6 9.7 %collective-permute-start.9 = (f32[48,128]{1,0:T(8,128)S(1)}, f32[48,128]{1,0:T(8,128)S(1)}, u32[]{:S(2)}, u32[]{:S(2)}) collective-permute-start(f32[48,128]{1,0:T(8,128)S(1)} %add_add_fusion.5), channel_id=1, source_target_pairs={{0,12},{1,13},{2,14},{3,15},{4,8},{5,9},{6,10},{7,11},{8,4},{9,5},... | collective-permute-start | bytes 73736 | tf_op jit(solution)/shard_map/ppermute | solution.py:512
  35.0 5.4 %collective-permute-start.8 = (f32[48,128]{1,0:T(8,128)S(1)}, f32[48,128]{1,0:T(8,128)S(1)}, u32[]{:S(2)}, u32[]{:S(2)}) collective-permute-start(f32[48,128]{1,0:T(8,128)S(1)} %add_add_fusion.5), channel_id=1, source_target_pairs={{0,8},{1,9},{2,10},{3,11},{4,12},{5,13},{6,14},{7,15},{8,0},{9,1},... | collective-permute-start | bytes 73736 | tf_op jit(solution)/shard_map/ppermute | solution.py:512
  35.0 5.4 %collective-permute-start.7 = (f32[48,128]{1,0:T(8,128)S(1)}, f32[48,128]{1,0:T(8,128)S(1)}, u32[]{:S(2)}, u32[]{:S(2)}) collective-permute-start(f32[48,128]{1,0:T(8,128)S(1)} %add_add_fusion.5), channel_id=1, source_target_pairs={{0,4},{1,5},{2,6},{3,7},{4,0},{5,1},{6,2},{7,3},{8,12},{9,13},{10,... | collective-permute-start | bytes 73736 | tf_op jit(solution)/shard_map/ppermute | solution.py:512
  53.0 3.4 %collective-permute-start.14 = (f32[64,128]{1,0:T(8,128)S(1)}, f32[64,128]{1,0:T(8,128)S(1)}, u32[]{:S(2)}, u32[]{:S(2)}) collective-permute-start(f32[64,128]{1,0:T(8,128)S(1)} %get-tuple-element.43), channel_id=1, source_target_pairs={{0,3},{1,2},{2,1},{3,0},{4,7},{5,6},{6,5},{7,4},{8,11},{9,10},{10,... | collective-permute-start | bytes 98312 | tf_op jit(solution)/shard_map/ppermute | solution.py:512
  53.1 4.0 %collective-permute-start.13 = (f32[64,128]{1,0:T(8,128)S(1)}, f32[64,128]{1,0:T(8,128)S(1)}, u32[]{:S(2)}, u32[]{:S(2)}) collective-permute-start(f32[64,128]{1,0:T(8,128)S(1)} %get-tuple-element.43), channel_id=1, source_target_pairs={{0,2},{1,3},{2,0},{3,1},{4,6},{5,7},{6,4},{7,5},{8,10},{9,11},{10,... | collective-permute-start | bytes 98312 | tf_op jit(solution)/shard_map/ppermute | solution.py:512
  53.3 3.8 %collective-permute-start.12 = (f32[64,128]{1,0:T(8,128)S(1)}, f32[64,128]{1,0:T(8,128)S(1)}, u32[]{:S(2)}, u32[]{:S(2)}) collective-permute-start(f32[64,128]{1,0:T(8,128)S(1)} %get-tuple-element.43), channel_id=1, source_target_pairs={{0,1},{1,0},{2,3},{3,2},{4,5},{5,4},{6,7},{7,6},{8,9},{9,8},{10,11... | collective-permute-start | bytes 98312 | tf_op jit(solution)/shard_map/ppermute | solution.py:512
  54.9 11.8 %collective-permute-start.18 = (f32[576,128]{1,0:T(8,128)S(1)}, f32[576,128]{1,0:T(8,128)S(1)}, u32[]{:S(2)}, u32[]{:S(2)}) collective-permute-start(f32[576,128]{1,0:T(8,128)S(1)} %get-tuple-element.46.new_a), channel_id=1, source_target_pairs={{0,1},{2,3},{4,5},{6,7},{8,9},{10,11},{12,13},{14,15},{1,0},{3,2},... | collective-permute-start | bytes 884744 | tf_op jit(solution)/shard_map/ppermute | solution.py:531
  54.9 11.8 %collective-permute-start.19 = (f32[576,128]{1,0:T(8,128)S(1)}, f32[576,128]{1,0:T(8,128)S(1)}, u32[]{:S(2)}, u32[]{:S(2)}) collective-permute-start(f32[576,128]{1,0:T(8,128)S(1)} %get-tuple-element.47.new_b), channel_id=1, source_target_pairs={{1,2},{3,4},{5,6},{7,8},{9,10},{11,12},{13,14},{2,1},{4,3},{6,5},{... | collective-permute-start | bytes 884744 | tf_op jit(solution)/shard_map/ppermute | solution.py:531
  57.1 9.5 %collective-permute-start.17 = (f32[64,128]{1,0:T(8,128)S(1)}, f32[64,128]{1,0:T(8,128)S(1)}, u32[]{:S(2)}, u32[]{:S(2)}) collective-permute-start(f32[64,128]{1,0:T(8,128)S(1)} %add_add_fusion.3), channel_id=1, source_target_pairs={{0,12},{1,13},{2,14},{3,15},{4,8},{5,9},{6,10},{7,11},{8,4},{9,5},... | collective-permute-start | bytes 98312 | tf_op jit(solution)/shard_map/ppermute | solution.py:512
  60.7 6.0 %collective-permute-start.16 = (f32[64,128]{1,0:T(8,128)S(1)}, f32[64,128]{1,0:T(8,128)S(1)}, u32[]{:S(2)}, u32[]{:S(2)}) collective-permute-start(f32[64,128]{1,0:T(8,128)S(1)} %add_add_fusion.3), channel_id=1, source_target_pairs={{0,8},{1,9},{2,10},{3,11},{4,12},{5,13},{6,14},{7,15},{8,0},{9,1},... | collective-permute-start | bytes 98312 | tf_op jit(solution)/shard_map/ppermute | solution.py:512
  60.7 6.0 %collective-permute-start.15 = (f32[64,128]{1,0:T(8,128)S(1)}, f32[64,128]{1,0:T(8,128)S(1)}, u32[]{:S(2)}, u32[]{:S(2)}) collective-permute-start(f32[64,128]{1,0:T(8,128)S(1)} %add_add_fusion.3), channel_id=1, source_target_pairs={{0,4},{1,5},{2,6},{3,7},{4,0},{5,1},{6,2},{7,3},{8,12},{9,13},{10,... | collective-permute-start | bytes 98312 | tf_op jit(solution)/shard_map/ppermute | solution.py:512
  83.4 3.6 %collective-permute-start.22 = (f32[96,128]{1,0:T(8,128)S(1)}, f32[96,128]{1,0:T(8,128)S(1)}, u32[]{:S(2)}, u32[]{:S(2)}) collective-permute-start(f32[96,128]{1,0:T(8,128)S(1)} %get-tuple-element.48), channel_id=1, source_target_pairs={{0,3},{1,2},{2,1},{3,0},{4,7},{5,6},{6,5},{7,4},{8,11},{9,10},{10,... | collective-permute-start | bytes 147464 | tf_op jit(solution)/shard_map/ppermute | solution.py:512
  83.4 4.6 %collective-permute-start.21 = (f32[96,128]{1,0:T(8,128)S(1)}, f32[96,128]{1,0:T(8,128)S(1)}, u32[]{:S(2)}, u32[]{:S(2)}) collective-permute-start(f32[96,128]{1,0:T(8,128)S(1)} %get-tuple-element.48), channel_id=1, source_target_pairs={{0,2},{1,3},{2,0},{3,1},{4,6},{5,7},{6,4},{7,5},{8,10},{9,11},{10,... | collective-permute-start | bytes 147464 | tf_op jit(solution)/shard_map/ppermute | solution.py:512
  83.6 4.4 %collective-permute-start.20 = (f32[96,128]{1,0:T(8,128)S(1)}, f32[96,128]{1,0:T(8,128)S(1)}, u32[]{:S(2)}, u32[]{:S(2)}) collective-permute-start(f32[96,128]{1,0:T(8,128)S(1)} %get-tuple-element.48), channel_id=1, source_target_pairs={{0,1},{1,0},{2,3},{3,2},{4,5},{5,4},{6,7},{7,6},{8,9},{9,8},{10,11... | collective-permute-start | bytes 147464 | tf_op jit(solution)/shard_map/ppermute | solution.py:512
  88.0 6.4 %collective-permute-start.25 = (f32[96,128]{1,0:T(8,128)S(1)}, f32[96,128]{1,0:T(8,128)S(1)}, u32[]{:S(2)}, u32[]{:S(2)}) collective-permute-start(f32[96,128]{1,0:T(8,128)S(1)} %add_add_fusion.1), channel_id=1, source_target_pairs={{0,12},{1,13},{2,14},{3,15},{4,8},{5,9},{6,10},{7,11},{8,4},{9,5},... | collective-permute-start | bytes 147464 | tf_op jit(solution)/shard_map/ppermute | solution.py:512
  90.7 5.5 %collective-permute-start.24 = (f32[96,128]{1,0:T(8,128)S(1)}, f32[96,128]{1,0:T(8,128)S(1)}, u32[]{:S(2)}, u32[]{:S(2)}) collective-permute-start(f32[96,128]{1,0:T(8,128)S(1)} %add_add_fusion.1), channel_id=1, source_target_pairs={{0,8},{1,9},{2,10},{3,11},{4,12},{5,13},{6,14},{7,15},{8,0},{9,1},... | collective-permute-start | bytes 147464 | tf_op jit(solution)/shard_map/ppermute | solution.py:512
  91.0 5.2 %collective-permute-start.23 = (f32[96,128]{1,0:T(8,128)S(1)}, f32[96,128]{1,0:T(8,128)S(1)}, u32[]{:S(2)}, u32[]{:S(2)}) collective-permute-start(f32[96,128]{1,0:T(8,128)S(1)} %add_add_fusion.1), channel_id=1, source_target_pairs={{0,4},{1,5},{2,6},{3,7},{4,0},{5,1},{6,2},{7,3},{8,12},{9,13},{10,... | collective-permute-start | bytes 147464 | tf_op jit(solution)/shard_map/ppermute | solution.py:512

commit v7 on v6

--- a/solution.py
+++ b/solution.py
@@ -30,11 +30,11 @@
 
 
 def dot3(left, right, dims=NN):
+    rows = left.shape[0]
     left_high, left_low = split(left)
     right_high, right_low = split(right)
-    return dot1(left_high, right_high, dims) + (
-        dot1(left_high, right_low, dims) + dot1(left_low, right_high, dims)
-    )
+    both = dot1(jnp.concatenate([left_high, left_low], axis=0), right_high, dims)
+    return both[:rows] + (both[rows:] + dot1(left_high, right_low, dims))
 
 
 def dotf(left, right, dims=NN):
@@ -395,17 +395,14 @@
     state[0] = inverse
     state[1] = dotf(stiff_root, stiff_root, TN)
     state[2] = mass_gram
-    ratio_high, ratio_low = split(ratio)
     for copy in copies:
         copy.wait()
     pieces = []
     for c in range(comps):
         row = c * 2 * modes
         left = jnp.concatenate([part[row : row + modes, :] for part in tiles], axis=1)
-        right_high, right_low = split(jnp.concatenate([part[row + modes : row + 2 * modes, :] for part in tiles], axis=1))
-        pieces.append(
-            left - (dot1(ratio_high, right_high, NN) + (dot1(ratio_high, right_low, NN) + dot1(ratio_low, right_high, NN)))
-        )
+        right = jnp.concatenate([part[row + modes : row + 2 * modes, :] for part in tiles], axis=1)
+        pieces.append(left - dot3(ratio, right))
     ext = jnp.concatenate(pieces, axis=0)
     residual[...] = ext[:, LANES : 3 * LANES]
     all_products(dims, ext, stiffness, mass, edges, connect, edge_nodes, picked, high, low, marks, sums)
@@ -472,7 +469,6 @@
     state[1] = mass_all
     bent = dotf(rayleigh, coeff)
     mixed = jnp.concatenate([coeff[:, :modes], -bent[:, :modes], coeff[:, modes:], -bent[:, modes:]], axis=1)
-    mixed_high, mixed_low = split(mixed)
     for copy in copies:
         copy.wait()
     pieces = []
@@ -481,8 +477,7 @@
         right = jnp.concatenate(
             [jnp.concatenate([part[rows, :] for part in parts], axis=0) for parts in tiles], axis=1
         )
-        right_high, right_low = split(right)
-        pieces.append(dot1(mixed_high, right_high, NN) + (dot1(mixed_high, right_low, NN) + dot1(mixed_low, right_high, NN)))
+        pieces.append(dot3(mixed, right))
     ext = jnp.concatenate(pieces, axis=0)
     new[...] = ext[:, LANES : 3 * LANES]
     all_products(dims, ext, stiffness, mass, edges, connect, edge_nodes, picked, high, low, marks, sums)
@@ -494,13 +489,9 @@
     comps, modes = dims
     coeff, half, root, _, _ = small_step(unfold(gram_in[...], modes), state_in[0], state_in[1], coeff_in[...], modes)
     ritz_out[...] = jnp.sum(dotf(half, root, NT) * eye(modes), axis=0, keepdims=True)
-    coeff_high, coeff_low = split(coeff)
     for c in range(comps):
         rows = slice(c * modes, (c + 1) * modes)
-        right_high, right_low = split(jnp.concatenate([part[rows, :] for part in (block, residual, new)], axis=0))
-        modes_out[rows, :] = dot1(coeff_high, right_high, NN) + (
-            dot1(coeff_high, right_low, NN) + dot1(coeff_low, right_high, NN)
-        )
+        modes_out[rows, :] = dot3(coeff, jnp.concatenate([part[rows, :] for part in (block, residual, new)], axis=0))
 
 
 def total_over(value, axis):

time: 103 us -> 103 us (level)
  no operation moved by 1% of the time
where the time goes in v7:
time: 103 us
  Pallas kernels  48 us (47%)
  starting transfers between devices  34.1 us (33%)
  waiting for transfers between devices  19.9 us (19%)
    pallas_call x7, Pallas kernels, call(): pl.pallas_call(functools.partial(kernel, dims), out_shape=shapes, in_spec...  48 us
    ppermute x18, starting transfers between devices, from_partner(): return lax.ppermute(part, axis, [(i, i ^ bits) for i in range(count)])  26.5 us
    ppermute x18, waiting for transfers between devices, from_partner(): return lax.ppermute(part, axis, [(i, i ^ bits) for i in range(count)])  19.5 us
    ppermute x8, starting transfers between devices, swap(): return lax.ppermute(value, axis, pairs + [(b, a) for a, b in pairs])  7.63 us
  transfers between devices with their start and end apart: 26, of which 10 were waited for; matrix products, arithmetic and copies ran while one was open for 0% of the time, Pallas kernels for 7%

profile of v7, /device:TPU:0, one launch (start us, length us, event | category | flops | bytes accessed | tf_op | source)
XLA Modules:
  0.0 102.9 jit_solution(11071699437143540679)
XLA Ops:
  0.6 1.4 %shard_map.60 = (s32[4,256]{1,0:T(4,128)S(1)}, f32[24,24,256]{2,1,0:T(8,128)S(1)}, f32[24,24,256]{2,1,0:T(8,128)S(1)}, f32[296,128]{1,0:T(8,128)S(1)}, f32[296,128]{1,0:T(8,128)S(1)}) custom-call(s32[4,256]{1,0:T(4,128)} %connect_in.1, f32[24,24,256]{2,1,0:T(8,128)} %stiff_in.1, f32[24,24,256]{2,1,0:T(8,128)} %mass_in.1), custom_call_target="tpu_custom_call" | custom-call | tf_op jit(solution)/shard_map/pallas_call | solution.py:536
  2.1 0.6 collective-permute-start.2
  2.6 0.7 collective-permute-start.3
  3.3 1.0 shard_map.59
  4.3 3.9 %collective-permute-start = (f32[288,128]{1,0:T(8,128)S(1)}, f32[288,128]{1,0:T(8,128)S(1)}, u32[]{:S(2)}, u32[]{:S(2)}) collective-permute-start(f32[288,128]{1,0:T(8,128)S(1)} %get-tuple-element.32), channel_id=1, source_target_pairs={{0,1},{2,3},{4,5},{6,7},{8,9},{10,11},{12,13},{14,15},{1,0},{3,2},... | collective-permute-start | bytes 442376 | tf_op jit(solution)/shard_map/ppermute | solution.py:522
  8.2 0.7 collective-permute-start.1
  8.9 0.3 collective-permute-done.from_a
  9.2 0.0 collective-permute-done.1.from_b
  9.2 6.4 %shard_map.61 = (f32[288,512]{1,0:T(8,128)S(1)}, f32[672,256]{1,0:T(8,128)S(1)}) custom-call(f32[288,256]{1,0:T(8,128)S(1)} %get-tuple-element.28.block, s32[4,256]{1,0:T(4,128)S(1)} %get-tuple-element.29.connect, f32[24,24,256]{2,1,0:T(8,128)S(1)} %get-tuple-element.30.stiffness, f32[24,24,256]{2,1,0:T(8,128)S(1)} %get-tuple-element.31.mass, ...), custom_call_target="tpu_custom_call" | custom-call | tf_op jit(solution)/shard_map/pallas_call | solution.py:536
  15.7 0.0 collective-permute-done.2.from_a
  15.7 0.0 collective-permute-done.3.from_b
  15.7 3.1 %shard_map.62 = (f32[2,12,24,128]{3,2,1,0:T(8,128)S(1)}, s32[8,128]{1,0:T(8,128)S(1)}, f32[576,128]{1,0:T(8,128)S(1)}, f32[576,128]{1,0:T(8,128)S(1)}, f32[48,128]{1,0:T(8,128)S(1)}) custom-call(f32[288,256]{1,0:T(8,128)S(1)} %get-tuple-element.28.block, s32[4,256]{1,0:T(4,128)S(1)} %get-tuple-element.29.connect, f32[288,512]{1,0:T(8,128)S(1)} %get-tuple-element.34.ext, ...), custom_call_target="tpu_custom_call" | custom-call | tf_op jit(solution)/shard_map/pallas_call | solution.py:536
  18.8 7.7 %collective-permute-start.6 = (f32[48,128]{1,0:T(8,128)S(1)}, f32[48,128]{1,0:T(8,128)S(1)}, u32[]{:S(2)}, u32[]{:S(2)}) collective-permute-start(f32[48,128]{1,0:T(8,128)S(1)} %get-tuple-element.38), channel_id=1, source_target_pairs={{0,3},{1,2},{2,1},{3,0},{4,7},{5,6},{6,5},{7,4},{8,11},{9,10},{10,... | collective-permute-start | bytes 73736 | tf_op jit(solution)/shard_map/ppermute | solution.py:503
  26.5 1.0 collective-permute-start.5
  27.5 0.0 collective-permute-start.4
  27.6 0.5 collective-permute-start.10
  28.0 0.7 collective-permute-start.11
  28.7 0.0 collective-permute-done.6
  28.7 1.8 %collective-permute-done.5 = f32[48,128]{1,0:T(8,128)S(1)} collective-permute-done((f32[48,128]{1,0:T(8,128)S(1)}, f32[48,128]{1,0:T(8,128)S(1)}, u32[]{:S(2)}, u32[]{:S(2)}) %collective-permute-start.5) | collective-permute-done | bytes 24608 | tf_op jit(solution)/shard_map/ppermute | solution.py:503
  30.5 0.0 collective-permute-done.4
  30.5 4.4 %collective-permute-start.9 = (f32[48,128]{1,0:T(8,128)S(1)}, f32[48,128]{1,0:T(8,128)S(1)}, u32[]{:S(2)}, u32[]{:S(2)}) collective-permute-start(f32[48,128]{1,0:T(8,128)S(1)} %add_add_fusion.5), channel_id=1, source_target_pairs={{0,12},{1,13},{2,14},{3,15},{4,8},{5,9},{6,10},{7,11},{8,4},{9,5},... | collective-permute-start | bytes 73736 | tf_op jit(solution)/shard_map/ppermute | solution.py:503
  34.9 0.0 collective-permute-start.8
  34.9 0.6 collective-permute-start.7
  35.6 4.7 %collective-permute-done.9 = f32[48,128]{1,0:T(8,128)S(1)} collective-permute-done((f32[48,128]{1,0:T(8,128)S(1)}, f32[48,128]{1,0:T(8,128)S(1)}, u32[]{:S(2)}, u32[]{:S(2)}) %collective-permute-start.9) | collective-permute-done | bytes 24608 | tf_op jit(solution)/shard_map/ppermute | solution.py:503
  40.3 0.0 collective-permute-done.8
  40.3 0.0 collective-permute-done.7
  40.3 0.0 collective-permute-done.10.from_a
  40.3 0.0 collective-permute-done.11.from_b
  40.3 12.5 %shard_map.63 = (f32[288,256]{1,0:T(8,128)S(1)}, f32[576,128]{1,0:T(8,128)S(1)}, f32[576,128]{1,0:T(8,128)S(1)}, f32[64,128]{1,0:T(8,128)S(1)}, f32[3,48,48]{2,1,0:T(8,128)S(1)}) custom-call(f32[48,128]{1,0:T(8,128)S(1)} %add_add_fusion.4.gram_in, s32[4,256]{1,0:T(4,128)S(1)} %get-tuple-element.29.connect, s32[8,128]{1,0:T(8,128)S(1)} %get-tuple-element.39.edge_nodes, ...), custom_call_target="tpu_custom_call" | custom-call | tf_op jit(solution)/shard_map/pallas_call | solution.py:536
  52.9 0.1 collective-permute-start.14
  52.9 0.2 collective-permute-start.13
  53.2 1.6 %collective-permute-start.12 = (f32[64,128]{1,0:T(8,128)S(1)}, f32[64,128]{1,0:T(8,128)S(1)}, u32[]{:S(2)}, u32[]{:S(2)}) collective-permute-start(f32[64,128]{1,0:T(8,128)S(1)} %get-tuple-element.43), channel_id=1, source_target_pairs={{0,1},{1,0},{2,3},{3,2},{4,5},{5,4},{6,7},{7,6},{8,9},{9,8},{10,11... | collective-permute-start | bytes 98312 | tf_op jit(solution)/shard_map/ppermute | solution.py:503
  54.8 0.0 collective-permute-start.18
  54.8 0.7 collective-permute-start.19
  55.5 0.8 collective-permute-done.14
  56.3 0.7 collective-permute-done.13
  57.0 0.0 collective-permute-done.12
  57.0 3.6 %collective-permute-start.17 = (f32[64,128]{1,0:T(8,128)S(1)}, f32[64,128]{1,0:T(8,128)S(1)}, u32[]{:S(2)}, u32[]{:S(2)}) collective-permute-start(f32[64,128]{1,0:T(8,128)S(1)} %add_add_fusion.3), channel_id=1, source_target_pairs={{0,12},{1,13},{2,14},{3,15},{4,8},{5,9},{6,10},{7,11},{8,4},{9,5},... | collective-permute-start | bytes 98312 | tf_op jit(solution)/shard_map/ppermute | solution.py:503
  60.6 0.0 collective-permute-start.16
  60.6 0.9 collective-permute-start.15
  61.4 5.1 %collective-permute-done.17 = f32[64,128]{1,0:T(8,128)S(1)} collective-permute-done((f32[64,128]{1,0:T(8,128)S(1)}, f32[64,128]{1,0:T(8,128)S(1)}, u32[]{:S(2)}, u32[]{:S(2)}) %collective-permute-start.17) | collective-permute-done | bytes 32800 | tf_op jit(solution)/shard_map/ppermute | solution.py:503
  66.5 0.0 collective-permute-done.16
  66.5 0.0 collective-permute-done.15
  66.5 0.0 collective-permute-done.18.more_a
  66.6 0.0 collective-permute-done.19.more_b
  66.6 16.5 %shard_map.64 = (f32[288,256]{1,0:T(8,128)S(1)}, f32[96,128]{1,0:T(8,128)S(1)}, f32[48,96]{1,0:T(8,128)S(1)}, f32[2,96,96]{2,1,0:T(8,128)S(1)}) custom-call(f32[64,128]{1,0:T(8,128)S(1)} %add_add_fusion.2.gram_in, f32[3,48,48]{2,1,0:T(8,128)S(1)} %get-tuple-element.44.state_in, s32[4,256]{1,0:T(4,128)S(1)} %get-tuple-element.29.connect, ...), custom_call_target="tpu_custom_call" | custom-call | tf_op jit(solution)/shard_map/pallas_call | solution.py:536
  83.1 0.1 collective-permute-start.22
  83.2 0.2 collective-permute-start.21
  83.3 1.7 %collective-permute-start.20 = (f32[96,128]{1,0:T(8,128)S(1)}, f32[96,128]{1,0:T(8,128)S(1)}, u32[]{:S(2)}, u32[]{:S(2)}) collective-permute-start(f32[96,128]{1,0:T(8,128)S(1)} %get-tuple-element.48), channel_id=1, source_target_pairs={{0,1},{1,0},{2,3},{3,2},{4,5},{5,4},{6,7},{7,6},{8,9},{9,8},{10,11... | collective-permute-start | bytes 147464 | tf_op jit(solution)/shard_map/ppermute | solution.py:503
  85.0 1.7 %collective-permute-done.22 = f32[96,128]{1,0:T(8,128)S(1)} collective-permute-done((f32[96,128]{1,0:T(8,128)S(1)}, f32[96,128]{1,0:T(8,128)S(1)}, u32[]{:S(2)}, u32[]{:S(2)}) %collective-permute-start.22) | collective-permute-done | bytes 49184 | tf_op jit(solution)/shard_map/ppermute | solution.py:503
  86.7 1.1 %collective-permute-done.21 = f32[96,128]{1,0:T(8,128)S(1)} collective-permute-done((f32[96,128]{1,0:T(8,128)S(1)}, f32[96,128]{1,0:T(8,128)S(1)}, u32[]{:S(2)}, u32[]{:S(2)}) %collective-permute-start.21) | collective-permute-done | bytes 49184 | tf_op jit(solution)/shard_map/ppermute | solution.py:503
  87.7 0.0 collective-permute-done.20
  87.7 2.6 %collective-permute-start.25 = (f32[96,128]{1,0:T(8,128)S(1)}, f32[96,128]{1,0:T(8,128)S(1)}, u32[]{:S(2)}, u32[]{:S(2)}) collective-permute-start(f32[96,128]{1,0:T(8,128)S(1)} %add_add_fusion.1), channel_id=1, source_target_pairs={{0,12},{1,13},{2,14},{3,15},{4,8},{5,9},{6,10},{7,11},{8,4},{9,5},... | collective-permute-start | bytes 147464 | tf_op jit(solution)/shard_map/ppermute | solution.py:503
  90.4 0.3 collective-permute-start.24
  90.7 1.5 %collective-permute-start.23 = (f32[96,128]{1,0:T(8,128)S(1)}, f32[96,128]{1,0:T(8,128)S(1)}, u32[]{:S(2)}, u32[]{:S(2)}) collective-permute-start(f32[96,128]{1,0:T(8,128)S(1)} %add_add_fusion.1), channel_id=1, source_target_pairs={{0,4},{1,5},{2,6},{3,7},{4,0},{5,1},{6,2},{7,3},{8,12},{9,13},{10,... | collective-permute-start | bytes 147464 | tf_op jit(solution)/shard_map/ppermute | solution.py:503
  92.2 1.9 %collective-permute-done.25 = f32[96,128]{1,0:T(8,128)S(1)} collective-permute-done((f32[96,128]{1,0:T(8,128)S(1)}, f32[96,128]{1,0:T(8,128)S(1)}, u32[]{:S(2)}, u32[]{:S(2)}) %collective-permute-start.25) | collective-permute-done | bytes 49184 | tf_op jit(solution)/shard_map/ppermute | solution.py:503
  94.1 1.8 %collective-permute-done.24 = f32[96,128]{1,0:T(8,128)S(1)} collective-permute-done((f32[96,128]{1,0:T(8,128)S(1)}, f32[96,128]{1,0:T(8,128)S(1)}, u32[]{:S(2)}, u32[]{:S(2)}) %collective-permute-start.24) | collective-permute-done | bytes 49184 | tf_op jit(solution)/shard_map/ppermute | solution.py:503
  95.9 0.0 collective-permute-done.23
  95.9 7.0 %shard_map.65 = (f32[288,256]{1,0:T(8,128)}, f32[1,48]{1,0:T(1,128)}) custom-call(f32[96,128]{1,0:T(8,128)S(1)} %add_add_fusion.gram_in, f32[48,96]{1,0:T(8,128)S(1)} %get-tuple-element.49.coeff_in, f32[2,96,96]{2,1,0:T(8,128)S(1)} %get-tuple-element.50.state_in, f32[288,256]{1,0:T(8,128)S(1)} %get-tuple-element.28.block, ...), custom_call_target="tpu_custom_call" | custom-call | tf_op jit(solution)/shard_map/pallas_call | solution.py:536
  (6 shorter events, 0.1 us)
Async XLA Ops:
  2.1 13.6 %collective-permute-start.2 = (f32[296,128]{1,0:T(8,128)S(1)}, f32[296,128]{1,0:T(8,128)S(1)}, u32[]{:S(2)}, u32[]{:S(2)}) collective-permute-start(f32[296,128]{1,0:T(8,128)S(1)} %get-tuple-element.36), channel_id=1, source_target_pairs={{0,1},{2,3},{4,5},{6,7},{8,9},{10,11},{12,13},{14,15},{1,0},{3,2},... | collective-permute-start | bytes 454664 | tf_op jit(solution)/shard_map/ppermute | solution.py:522
  2.6 13.1 %collective-permute-start.3 = (f32[296,128]{1,0:T(8,128)S(1)}, f32[296,128]{1,0:T(8,128)S(1)}, u32[]{:S(2)}, u32[]{:S(2)}) collective-permute-start(f32[296,128]{1,0:T(8,128)S(1)} %get-tuple-element.37), channel_id=1, source_target_pairs={{1,2},{3,4},{5,6},{7,8},{9,10},{11,12},{13,14},{2,1},{4,3},{6,5},{... | collective-permute-start | bytes 454664 | tf_op jit(solution)/shard_map/ppermute | solution.py:522
  4.3 5.0 %collective-permute-start = (f32[288,128]{1,0:T(8,128)S(1)}, f32[288,128]{1,0:T(8,128)S(1)}, u32[]{:S(2)}, u32[]{:S(2)}) collective-permute-start(f32[288,128]{1,0:T(8,128)S(1)} %get-tuple-element.32), channel_id=1, source_target_pairs={{0,1},{2,3},{4,5},{6,7},{8,9},{10,11},{12,13},{14,15},{1,0},{3,2},... | collective-permute-start | bytes 442376 | tf_op jit(solution)/shard_map/ppermute | solution.py:522
  8.2 1.0 collective-permute-start.1
  18.8 9.9 %collective-permute-start.6 = (f32[48,128]{1,0:T(8,128)S(1)}, f32[48,128]{1,0:T(8,128)S(1)}, u32[]{:S(2)}, u32[]{:S(2)}) collective-permute-start(f32[48,128]{1,0:T(8,128)S(1)} %get-tuple-element.38), channel_id=1, source_target_pairs={{0,3},{1,2},{2,1},{3,0},{4,7},{5,6},{6,5},{7,4},{8,11},{9,10},{10,... | collective-permute-start | bytes 73736 | tf_op jit(solution)/shard_map/ppermute | solution.py:503
  26.5 4.0 %collective-permute-start.5 = (f32[48,128]{1,0:T(8,128)S(1)}, f32[48,128]{1,0:T(8,128)S(1)}, u32[]{:S(2)}, u32[]{:S(2)}) collective-permute-start(f32[48,128]{1,0:T(8,128)S(1)} %get-tuple-element.38), channel_id=1, source_target_pairs={{0,2},{1,3},{2,0},{3,1},{4,6},{5,7},{6,4},{7,5},{8,10},{9,11},{10,... | collective-permute-start | bytes 73736 | tf_op jit(solution)/shard_map/ppermute | solution.py:503
  27.5 3.0 %collective-permute-start.4 = (f32[48,128]{1,0:T(8,128)S(1)}, f32[48,128]{1,0:T(8,128)S(1)}, u32[]{:S(2)}, u32[]{:S(2)}) collective-permute-start(f32[48,128]{1,0:T(8,128)S(1)} %get-tuple-element.38), channel_id=1, source_target_pairs={{0,1},{1,0},{2,3},{3,2},{4,5},{5,4},{6,7},{7,6},{8,9},{9,8},{10,11... | collective-permute-start | bytes 73736 | tf_op jit(solution)/shard_map/ppermute | solution.py:503
  27.6 12.7 %collective-permute-start.10 = (f32[576,128]{1,0:T(8,128)S(1)}, f32[576,128]{1,0:T(8,128)S(1)}, u32[]{:S(2)}, u32[]{:S(2)}) collective-permute-start(f32[576,128]{1,0:T(8,128)S(1)} %get-tuple-element.41.own_a), channel_id=1, source_target_pairs={{0,1},{2,3},{4,5},{6,7},{8,9},{10,11},{12,13},{14,15},{1,0},{3,2},... | collective-permute-start | bytes 884744 | tf_op jit(solution)/shard_map/ppermute | solution.py:522
  28.0 12.3 %collective-permute-start.11 = (f32[576,128]{1,0:T(8,128)S(1)}, f32[576,128]{1,0:T(8,128)S(1)}, u32[]{:S(2)}, u32[]{:S(2)}) collective-permute-start(f32[576,128]{1,0:T(8,128)S(1)} %get-tuple-element.42.own_b), channel_id=1, source_target_pairs={{1,2},{3,4},{5,6},{7,8},{9,10},{11,12},{13,14},{2,1},{4,3},{6,5},{... | collective-permute-start | bytes 884744 | tf_op jit(solution)/shard_map/ppermute | solution.py:522
  30.5 9.7 %collective-permute-start.9 = (f32[48,128]{1,0:T(8,128)S(1)}, f32[48,128]{1,0:T(8,128)S(1)}, u32[]{:S(2)}, u32[]{:S(2)}) collective-permute-start(f32[48,128]{1,0:T(8,128)S(1)} %add_add_fusion.5), channel_id=1, source_target_pairs={{0,12},{1,13},{2,14},{3,15},{4,8},{5,9},{6,10},{7,11},{8,4},{9,5},... | collective-permute-start | bytes 73736 | tf_op jit(solution)/shard_map/ppermute | solution.py:503
  34.9 5.4 %collective-permute-start.8 = (f32[48,128]{1,0:T(8,128)S(1)}, f32[48,128]{1,0:T(8,128)S(1)}, u32[]{:S(2)}, u32[]{:S(2)}) collective-permute-start(f32[48,128]{1,0:T(8,128)S(1)} %add_add_fusion.5), channel_id=1, source_target_pairs={{0,8},{1,9},{2,10},{3,11},{4,12},{5,13},{6,14},{7,15},{8,0},{9,1},... | collective-permute-start | bytes 73736 | tf_op jit(solution)/shard_map/ppermute | solution.py:503
  34.9 5.4 %collective-permute-start.7 = (f32[48,128]{1,0:T(8,128)S(1)}, f32[48,128]{1,0:T(8,128)S(1)}, u32[]{:S(2)}, u32[]{:S(2)}) collective-permute-start(f32[48,128]{1,0:T(8,128)S(1)} %add_add_fusion.5), channel_id=1, source_target_pairs={{0,4},{1,5},{2,6},{3,7},{4,0},{5,1},{6,2},{7,3},{8,12},{9,13},{10,... | collective-permute-start | bytes 73736 | tf_op jit(solution)/shard_map/ppermute | solution.py:503
  52.9 3.4 %collective-permute-start.14 = (f32[64,128]{1,0:T(8,128)S(1)}, f32[64,128]{1,0:T(8,128)S(1)}, u32[]{:S(2)}, u32[]{:S(2)}) collective-permute-start(f32[64,128]{1,0:T(8,128)S(1)} %get-tuple-element.43), channel_id=1, source_target_pairs={{0,3},{1,2},{2,1},{3,0},{4,7},{5,6},{6,5},{7,4},{8,11},{9,10},{10,... | collective-permute-start | bytes 98312 | tf_op jit(solution)/shard_map/ppermute | solution.py:503
  52.9 4.0 %collective-permute-start.13 = (f32[64,128]{1,0:T(8,128)S(1)}, f32[64,128]{1,0:T(8,128)S(1)}, u32[]{:S(2)}, u32[]{:S(2)}) collective-permute-start(f32[64,128]{1,0:T(8,128)S(1)} %get-tuple-element.43), channel_id=1, source_target_pairs={{0,2},{1,3},{2,0},{3,1},{4,6},{5,7},{6,4},{7,5},{8,10},{9,11},{10,... | collective-permute-start | bytes 98312 | tf_op jit(solution)/shard_map/ppermute | solution.py:503
  53.2 3.8 %collective-permute-start.12 = (f32[64,128]{1,0:T(8,128)S(1)}, f32[64,128]{1,0:T(8,128)S(1)}, u32[]{:S(2)}, u32[]{:S(2)}) collective-permute-start(f32[64,128]{1,0:T(8,128)S(1)} %get-tuple-element.43), channel_id=1, source_target_pairs={{0,1},{1,0},{2,3},{3,2},{4,5},{5,4},{6,7},{7,6},{8,9},{9,8},{10,11... | collective-permute-start | bytes 98312 | tf_op jit(solution)/shard_map/ppermute | solution.py:503
  54.8 11.8 %collective-permute-start.18 = (f32[576,128]{1,0:T(8,128)S(1)}, f32[576,128]{1,0:T(8,128)S(1)}, u32[]{:S(2)}, u32[]{:S(2)}) collective-permute-start(f32[576,128]{1,0:T(8,128)S(1)} %get-tuple-element.46.new_a), channel_id=1, source_target_pairs={{0,1},{2,3},{4,5},{6,7},{8,9},{10,11},{12,13},{14,15},{1,0},{3,2},... | collective-permute-start | bytes 884744 | tf_op jit(solution)/shard_map/ppermute | solution.py:522
  54.8 11.8 %collective-permute-start.19 = (f32[576,128]{1,0:T(8,128)S(1)}, f32[576,128]{1,0:T(8,128)S(1)}, u32[]{:S(2)}, u32[]{:S(2)}) collective-permute-start(f32[576,128]{1,0:T(8,128)S(1)} %get-tuple-element.47.new_b), channel_id=1, source_target_pairs={{1,2},{3,4},{5,6},{7,8},{9,10},{11,12},{13,14},{2,1},{4,3},{6,5},{... | collective-permute-start | bytes 884744 | tf_op jit(solution)/shard_map/ppermute | solution.py:522
  57.0 9.5 %collective-permute-start.17 = (f32[64,128]{1,0:T(8,128)S(1)}, f32[64,128]{1,0:T(8,128)S(1)}, u32[]{:S(2)}, u32[]{:S(2)}) collective-permute-start(f32[64,128]{1,0:T(8,128)S(1)} %add_add_fusion.3), channel_id=1, source_target_pairs={{0,12},{1,13},{2,14},{3,15},{4,8},{5,9},{6,10},{7,11},{8,4},{9,5},... | collective-permute-start | bytes 98312 | tf_op jit(solution)/shard_map/ppermute | solution.py:503
  60.6 6.0 %collective-permute-start.16 = (f32[64,128]{1,0:T(8,128)S(1)}, f32[64,128]{1,0:T(8,128)S(1)}, u32[]{:S(2)}, u32[]{:S(2)}) collective-permute-start(f32[64,128]{1,0:T(8,128)S(1)} %add_add_fusion.3), channel_id=1, source_target_pairs={{0,8},{1,9},{2,10},{3,11},{4,12},{5,13},{6,14},{7,15},{8,0},{9,1},... | collective-permute-start | bytes 98312 | tf_op jit(solution)/shard_map/ppermute | solution.py:503
  60.6 6.0 %collective-permute-start.15 = (f32[64,128]{1,0:T(8,128)S(1)}, f32[64,128]{1,0:T(8,128)S(1)}, u32[]{:S(2)}, u32[]{:S(2)}) collective-permute-start(f32[64,128]{1,0:T(8,128)S(1)} %add_add_fusion.3), channel_id=1, source_target_pairs={{0,4},{1,5},{2,6},{3,7},{4,0},{5,1},{6,2},{7,3},{8,12},{9,13},{10,... | collective-permute-start | bytes 98312 | tf_op jit(solution)/shard_map/ppermute | solution.py:503
  83.1 3.6 %collective-permute-start.22 = (f32[96,128]{1,0:T(8,128)S(1)}, f32[96,128]{1,0:T(8,128)S(1)}, u32[]{:S(2)}, u32[]{:S(2)}) collective-permute-start(f32[96,128]{1,0:T(8,128)S(1)} %get-tuple-element.48), channel_id=1, source_target_pairs={{0,3},{1,2},{2,1},{3,0},{4,7},{5,6},{6,5},{7,4},{8,11},{9,10},{10,... | collective-permute-start | bytes 147464 | tf_op jit(solution)/shard_map/ppermute | solution.py:503
  83.2 4.6 %collective-permute-start.21 = (f32[96,128]{1,0:T(8,128)S(1)}, f32[96,128]{1,0:T(8,128)S(1)}, u32[]{:S(2)}, u32[]{:S(2)}) collective-permute-start(f32[96,128]{1,0:T(8,128)S(1)} %get-tuple-element.48), channel_id=1, source_target_pairs={{0,2},{1,3},{2,0},{3,1},{4,6},{5,7},{6,4},{7,5},{8,10},{9,11},{10,... | collective-permute-start | bytes 147464 | tf_op jit(solution)/shard_map/ppermute | solution.py:503
  83.3 4.4 %collective-permute-start.20 = (f32[96,128]{1,0:T(8,128)S(1)}, f32[96,128]{1,0:T(8,128)S(1)}, u32[]{:S(2)}, u32[]{:S(2)}) collective-permute-start(f32[96,128]{1,0:T(8,128)S(1)} %get-tuple-element.48), channel_id=1, source_target_pairs={{0,1},{1,0},{2,3},{3,2},{4,5},{5,4},{6,7},{7,6},{8,9},{9,8},{10,11... | collective-permute-start | bytes 147464 | tf_op jit(solution)/shard_map/ppermute | solution.py:503
  87.7 6.3 %collective-permute-start.25 = (f32[96,128]{1,0:T(8,128)S(1)}, f32[96,128]{1,0:T(8,128)S(1)}, u32[]{:S(2)}, u32[]{:S(2)}) collective-permute-start(f32[96,128]{1,0:T(8,128)S(1)} %add_add_fusion.1), channel_id=1, source_target_pairs={{0,12},{1,13},{2,14},{3,15},{4,8},{5,9},{6,10},{7,11},{8,4},{9,5},... | collective-permute-start | bytes 147464 | tf_op jit(solution)/shard_map/ppermute | solution.py:503
  90.4 5.5 %collective-permute-start.24 = (f32[96,128]{1,0:T(8,128)S(1)}, f32[96,128]{1,0:T(8,128)S(1)}, u32[]{:S(2)}, u32[]{:S(2)}) collective-permute-start(f32[96,128]{1,0:T(8,128)S(1)} %add_add_fusion.1), channel_id=1, source_target_pairs={{0,8},{1,9},{2,10},{3,11},{4,12},{5,13},{6,14},{7,15},{8,0},{9,1},... | collective-permute-start | bytes 147464 | tf_op jit(solution)/shard_map/ppermute | solution.py:503
  90.7 5.2 %collective-permute-start.23 = (f32[96,128]{1,0:T(8,128)S(1)}, f32[96,128]{1,0:T(8,128)S(1)}, u32[]{:S(2)}, u32[]{:S(2)}) collective-permute-start(f32[96,128]{1,0:T(8,128)S(1)} %add_add_fusion.1), channel_id=1, source_target_pairs={{0,4},{1,5},{2,6},{3,7},{4,0},{5,1},{6,2},{7,3},{8,12},{9,13},{10,... | collective-permute-start | bytes 147464 | tf_op jit(solution)/shard_map/ppermute | solution.py:503

commit v8 on v7

--- a/solution.py
+++ b/solution.py
@@ -445,12 +445,12 @@
     base = jnp.concatenate([dotf(behind, solver), jnp.zeros((modes, modes), F32)], axis=1)
     solved = base + dotf(along, root, TN)
     solver = wide + dotf(root, root, TN)
-    again = dotf(solved, mass_all)
-    (pushed,) = eliminate(symmetric(dotf(solved, again, NT)), [again], modes)
-    solved = dotf(pushed, solver)
-    again = dotf(solved, mass_all)
-    normal = symmetric(dotf(solved, again, NT))
-    energy = dotf(solved, pushed, NT)
+    again = dot3(solved, mass_all)
+    (pushed,) = eliminate(symmetric(dot3(solved, again, NT)), [again], modes)
+    solved = dot3(pushed, solver)
+    again = dot3(solved, mass_all)
+    normal = symmetric(dot3(solved, again, NT))
+    energy = dot3(solved, pushed, NT)
     coeff, half, root = eliminate(normal, [solved, energy, unit], modes)
     return coeff, half, root, solver, mass_all
 

time: 103 us -> 103 us (level)
  no operation moved by 1% of the time
where the time goes in v8:
time: 103 us; the launch traced here: 102 us
  Pallas kernels  47.5 us (46%)
  starting transfers between devices  34.1 us (33%)
  waiting for transfers between devices  19.9 us (19%)
    pallas_call x7, Pallas kernels, call(): pl.pallas_call(functools.partial(kernel, dims), out_shape=shapes, in_spec...  47.5 us
    ppermute x18, starting transfers between devices, from_partner(): return lax.ppermute(part, axis, [(i, i ^ bits) for i in range(count)])  26.5 us
    ppermute x18, waiting for transfers between devices, from_partner(): return lax.ppermute(part, axis, [(i, i ^ bits) for i in range(count)])  19.5 us
    ppermute x8, starting transfers between devices, swap(): return lax.ppermute(value, axis, pairs + [(b, a) for a, b in pairs])  7.63 us
  transfers between devices with their start and end apart: 26, of which 10 were waited for; matrix products, arithmetic and copies ran while one was open for 0% of the time, Pallas kernels for 7%

profile of v8, /device:TPU:0, one launch (start us, length us, event | category | flops | bytes accessed | tf_op | source)
XLA Modules:
  0.0 102.4 jit_solution(17294455838677306876)
XLA Ops:
  0.6 1.4 %shard_map.60 = (s32[4,256]{1,0:T(4,128)S(1)}, f32[24,24,256]{2,1,0:T(8,128)S(1)}, f32[24,24,256]{2,1,0:T(8,128)S(1)}, f32[296,128]{1,0:T(8,128)S(1)}, f32[296,128]{1,0:T(8,128)S(1)}) custom-call(s32[4,256]{1,0:T(4,128)} %connect_in.1, f32[24,24,256]{2,1,0:T(8,128)} %stiff_in.1, f32[24,24,256]{2,1,0:T(8,128)} %mass_in.1), custom_call_target="tpu_custom_call" | custom-call | tf_op jit(solution)/shard_map/pallas_call | solution.py:536
  2.1 0.6 collective-permute-start.2
  2.6 0.7 collective-permute-start.3
  3.3 1.0 shard_map.59
  4.3 3.9 %collective-permute-start = (f32[288,128]{1,0:T(8,128)S(1)}, f32[288,128]{1,0:T(8,128)S(1)}, u32[]{:S(2)}, u32[]{:S(2)}) collective-permute-start(f32[288,128]{1,0:T(8,128)S(1)} %get-tuple-element.32), channel_id=1, source_target_pairs={{0,1},{2,3},{4,5},{6,7},{8,9},{10,11},{12,13},{14,15},{1,0},{3,2},... | collective-permute-start | bytes 442376 | tf_op jit(solution)/shard_map/ppermute | solution.py:522
  8.2 0.7 collective-permute-start.1
  8.9 0.3 collective-permute-done.from_a
  9.2 0.0 collective-permute-done.1.from_b
  9.2 6.4 %shard_map.61 = (f32[288,512]{1,0:T(8,128)S(1)}, f32[672,256]{1,0:T(8,128)S(1)}) custom-call(f32[288,256]{1,0:T(8,128)S(1)} %get-tuple-element.28.block, s32[4,256]{1,0:T(4,128)S(1)} %get-tuple-element.29.connect, f32[24,24,256]{2,1,0:T(8,128)S(1)} %get-tuple-element.30.stiffness, f32[24,24,256]{2,1,0:T(8,128)S(1)} %get-tuple-element.31.mass, ...), custom_call_target="tpu_custom_call" | custom-call | tf_op jit(solution)/shard_map/pallas_call | solution.py:536
  15.7 0.0 collective-permute-done.2.from_a
  15.7 0.0 collective-permute-done.3.from_b
  15.7 3.1 %shard_map.62 = (f32[2,12,24,128]{3,2,1,0:T(8,128)S(1)}, s32[8,128]{1,0:T(8,128)S(1)}, f32[576,128]{1,0:T(8,128)S(1)}, f32[576,128]{1,0:T(8,128)S(1)}, f32[48,128]{1,0:T(8,128)S(1)}) custom-call(f32[288,256]{1,0:T(8,128)S(1)} %get-tuple-element.28.block, s32[4,256]{1,0:T(4,128)S(1)} %get-tuple-element.29.connect, f32[288,512]{1,0:T(8,128)S(1)} %get-tuple-element.34.ext, ...), custom_call_target="tpu_custom_call" | custom-call | tf_op jit(solution)/shard_map/pallas_call | solution.py:536
  18.8 7.7 %collective-permute-start.6 = (f32[48,128]{1,0:T(8,128)S(1)}, f32[48,128]{1,0:T(8,128)S(1)}, u32[]{:S(2)}, u32[]{:S(2)}) collective-permute-start(f32[48,128]{1,0:T(8,128)S(1)} %get-tuple-element.38), channel_id=1, source_target_pairs={{0,3},{1,2},{2,1},{3,0},{4,7},{5,6},{6,5},{7,4},{8,11},{9,10},{10,... | collective-permute-start | bytes 73736 | tf_op jit(solution)/shard_map/ppermute | solution.py:503
  26.5 1.0 collective-permute-start.5
  27.5 0.0 collective-permute-start.4
  27.6 0.5 collective-permute-start.10
  28.0 0.7 collective-permute-start.11
  28.7 0.0 collective-permute-done.6
  28.7 1.8 %collective-permute-done.5 = f32[48,128]{1,0:T(8,128)S(1)} collective-permute-done((f32[48,128]{1,0:T(8,128)S(1)}, f32[48,128]{1,0:T(8,128)S(1)}, u32[]{:S(2)}, u32[]{:S(2)}) %collective-permute-start.5) | collective-permute-done | bytes 24608 | tf_op jit(solution)/shard_map/ppermute | solution.py:503
  30.5 0.0 collective-permute-done.4
  30.5 4.4 %collective-permute-start.9 = (f32[48,128]{1,0:T(8,128)S(1)}, f32[48,128]{1,0:T(8,128)S(1)}, u32[]{:S(2)}, u32[]{:S(2)}) collective-permute-start(f32[48,128]{1,0:T(8,128)S(1)} %add_add_fusion.5), channel_id=1, source_target_pairs={{0,12},{1,13},{2,14},{3,15},{4,8},{5,9},{6,10},{7,11},{8,4},{9,5},... | collective-permute-start | bytes 73736 | tf_op jit(solution)/shard_map/ppermute | solution.py:503
  34.9 0.0 collective-permute-start.8
  34.9 0.6 collective-permute-start.7
  35.6 4.7 %collective-permute-done.9 = f32[48,128]{1,0:T(8,128)S(1)} collective-permute-done((f32[48,128]{1,0:T(8,128)S(1)}, f32[48,128]{1,0:T(8,128)S(1)}, u32[]{:S(2)}, u32[]{:S(2)}) %collective-permute-start.9) | collective-permute-done | bytes 24608 | tf_op jit(solution)/shard_map/ppermute | solution.py:503
  40.3 0.0 collective-permute-done.8
  40.3 0.0 collective-permute-done.7
  40.3 0.0 collective-permute-done.10.from_a
  40.3 0.0 collective-permute-done.11.from_b
  40.3 12.5 %shard_map.63 = (f32[288,256]{1,0:T(8,128)S(1)}, f32[576,128]{1,0:T(8,128)S(1)}, f32[576,128]{1,0:T(8,128)S(1)}, f32[64,128]{1,0:T(8,128)S(1)}, f32[3,48,48]{2,1,0:T(8,128)S(1)}) custom-call(f32[48,128]{1,0:T(8,128)S(1)} %add_add_fusion.4.gram_in, s32[4,256]{1,0:T(4,128)S(1)} %get-tuple-element.29.connect, s32[8,128]{1,0:T(8,128)S(1)} %get-tuple-element.39.edge_nodes, ...), custom_call_target="tpu_custom_call" | custom-call | tf_op jit(solution)/shard_map/pallas_call | solution.py:536
  52.9 0.1 collective-permute-start.14
  52.9 0.2 collective-permute-start.13
  53.2 1.6 %collective-permute-start.12 = (f32[64,128]{1,0:T(8,128)S(1)}, f32[64,128]{1,0:T(8,128)S(1)}, u32[]{:S(2)}, u32[]{:S(2)}) collective-permute-start(f32[64,128]{1,0:T(8,128)S(1)} %get-tuple-element.43), channel_id=1, source_target_pairs={{0,1},{1,0},{2,3},{3,2},{4,5},{5,4},{6,7},{7,6},{8,9},{9,8},{10,11... | collective-permute-start | bytes 98312 | tf_op jit(solution)/shard_map/ppermute | solution.py:503
  54.8 0.0 collective-permute-start.18
  54.8 0.7 collective-permute-start.19
  55.5 0.8 collective-permute-done.14
  56.3 0.7 collective-permute-done.13
  57.0 0.0 collective-permute-done.12
  57.0 3.6 %collective-permute-start.17 = (f32[64,128]{1,0:T(8,128)S(1)}, f32[64,128]{1,0:T(8,128)S(1)}, u32[]{:S(2)}, u32[]{:S(2)}) collective-permute-start(f32[64,128]{1,0:T(8,128)S(1)} %add_add_fusion.3), channel_id=1, source_target_pairs={{0,12},{1,13},{2,14},{3,15},{4,8},{5,9},{6,10},{7,11},{8,4},{9,5},... | collective-permute-start | bytes 98312 | tf_op jit(solution)/shard_map/ppermute | solution.py:503
  60.6 0.0 collective-permute-start.16
  60.6 0.9 collective-permute-start.15
  61.4 5.1 %collective-permute-done.17 = f32[64,128]{1,0:T(8,128)S(1)} collective-permute-done((f32[64,128]{1,0:T(8,128)S(1)}, f32[64,128]{1,0:T(8,128)S(1)}, u32[]{:S(2)}, u32[]{:S(2)}) %collective-permute-start.17) | collective-permute-done | bytes 32800 | tf_op jit(solution)/shard_map/ppermute | solution.py:503
  66.5 0.0 collective-permute-done.16
  66.5 0.0 collective-permute-done.15
  66.5 0.0 collective-permute-done.18.more_a
  66.6 0.0 collective-permute-done.19.more_b
  66.6 16.3 %shard_map.64 = (f32[288,256]{1,0:T(8,128)S(1)}, f32[96,128]{1,0:T(8,128)S(1)}, f32[48,96]{1,0:T(8,128)S(1)}, f32[2,96,96]{2,1,0:T(8,128)S(1)}) custom-call(f32[64,128]{1,0:T(8,128)S(1)} %add_add_fusion.2.gram_in, f32[3,48,48]{2,1,0:T(8,128)S(1)} %get-tuple-element.44.state_in, s32[4,256]{1,0:T(4,128)S(1)} %get-tuple-element.29.connect, ...), custom_call_target="tpu_custom_call" | custom-call | tf_op jit(solution)/shard_map/pallas_call | solution.py:536
  82.9 0.1 collective-permute-start.22
  83.0 0.2 collective-permute-start.21
  83.1 1.7 %collective-permute-start.20 = (f32[96,128]{1,0:T(8,128)S(1)}, f32[96,128]{1,0:T(8,128)S(1)}, u32[]{:S(2)}, u32[]{:S(2)}) collective-permute-start(f32[96,128]{1,0:T(8,128)S(1)} %get-tuple-element.48), channel_id=1, source_target_pairs={{0,1},{1,0},{2,3},{3,2},{4,5},{5,4},{6,7},{7,6},{8,9},{9,8},{10,11... | collective-permute-start | bytes 147464 | tf_op jit(solution)/shard_map/ppermute | solution.py:503
  84.8 1.7 %collective-permute-done.22 = f32[96,128]{1,0:T(8,128)S(1)} collective-permute-done((f32[96,128]{1,0:T(8,128)S(1)}, f32[96,128]{1,0:T(8,128)S(1)}, u32[]{:S(2)}, u32[]{:S(2)}) %collective-permute-start.22) | collective-permute-done | bytes 49184 | tf_op jit(solution)/shard_map/ppermute | solution.py:503
  86.5 1.1 %collective-permute-done.21 = f32[96,128]{1,0:T(8,128)S(1)} collective-permute-done((f32[96,128]{1,0:T(8,128)S(1)}, f32[96,128]{1,0:T(8,128)S(1)}, u32[]{:S(2)}, u32[]{:S(2)}) %collective-permute-start.21) | collective-permute-done | bytes 49184 | tf_op jit(solution)/shard_map/ppermute | solution.py:503
  87.5 0.0 collective-permute-done.20
  87.5 2.7 %collective-permute-start.25 = (f32[96,128]{1,0:T(8,128)S(1)}, f32[96,128]{1,0:T(8,128)S(1)}, u32[]{:S(2)}, u32[]{:S(2)}) collective-permute-start(f32[96,128]{1,0:T(8,128)S(1)} %add_add_fusion.1), channel_id=1, source_target_pairs={{0,12},{1,13},{2,14},{3,15},{4,8},{5,9},{6,10},{7,11},{8,4},{9,5},... | collective-permute-start | bytes 147464 | tf_op jit(solution)/shard_map/ppermute | solution.py:503
  90.2 0.3 collective-permute-start.24
  90.5 1.5 %collective-permute-start.23 = (f32[96,128]{1,0:T(8,128)S(1)}, f32[96,128]{1,0:T(8,128)S(1)}, u32[]{:S(2)}, u32[]{:S(2)}) collective-permute-start(f32[96,128]{1,0:T(8,128)S(1)} %add_add_fusion.1), channel_id=1, source_target_pairs={{0,4},{1,5},{2,6},{3,7},{4,0},{5,1},{6,2},{7,3},{8,12},{9,13},{10,... | collective-permute-start | bytes 147464 | tf_op jit(solution)/shard_map/ppermute | solution.py:503
  92.0 1.9 %collective-permute-done.25 = f32[96,128]{1,0:T(8,128)S(1)} collective-permute-done((f32[96,128]{1,0:T(8,128)S(1)}, f32[96,128]{1,0:T(8,128)S(1)}, u32[]{:S(2)}, u32[]{:S(2)}) %collective-permute-start.25) | collective-permute-done | bytes 49184 | tf_op jit(solution)/shard_map/ppermute | solution.py:503
  93.9 1.7 %collective-permute-done.24 = f32[96,128]{1,0:T(8,128)S(1)} collective-permute-done((f32[96,128]{1,0:T(8,128)S(1)}, f32[96,128]{1,0:T(8,128)S(1)}, u32[]{:S(2)}, u32[]{:S(2)}) %collective-permute-start.24) | collective-permute-done | bytes 49184 | tf_op jit(solution)/shard_map/ppermute | solution.py:503
  95.7 0.0 collective-permute-done.23
  95.7 6.7 %shard_map.65 = (f32[288,256]{1,0:T(8,128)}, f32[1,48]{1,0:T(1,128)}) custom-call(f32[96,128]{1,0:T(8,128)S(1)} %add_add_fusion.gram_in, f32[48,96]{1,0:T(8,128)S(1)} %get-tuple-element.49.coeff_in, f32[2,96,96]{2,1,0:T(8,128)S(1)} %get-tuple-element.50.state_in, f32[288,256]{1,0:T(8,128)S(1)} %get-tuple-element.28.block, ...), custom_call_target="tpu_custom_call" | custom-call | tf_op jit(solution)/shard_map/pallas_call | solution.py:536
  (6 shorter events, 0.1 us)
Async XLA Ops:
  2.1 13.6 %collective-permute-start.2 = (f32[296,128]{1,0:T(8,128)S(1)}, f32[296,128]{1,0:T(8,128)S(1)}, u32[]{:S(2)}, u32[]{:S(2)}) collective-permute-start(f32[296,128]{1,0:T(8,128)S(1)} %get-tuple-element.36), channel_id=1, source_target_pairs={{0,1},{2,3},{4,5},{6,7},{8,9},{10,11},{12,13},{14,15},{1,0},{3,2},... | collective-permute-start | bytes 454664 | tf_op jit(solution)/shard_map/ppermute | solution.py:522
  2.6 13.1 %collective-permute-start.3 = (f32[296,128]{1,0:T(8,128)S(1)}, f32[296,128]{1,0:T(8,128)S(1)}, u32[]{:S(2)}, u32[]{:S(2)}) collective-permute-start(f32[296,128]{1,0:T(8,128)S(1)} %get-tuple-element.37), channel_id=1, source_target_pairs={{1,2},{3,4},{5,6},{7,8},{9,10},{11,12},{13,14},{2,1},{4,3},{6,5},{... | collective-permute-start | bytes 454664 | tf_op jit(solution)/shard_map/ppermute | solution.py:522
  4.3 5.0 %collective-permute-start = (f32[288,128]{1,0:T(8,128)S(1)}, f32[288,128]{1,0:T(8,128)S(1)}, u32[]{:S(2)}, u32[]{:S(2)}) collective-permute-start(f32[288,128]{1,0:T(8,128)S(1)} %get-tuple-element.32), channel_id=1, source_target_pairs={{0,1},{2,3},{4,5},{6,7},{8,9},{10,11},{12,13},{14,15},{1,0},{3,2},... | collective-permute-start | bytes 442376 | tf_op jit(solution)/shard_map/ppermute | solution.py:522
  8.2 1.0 collective-permute-start.1
  18.8 9.9 %collective-permute-start.6 = (f32[48,128]{1,0:T(8,128)S(1)}, f32[48,128]{1,0:T(8,128)S(1)}, u32[]{:S(2)}, u32[]{:S(2)}) collective-permute-start(f32[48,128]{1,0:T(8,128)S(1)} %get-tuple-element.38), channel_id=1, source_target_pairs={{0,3},{1,2},{2,1},{3,0},{4,7},{5,6},{6,5},{7,4},{8,11},{9,10},{10,... | collective-permute-start | bytes 73736 | tf_op jit(solution)/shard_map/ppermute | solution.py:503
  26.5 4.0 %collective-permute-start.5 = (f32[48,128]{1,0:T(8,128)S(1)}, f32[48,128]{1,0:T(8,128)S(1)}, u32[]{:S(2)}, u32[]{:S(2)}) collective-permute-start(f32[48,128]{1,0:T(8,128)S(1)} %get-tuple-element.38), channel_id=1, source_target_pairs={{0,2},{1,3},{2,0},{3,1},{4,6},{5,7},{6,4},{7,5},{8,10},{9,11},{10,... | collective-permute-start | bytes 73736 | tf_op jit(solution)/shard_map/ppermute | solution.py:503
  27.5 3.0 %collective-permute-start.4 = (f32[48,128]{1,0:T(8,128)S(1)}, f32[48,128]{1,0:T(8,128)S(1)}, u32[]{:S(2)}, u32[]{:S(2)}) collective-permute-start(f32[48,128]{1,0:T(8,128)S(1)} %get-tuple-element.38), channel_id=1, source_target_pairs={{0,1},{1,0},{2,3},{3,2},{4,5},{5,4},{6,7},{7,6},{8,9},{9,8},{10,11... | collective-permute-start | bytes 73736 | tf_op jit(solution)/shard_map/ppermute | solution.py:503
  27.6 12.7 %collective-permute-start.10 = (f32[576,128]{1,0:T(8,128)S(1)}, f32[576,128]{1,0:T(8,128)S(1)}, u32[]{:S(2)}, u32[]{:S(2)}) collective-permute-start(f32[576,128]{1,0:T(8,128)S(1)} %get-tuple-element.41.own_a), channel_id=1, source_target_pairs={{0,1},{2,3},{4,5},{6,7},{8,9},{10,11},{12,13},{14,15},{1,0},{3,2},... | collective-permute-start | bytes 884744 | tf_op jit(solution)/shard_map/ppermute | solution.py:522
  28.0 12.3 %collective-permute-start.11 = (f32[576,128]{1,0:T(8,128)S(1)}, f32[576,128]{1,0:T(8,128)S(1)}, u32[]{:S(2)}, u32[]{:S(2)}) collective-permute-start(f32[576,128]{1,0:T(8,128)S(1)} %get-tuple-element.42.own_b), channel_id=1, source_target_pairs={{1,2},{3,4},{5,6},{7,8},{9,10},{11,12},{13,14},{2,1},{4,3},{6,5},{... | collective-permute-start | bytes 884744 | tf_op jit(solution)/shard_map/ppermute | solution.py:522
  30.5 9.7 %collective-permute-start.9 = (f32[48,128]{1,0:T(8,128)S(1)}, f32[48,128]{1,0:T(8,128)S(1)}, u32[]{:S(2)}, u32[]{:S(2)}) collective-permute-start(f32[48,128]{1,0:T(8,128)S(1)} %add_add_fusion.5), channel_id=1, source_target_pairs={{0,12},{1,13},{2,14},{3,15},{4,8},{5,9},{6,10},{7,11},{8,4},{9,5},... | collective-permute-start | bytes 73736 | tf_op jit(solution)/shard_map/ppermute | solution.py:503
  34.9 5.4 %collective-permute-start.8 = (f32[48,128]{1,0:T(8,128)S(1)}, f32[48,128]{1,0:T(8,128)S(1)}, u32[]{:S(2)}, u32[]{:S(2)}) collective-permute-start(f32[48,128]{1,0:T(8,128)S(1)} %add_add_fusion.5), channel_id=1, source_target_pairs={{0,8},{1,9},{2,10},{3,11},{4,12},{5,13},{6,14},{7,15},{8,0},{9,1},... | collective-permute-start | bytes 73736 | tf_op jit(solution)/shard_map/ppermute | solution.py:503
  34.9 5.4 %collective-permute-start.7 = (f32[48,128]{1,0:T(8,128)S(1)}, f32[48,128]{1,0:T(8,128)S(1)}, u32[]{:S(2)}, u32[]{:S(2)}) collective-permute-start(f32[48,128]{1,0:T(8,128)S(1)} %add_add_fusion.5), channel_id=1, source_target_pairs={{0,4},{1,5},{2,6},{3,7},{4,0},{5,1},{6,2},{7,3},{8,12},{9,13},{10,... | collective-permute-start | bytes 73736 | tf_op jit(solution)/shard_map/ppermute | solution.py:503
  52.9 3.4 %collective-permute-start.14 = (f32[64,128]{1,0:T(8,128)S(1)}, f32[64,128]{1,0:T(8,128)S(1)}, u32[]{:S(2)}, u32[]{:S(2)}) collective-permute-start(f32[64,128]{1,0:T(8,128)S(1)} %get-tuple-element.43), channel_id=1, source_target_pairs={{0,3},{1,2},{2,1},{3,0},{4,7},{5,6},{6,5},{7,4},{8,11},{9,10},{10,... | collective-permute-start | bytes 98312 | tf_op jit(solution)/shard_map/ppermute | solution.py:503
  52.9 4.0 %collective-permute-start.13 = (f32[64,128]{1,0:T(8,128)S(1)}, f32[64,128]{1,0:T(8,128)S(1)}, u32[]{:S(2)}, u32[]{:S(2)}) collective-permute-start(f32[64,128]{1,0:T(8,128)S(1)} %get-tuple-element.43), channel_id=1, source_target_pairs={{0,2},{1,3},{2,0},{3,1},{4,6},{5,7},{6,4},{7,5},{8,10},{9,11},{10,... | collective-permute-start | bytes 98312 | tf_op jit(solution)/shard_map/ppermute | solution.py:503
  53.2 3.8 %collective-permute-start.12 = (f32[64,128]{1,0:T(8,128)S(1)}, f32[64,128]{1,0:T(8,128)S(1)}, u32[]{:S(2)}, u32[]{:S(2)}) collective-permute-start(f32[64,128]{1,0:T(8,128)S(1)} %get-tuple-element.43), channel_id=1, source_target_pairs={{0,1},{1,0},{2,3},{3,2},{4,5},{5,4},{6,7},{7,6},{8,9},{9,8},{10,11... | collective-permute-start | bytes 98312 | tf_op jit(solution)/shard_map/ppermute | solution.py:503
  54.8 11.8 %collective-permute-start.18 = (f32[576,128]{1,0:T(8,128)S(1)}, f32[576,128]{1,0:T(8,128)S(1)}, u32[]{:S(2)}, u32[]{:S(2)}) collective-permute-start(f32[576,128]{1,0:T(8,128)S(1)} %get-tuple-element.46.new_a), channel_id=1, source_target_pairs={{0,1},{2,3},{4,5},{6,7},{8,9},{10,11},{12,13},{14,15},{1,0},{3,2},... | collective-permute-start | bytes 884744 | tf_op jit(solution)/shard_map/ppermute | solution.py:522
  54.8 11.8 %collective-permute-start.19 = (f32[576,128]{1,0:T(8,128)S(1)}, f32[576,128]{1,0:T(8,128)S(1)}, u32[]{:S(2)}, u32[]{:S(2)}) collective-permute-start(f32[576,128]{1,0:T(8,128)S(1)} %get-tuple-element.47.new_b), channel_id=1, source_target_pairs={{1,2},{3,4},{5,6},{7,8},{9,10},{11,12},{13,14},{2,1},{4,3},{6,5},{... | collective-permute-start | bytes 884744 | tf_op jit(solution)/shard_map/ppermute | solution.py:522
  57.0 9.5 %collective-permute-start.17 = (f32[64,128]{1,0:T(8,128)S(1)}, f32[64,128]{1,0:T(8,128)S(1)}, u32[]{:S(2)}, u32[]{:S(2)}) collective-permute-start(f32[64,128]{1,0:T(8,128)S(1)} %add_add_fusion.3), channel_id=1, source_target_pairs={{0,12},{1,13},{2,14},{3,15},{4,8},{5,9},{6,10},{7,11},{8,4},{9,5},... | collective-permute-start | bytes 98312 | tf_op jit(solution)/shard_map/ppermute | solution.py:503
  60.6 6.0 %collective-permute-start.16 = (f32[64,128]{1,0:T(8,128)S(1)}, f32[64,128]{1,0:T(8,128)S(1)}, u32[]{:S(2)}, u32[]{:S(2)}) collective-permute-start(f32[64,128]{1,0:T(8,128)S(1)} %add_add_fusion.3), channel_id=1, source_target_pairs={{0,8},{1,9},{2,10},{3,11},{4,12},{5,13},{6,14},{7,15},{8,0},{9,1},... | collective-permute-start | bytes 98312 | tf_op jit(solution)/shard_map/ppermute | solution.py:503
  60.6 6.0 %collective-permute-start.15 = (f32[64,128]{1,0:T(8,128)S(1)}, f32[64,128]{1,0:T(8,128)S(1)}, u32[]{:S(2)}, u32[]{:S(2)}) collective-permute-start(f32[64,128]{1,0:T(8,128)S(1)} %add_add_fusion.3), channel_id=1, source_target_pairs={{0,4},{1,5},{2,6},{3,7},{4,0},{5,1},{6,2},{7,3},{8,12},{9,13},{10,... | collective-permute-start | bytes 98312 | tf_op jit(solution)/shard_map/ppermute | solution.py:503
  82.9 3.6 %collective-permute-start.22 = (f32[96,128]{1,0:T(8,128)S(1)}, f32[96,128]{1,0:T(8,128)S(1)}, u32[]{:S(2)}, u32[]{:S(2)}) collective-permute-start(f32[96,128]{1,0:T(8,128)S(1)} %get-tuple-element.48), channel_id=1, source_target_pairs={{0,3},{1,2},{2,1},{3,0},{4,7},{5,6},{6,5},{7,4},{8,11},{9,10},{10,... | collective-permute-start | bytes 147464 | tf_op jit(solution)/shard_map/ppermute | solution.py:503
  83.0 4.6 %collective-permute-start.21 = (f32[96,128]{1,0:T(8,128)S(1)}, f32[96,128]{1,0:T(8,128)S(1)}, u32[]{:S(2)}, u32[]{:S(2)}) collective-permute-start(f32[96,128]{1,0:T(8,128)S(1)} %get-tuple-element.48), channel_id=1, source_target_pairs={{0,2},{1,3},{2,0},{3,1},{4,6},{5,7},{6,4},{7,5},{8,10},{9,11},{10,... | collective-permute-start | bytes 147464 | tf_op jit(solution)/shard_map/ppermute | solution.py:503
  83.1 4.4 %collective-permute-start.20 = (f32[96,128]{1,0:T(8,128)S(1)}, f32[96,128]{1,0:T(8,128)S(1)}, u32[]{:S(2)}, u32[]{:S(2)}) collective-permute-start(f32[96,128]{1,0:T(8,128)S(1)} %get-tuple-element.48), channel_id=1, source_target_pairs={{0,1},{1,0},{2,3},{3,2},{4,5},{5,4},{6,7},{7,6},{8,9},{9,8},{10,11... | collective-permute-start | bytes 147464 | tf_op jit(solution)/shard_map/ppermute | solution.py:503
  87.5 6.4 %collective-permute-start.25 = (f32[96,128]{1,0:T(8,128)S(1)}, f32[96,128]{1,0:T(8,128)S(1)}, u32[]{:S(2)}, u32[]{:S(2)}) collective-permute-start(f32[96,128]{1,0:T(8,128)S(1)} %add_add_fusion.1), channel_id=1, source_target_pairs={{0,12},{1,13},{2,14},{3,15},{4,8},{5,9},{6,10},{7,11},{8,4},{9,5},... | collective-permute-start | bytes 147464 | tf_op jit(solution)/shard_map/ppermute | solution.py:503
  90.2 5.5 %collective-permute-start.24 = (f32[96,128]{1,0:T(8,128)S(1)}, f32[96,128]{1,0:T(8,128)S(1)}, u32[]{:S(2)}, u32[]{:S(2)}) collective-permute-start(f32[96,128]{1,0:T(8,128)S(1)} %add_add_fusion.1), channel_id=1, source_target_pairs={{0,8},{1,9},{2,10},{3,11},{4,12},{5,13},{6,14},{7,15},{8,0},{9,1},... | collective-permute-start | bytes 147464 | tf_op jit(solution)/shard_map/ppermute | solution.py:503
  90.5 5.2 %collective-permute-start.23 = (f32[96,128]{1,0:T(8,128)S(1)}, f32[96,128]{1,0:T(8,128)S(1)}, u32[]{:S(2)}, u32[]{:S(2)}) collective-permute-start(f32[96,128]{1,0:T(8,128)S(1)} %add_add_fusion.1), channel_id=1, source_target_pairs={{0,4},{1,5},{2,6},{3,7},{4,0},{5,1},{6,2},{7,3},{8,12},{9,13},{10,... | collective-permute-start | bytes 147464 | tf_op jit(solution)/shard_map/ppermute | solution.py:503
